TPU v7x, 32 devices: a whole 2x2x4 slice. The times are simulated.
32 devices in a mesh: exp: 4 (over y, x), imp: 2 (over core), wk: 4 (over z).
Axes of the slice: x: 2, y: 2, z: 4, core: 2. Of those that a mesh axis runs over, the one named last changes fastest.
Arguments:
- flows: float32 [4, 2048, 256], P('wk', 'exp', 'imp'), may hold values from 0.0112 to 284, as said below
- importer_factor: float32 [256, 256], P('imp'), may hold values from -0.5 to 1.5
- week_factor: float32 [4, 256], P('wk'), may hold values from 0 to 1
Outputs:
- exporter_out: float32 [2048, 256], P('exp')
- importer_out: float32 [256, 256], P('imp')
- week_out: float32 [4, 256], P('wk')
Inputs may be any that keep to these rules, and one draw needn't show every extreme that they name: `flows`: flows are positive.
All inputs are finite; a program needn't handle non-finite values.
Results may differ from a plain program's by a relative error of at most 0.00022.
Values sent between devices are 32-bit elements; how exact they have to be, the bound alone decides.
No kernel may reach another device: no remote copies, remote signals or barrier semaphores. Data moves between devices by JAX's collectives and lax.ppermute only.
A program may use at most 64 MiB of HBM per device.

v0:
```python
import jax
import jax.numpy as jnp
from jax import lax
from jax.experimental import pallas as pl
from jax.experimental.pallas import tpu as pltpu
from jax.sharding import PartitionSpec as P

ridge = 0.2
eps = 1e-06
hp = lax.Precision.HIGHEST
block = 32


def dot(a, b):
    return jnp.dot(a, b, precision=hp, preferred_element_type=jnp.float32)


def pivot_panel(panel):
    groups, tiles = len(panel), len(panel[0])
    lane = lax.broadcasted_iota(jnp.int32, (8, 128), 1)
    sub = lax.broadcasted_iota(jnp.int32, (8, 128), 0)
    part = [list(r) for r in panel]
    for g in range(groups):
        cols = [
            [jnp.broadcast_to(part[h][0][:, 8 * g + q : 8 * g + q + 1], (8, 128)) for h in range(groups)]
            for q in range(8)
        ]
        for q in range(8):
            col = cols[q]
            inv = 1.0 / jnp.broadcast_to(col[g][q : q + 1, :], (8, 128))
            here = lane == 8 * g + q
            this = sub == q
            rows = []
            for t in range(tiles):
                row = jnp.broadcast_to(part[g][t][q : q + 1, :], (8, 128))
                if t == 0:
                    row = jnp.where(here, 1.0, row)
                rows.append(row * inv)
            for h in range(groups):
                for t in range(tiles):
                    base = jnp.where(here, 0.0, part[h][t]) if t == 0 else part[h][t]
                    new = base - col[h] * rows[t]
                    part[h][t] = jnp.where(this, rows[t], new) if h == g else new
            for q2 in range(q + 1, 8):
                factor = jnp.broadcast_to(cols[q2][g][q : q + 1, :], (8, 128)) * inv
                for h in range(groups):
                    new = cols[q2][h] - col[h] * factor
                    cols[q2][h] = jnp.where(this, factor, new) if h == g else new
    return jnp.concatenate([jnp.concatenate(r, axis=1) for r in part], axis=0)


def inverse_kernel(v_ref, o_ref, a_ref):
    n = v_ref.shape[0]
    a_ref[...] = v_ref[...]

    def step(_, carry):
        panel = [
            [a_ref[8 * g : 8 * g + 8, 128 * t : 128 * t + 128] for t in range(n // 128)]
            for g in range(block // 8)
        ]
        top = pivot_panel(panel)
        rest = a_ref[block:, :]
        lane = lax.broadcasted_iota(jnp.int32, rest.shape, 1)
        new = jnp.where(lane < block, 0.0, rest) - dot(rest[:, :block], top)
        a_ref[: n - block, :] = pltpu.roll(new, n - block, 1)
        a_ref[n - block :, :] = pltpu.roll(top, n - block, 1)
        return carry

    lax.fori_loop(0, n // block, step, 0)
    o_ref[...] = a_ref[...]


def inverse(v):
    n = v.shape[0]
    return pl.pallas_call(
        inverse_kernel,
        out_shape=jax.ShapeDtypeStruct((n, n), jnp.float32),
        in_specs=[pl.BlockSpec(memory_space=pltpu.VMEM)],
        out_specs=pl.BlockSpec(memory_space=pltpu.VMEM),
        scratch_shapes=[pltpu.VMEM((n, n), jnp.float32)],
        name="inverse",
    )(v)


def ridge_inverse(g1, g2):
    h = g1 * g2
    n = h.shape[0]
    eye = jnp.eye(n, dtype=jnp.float32)
    return inverse(h + (ridge * jnp.trace(h) / n) * eye)


def swap(x, axis, bit):
    n = lax.axis_size(axis)
    return lax.ppermute(x, axis, [(i, i ^ bit) for i in range(n)])


def bits(axis):
    n = lax.axis_size(axis)
    return [1 << b for b in range(n.bit_length() - 1)]


def total(x, axis):
    for bit in bits(axis):
        x = x + swap(x, axis, bit)
    return x


def scatter_total(x, axis):
    me = lax.axis_index(axis)
    for bit in reversed(bits(axis)):
        half = x.reshape((2, x.shape[0] // 2) + x.shape[1:])
        mine = jnp.where((me & bit) != 0, 1, 0)
        keep = lax.dynamic_index_in_dim(half, mine, 0, keepdims=False)
        give = lax.dynamic_index_in_dim(half, 1 - mine, 0, keepdims=False)
        x = keep + swap(give, axis, bit)
    return x


def gather_rows(x, axis):
    me = lax.axis_index(axis)
    for bit in bits(axis):
        other = swap(x, axis, bit)
        mine = (me & bit) != 0
        x = jnp.concatenate([jnp.where(mine, other, x), jnp.where(mine, x, other)], axis=0)
    return x


def by_index(pieces, axis):
    me = lax.axis_index(axis)
    out = jnp.zeros((len(pieces),) + pieces[0].shape, jnp.float32)
    for d, piece in enumerate(pieces):
        out = lax.dynamic_update_slice(out, piece[None], ((me ^ d),) + (0,) * piece.ndim)
    return out


def scale_of(gram, count):
    n = gram.shape[0]
    diag = jnp.where(jnp.eye(n, dtype=jnp.bool_), gram, 0.0)
    one = jnp.sqrt(jnp.sum(diag, 0) / count + eps)
    two = jnp.sqrt(jnp.sum(diag, 1) / count + eps)
    return one, gram / (two[:, None] * one[None, :])


def per_device(flows, importer_factor, week_factor):
    f = flows[0]
    w = week_factor
    rank = w.shape[1]
    rows_here, cols_here = f.shape
    weeks = lax.axis_size("wk")
    me_k = lax.axis_index("wk")
    me_i = lax.axis_index("imp")
    ni = lax.axis_size("imp")

    row_part = jnp.sum(f, 1)
    col_part = jnp.sum(f, 0)
    small = jnp.concatenate([dot(col_part[None], importer_factor)[0], jnp.sum(col_part)[None], col_part])
    m_part = dot(f, importer_factor * w)
    gram_b = total(dot(importer_factor.T, importer_factor), "imp")
    row_tot = total(row_part, "imp")
    share = scatter_total(m_part, "imp")

    pad = -rows_here % rank
    extra = jnp.concatenate([w, jnp.pad(row_tot, (0, pad)).reshape(-1, rank)], axis=0)
    chunk = share.shape[0] // weeks
    cut = share.reshape(weeks, chunk, rank)
    got = []
    for d in range(weeks):
        give = jnp.concatenate([lax.dynamic_index_in_dim(cut, me_k ^ d, 0, keepdims=False), extra], axis=0)
        got.append(swap(give, "wk", d) if d else give)
    own = sum(g[:chunk] for g in got[1:]) + got[0][:chunk]
    tails = by_index([g[chunk:] for g in got], "wk")
    w_all = tails[:, 0]
    row_all = tails[:, 1:].reshape(weeks, -1)[:, :rows_here]

    gram_c = dot(w_all.T, w_all)
    inv_a = ridge_inverse(gram_b, gram_c)

    small = total(small, "exp")
    heads = total(small[: rank + 1], "imp")
    grand = heads[rank]
    shift = w * (heads[:rank] / grand)[None]
    col_mean = small[rank + 1 :] / grand

    give = jnp.concatenate([own, shift], axis=0)
    got = by_index([swap(give, "wk", d) if d else give for d in range(weeks)], "wk")
    shifts = got[:, chunk]
    m_rows = gather_rows(got[:, :chunk].reshape(-1, rank), "imp")
    m_a = m_rows - dot(row_all.T, shifts)
    raw_a = dot(m_a, inv_a)

    resid = f - row_tot[:, None] * col_mean[None, :]
    t_part = dot(resid.T, raw_a)
    mine = lax.dynamic_slice(raw_a, (0, me_i * (rank // ni)), (rows_here, rank // ni))
    g_part = dot(mine.T, raw_a)
    g_a = gather_rows(total(g_part, "exp"), "imp")
    scale_a, gram_a = scale_of(g_a, rows_here * lax.axis_size("exp"))
    fac_a = raw_a / scale_a
    inv_b = ridge_inverse(gram_a, gram_c)

    t = total(t_part, "exp") / scale_a
    m_b = total(t * w, "wk")
    raw_b = dot(m_b, inv_b)
    g_b = total(dot(raw_b.T, raw_b), "imp")
    scale_b, gram_b2 = scale_of(g_b, cols_here * ni)
    fac_b = raw_b / scale_b
    inv_c = ridge_inverse(gram_a, gram_b2)

    m_mine = total(jnp.sum(fac_b * t, 0)[None], "imp")
    m_c = by_index([swap(m_mine, "wk", d) if d else m_mine for d in range(weeks)], "wk")[:, 0]
    raw_c = dot(m_c, inv_c)
    scale_c = jnp.sqrt(jnp.sum(raw_c * raw_c, 0) / weeks + eps)
    fac_c = lax.dynamic_slice(raw_c, (me_k, 0), (1, rank)) / scale_c
    return (fac_a, fac_b, fac_c)


def solution(mesh):
    in_specs = (P("wk", "exp", "imp"), P("imp", None), P("wk", None))
    out_specs = (P("exp", None), P("imp", None), P("wk", None))
    return jax.shard_map(
        per_device, mesh=mesh, in_specs=in_specs, out_specs=out_specs, check_vma=False
    )
```

profile of v0, /device:TPU:0, one launch (start us, length us, event | category | flops | bytes accessed | tf_op | source)
XLA Modules:
  0.0 115.3 jit_solution(15957482878178722676)
XLA Ops:
  0.6 0.7 copy-done.3
  1.3 1.6 %convolution_bitcast_fusion = f32[512,256]{0,1:T(8,128)S(1)} fusion(f32[1,512,128]{2,1,0:T(8,128)} %param.3, f32[128,256]{1,0:T(8,128)} %param.4, f32[256]{0:T(256)S(1)} %bitcast.77), kind=kOutput, calls=%fused_computation | convolution fusion | flops 201359360 | bytes 918528 | tf_op jit(solution)/shard_map/dot_general | solution.py:15
  3.0 0.3 reshape.77
  3.3 0.5 constant_dynamic-slice_fusion.2
  3.8 0.1 copy.12
  3.9 0.6 collective-permute-start
  4.5 0.2 copy-done
  4.7 0.7 fusion.32
  5.4 0.5 collective-permute-start.1
  5.9 0.2 fusion.27
  6.1 0.7 pad_maximum_fusion.8
  6.8 2.5 %collective-permute-start.5 = (f32[385]{0:T(512)S(1)}, f32[385]{0:T(512)S(1)}, u32[]{:S(2)}, u32[]{:S(2)}) collective-permute-start(f32[385]{0:T(512)S(1)} %pad_maximum_fusion.8), channel_id=1, source_target_pairs={{0,8},{8,0},{16,24},{24,16},{1,9},{9,1},{17,25},{25,17},{2,10},{10... | collective-permute-start | bytes 4628 | tf_op jit(solution)/shard_map/ppermute | solution.py:94
  9.3 0.4 fusion.34
  9.7 0.3 collective-permute-start.12
  10.0 0.9 collective-permute-done.5
  10.9 0.7 fusion.30
  11.6 2.0 %collective-permute-start.6 = (f32[385]{0:T(512)S(1)}, f32[385]{0:T(512)S(1)}, u32[]{:S(2)}, u32[]{:S(2)}) collective-permute-start(f32[385]{0:T(512)S(1)} %fusion.30), channel_id=1, source_target_pairs={{0,16},{8,24},{16,0},{24,8},{1,17},{9,25},{17,1},{25,9},{2,18},{10... | collective-permute-start | bytes 4628 | tf_op jit(solution)/shard_map/ppermute | solution.py:94
  13.8 1.4 %collective-permute-done.6 = f32[385]{0:T(512)S(1)} collective-permute-done((f32[385]{0:T(512)S(1)}, f32[385]{0:T(512)S(1)}, u32[]{:S(2)}, u32[]{:S(2)}) %collective-permute-start.6) | collective-permute-done | bytes 1572 | tf_op jit(solution)/shard_map/ppermute | solution.py:94
  15.3 1.1 collective-permute-done.7
  16.4 0.5 slice.47
  17.0 2.1 %collective-permute-start.2 = (f32[67,256]{1,0:T(8,128)S(1)}, f32[67,256]{1,0:T(8,128)S(1)}, u32[]{:S(2)}, u32[]{:S(2)}) collective-permute-start(f32[67,256]{1,0:T(8,128)S(1)} %get-tuple-element.28), channel_id=1, source_target_pairs={{0,1},{1,0},{2,3},{3,2},{4,5},{5,4},{6,7},{7,6},{8,9},{9,8},{10,11... | collective-permute-start | bytes 205832 | tf_op jit(solution)/shard_map/ppermute | solution.py:94
  19.1 2.6 %collective-permute-start.3 = (f32[67,256]{1,0:T(8,128)S(1)}, f32[67,256]{1,0:T(8,128)S(1)}, u32[]{:S(2)}, u32[]{:S(2)}) collective-permute-start(f32[67,256]{1,0:T(8,128)S(1)} %get-tuple-element.27), channel_id=1, source_target_pairs={{0,2},{1,3},{2,0},{3,1},{4,6},{5,7},{6,4},{7,5},{8,10},{9,11},{10,... | collective-permute-start | bytes 205832 | tf_op jit(solution)/shard_map/ppermute | solution.py:94
  21.7 0.6 slice_divide_fusion
  22.4 5.6 %collective-permute-done.3 = f32[67,256]{1,0:T(8,128)S(1)} collective-permute-done((f32[67,256]{1,0:T(8,128)S(1)}, f32[67,256]{1,0:T(8,128)S(1)}, u32[]{:S(2)}, u32[]{:S(2)}) %collective-permute-start.3) | collective-permute-done | bytes 68640 | tf_op jit(solution)/shard_map/ppermute | solution.py:94
  28.0 1.5 %collective-permute-start.8 = (f32[65,256]{1,0:T(8,128)S(1)}, f32[65,256]{1,0:T(8,128)S(1)}, u32[]{:S(2)}, u32[]{:S(2)}) collective-permute-start(f32[65,256]{1,0:T(8,128)S(1)} %pad_maximum_fusion.7), channel_id=1, source_target_pairs={{0,1},{1,0},{2,3},{3,2},{4,5},{5,4},{6,7},{7,6},{8,9},{9,8},{10,11... | collective-permute-start | bytes 199688 | tf_op jit(solution)/shard_map/ppermute | solution.py:94
  29.5 1.6 %collective-permute-start.9 = (f32[65,256]{1,0:T(8,128)S(1)}, f32[65,256]{1,0:T(8,128)S(1)}, u32[]{:S(2)}, u32[]{:S(2)}) collective-permute-start(f32[65,256]{1,0:T(8,128)S(1)} %pad_maximum_fusion.7), channel_id=1, source_target_pairs={{0,2},{1,3},{2,0},{3,1},{4,6},{5,7},{6,4},{7,5},{8,10},{9,11},{10,... | collective-permute-start | bytes 199688 | tf_op jit(solution)/shard_map/ppermute | solution.py:94
  31.2 1.3 %collective-permute-start.10 = (f32[65,256]{1,0:T(8,128)S(1)}, f32[65,256]{1,0:T(8,128)S(1)}, u32[]{:S(2)}, u32[]{:S(2)}) collective-permute-start(f32[65,256]{1,0:T(8,128)S(1)} %pad_maximum_fusion.7), channel_id=1, source_target_pairs={{0,3},{1,2},{2,1},{3,0},{4,7},{5,6},{6,5},{7,4},{8,11},{9,10},{10,... | collective-permute-start | bytes 199688 | tf_op jit(solution)/shard_map/ppermute | solution.py:94
  32.7 1.0 select_reduce_fusion.2
  34.5 3.1 %collective-permute-done.9 = f32[65,256]{1,0:T(8,128)S(1)} collective-permute-done((f32[65,256]{1,0:T(8,128)S(1)}, f32[65,256]{1,0:T(8,128)S(1)}, u32[]{:S(2)}, u32[]{:S(2)}) %collective-permute-start.9) | collective-permute-done | bytes 66592 | tf_op jit(solution)/shard_map/ppermute | solution.py:94
  37.7 0.8 select_add_fusion.2.v_ref
  38.5 11.5 %inverse.3 = f32[256,256]{1,0:T(8,128)} custom-call(f32[256,256]{1,0:T(8,128)} %select_add_fusion.2.v_ref), custom_call_target="tpu_custom_call" | custom-call | tf_op jit(solution)/shard_map/inverse/pallas_call | solution.py:75
  50.0 0.6 fusion.22
  50.7 0.9 copy-done.2
  51.6 0.6 fusion
  52.2 0.6 fusion.6
  52.8 1.6 %collective-permute-start.13 = (f32[128,256]{1,0:T(8,128)S(1)}, f32[128,256]{1,0:T(8,128)S(1)}, u32[]{:S(2)}, u32[]{:S(2)}) collective-permute-start(f32[128,256]{1,0:T(8,128)S(1)} %fusion.6), channel_id=1, source_target_pairs={{0,8},{8,0},{16,24},{24,16},{1,9},{9,1},{17,25},{25,17},{2,10},{10... | collective-permute-start | bytes 393224 | tf_op jit(solution)/shard_map/ppermute | solution.py:94
  54.4 0.7 slice_divide_fusion.1
  55.1 3.7 %collective-permute-done.13 = f32[128,256]{1,0:T(8,128)S(1)} collective-permute-done((f32[128,256]{1,0:T(8,128)S(1)}, f32[128,256]{1,0:T(8,128)S(1)}, u32[]{:S(2)}, u32[]{:S(2)}) %collective-permute-start.13) | collective-permute-done | bytes 131104 | tf_op jit(solution)/shard_map/ppermute | solution.py:94
  58.8 1.6 %collective-permute-start.14 = (f32[128,256]{1,0:T(8,128)S(1)}, f32[128,256]{1,0:T(8,128)S(1)}, u32[]{:S(2)}, u32[]{:S(2)}) collective-permute-start(f32[128,256]{1,0:T(8,128)S(1)} %add.150), channel_id=1, source_target_pairs={{0,16},{8,24},{16,0},{24,8},{1,17},{9,25},{17,1},{25,9},{2,18},{10... | collective-permute-start | bytes 393224 | tf_op jit(solution)/shard_map/ppermute | solution.py:94
  60.4 0.7 fusion.4
  61.1 1.6 %collective-permute-start.16 = (f32[128,256]{1,0:T(8,128)S(1)}, f32[128,256]{1,0:T(8,128)S(1)}, u32[]{:S(2)}, u32[]{:S(2)}) collective-permute-start(f32[128,256]{1,0:T(8,128)S(1)} %fusion.4), channel_id=1, source_target_pairs={{0,8},{8,0},{16,24},{24,16},{1,9},{9,1},{17,25},{25,17},{2,10},{10... | collective-permute-start | bytes 393224 | tf_op jit(solution)/shard_map/ppermute | solution.py:94
  62.7 1.3 %collective-permute-done.14 = f32[128,256]{1,0:T(8,128)S(1)} collective-permute-done((f32[128,256]{1,0:T(8,128)S(1)}, f32[128,256]{1,0:T(8,128)S(1)}, u32[]{:S(2)}, u32[]{:S(2)}) %collective-permute-start.14) | collective-permute-done | bytes 131104 | tf_op jit(solution)/shard_map/ppermute | solution.py:94
  64.1 2.1 %collective-permute-done.16 = f32[128,256]{1,0:T(8,128)S(1)} collective-permute-done((f32[128,256]{1,0:T(8,128)S(1)}, f32[128,256]{1,0:T(8,128)S(1)}, u32[]{:S(2)}, u32[]{:S(2)}) %collective-permute-start.16) | collective-permute-done | bytes 131104 | tf_op jit(solution)/shard_map/ppermute | solution.py:94
  66.2 0.6 collective-permute-start.17
  66.9 4.3 %collective-permute-done.17 = f32[128,256]{1,0:T(8,128)S(1)} collective-permute-done((f32[128,256]{1,0:T(8,128)S(1)}, f32[128,256]{1,0:T(8,128)S(1)}, u32[]{:S(2)}, u32[]{:S(2)}) %collective-permute-start.17) | collective-permute-done | bytes 131104 | tf_op jit(solution)/shard_map/ppermute | solution.py:94
  71.2 1.4 %collective-permute-start.18 = (f32[128,256]{1,0:T(8,128)S(1)}, f32[128,256]{1,0:T(8,128)S(1)}, u32[]{:S(2)}, u32[]{:S(2)}) collective-permute-start(f32[128,256]{1,0:T(8,128)S(1)} %broadcast_multiply_fusion), channel_id=1, source_target_pairs={{0,1},{1,0},{2,3},{3,2},{4,5},{5,4},{6,7},{7,6},{8,9},{9,8},{10,11... | collective-permute-start | bytes 393224 | tf_op jit(solution)/shard_map/ppermute | solution.py:94
  72.6 0.7 select_reduce_fusion.1
  74.0 3.3 %collective-permute-done.18 = f32[128,256]{1,0:T(8,128)S(1)} collective-permute-done((f32[128,256]{1,0:T(8,128)S(1)}, f32[128,256]{1,0:T(8,128)S(1)}, u32[]{:S(2)}, u32[]{:S(2)}) %collective-permute-start.18) | collective-permute-done | bytes 131104 | tf_op jit(solution)/shard_map/ppermute | solution.py:94
  77.3 1.4 %collective-permute-start.19 = (f32[128,256]{1,0:T(8,128)S(1)}, f32[128,256]{1,0:T(8,128)S(1)}, u32[]{:S(2)}, u32[]{:S(2)}) collective-permute-start(f32[128,256]{1,0:T(8,128)S(1)} %add.155), channel_id=1, source_target_pairs={{0,2},{1,3},{2,0},{3,1},{4,6},{5,7},{6,4},{7,5},{8,10},{9,11},{10,... | collective-permute-start | bytes 393224 | tf_op jit(solution)/shard_map/ppermute | solution.py:94
  78.8 0.7 select_add_fusion.1.v_ref
  79.5 11.5 %inverse.4 = f32[256,256]{1,0:T(8,128)} custom-call(f32[256,256]{1,0:T(8,128)} %select_add_fusion.1.v_ref), custom_call_target="tpu_custom_call" | custom-call | tf_op jit(solution)/shard_map/inverse/pallas_call | solution.py:75
  91.0 1.2 %fusion.14 = f32[128,256]{1,0:T(8,128)S(1)} fusion(f32[256,256]{1,0:T(8,128)} %inverse.4, f32[128,256]{1,0:T(8,128)S(1)} %add.155, f32[128,256]{1,0:T(8,128)S(1)} %collective-permute-done.19), kind=kOutput, calls=%fused_computation.37 | convolution fusion | flops 100696064 | bytes 655360 | tf_op jit(solution)/shard_map/dot_general | solution.py:15
  92.3 0.4 fusion.35
  92.8 0.8 broadcast_divide_fusion
  93.6 0.7 collective-permute-done.20
  94.4 0.7 multiply_reduce_fusion
  95.2 0.7 select_reduce_fusion
  96.7 1.1 collective-permute-start.22
  97.8 1.6 %collective-permute-start.23 = (f32[1,256]{1,0:T(1,128)S(1)}, f32[1,256]{1,0:T(1,128)S(1)}, u32[]{:S(2)}, u32[]{:S(2)}) collective-permute-start(f32[1,256]{1,0:T(1,128)S(1)} %add.161), channel_id=1, source_target_pairs={{0,2},{1,3},{2,0},{3,1},{4,6},{5,7},{6,4},{7,5},{8,10},{9,11},{10,... | collective-permute-start | bytes 3080 | tf_op jit(solution)/shard_map/ppermute | solution.py:94
  99.4 1.7 %collective-permute-start.24 = (f32[1,256]{1,0:T(1,128)S(1)}, f32[1,256]{1,0:T(1,128)S(1)}, u32[]{:S(2)}, u32[]{:S(2)}) collective-permute-start(f32[1,256]{1,0:T(1,128)S(1)} %add.161), channel_id=1, source_target_pairs={{0,3},{1,2},{2,1},{3,0},{4,7},{5,6},{6,5},{7,4},{8,11},{9,10},{10,... | collective-permute-start | bytes 3080 | tf_op jit(solution)/shard_map/ppermute | solution.py:94
  101.1 0.7 select_add_fusion.v_ref
  101.8 11.5 %inverse.5 = f32[256,256]{1,0:T(8,128)} custom-call(f32[256,256]{1,0:T(8,128)} %select_add_fusion.v_ref), custom_call_target="tpu_custom_call" | custom-call | tf_op jit(solution)/shard_map/inverse/pallas_call | solution.py:75
  113.5 1.2 %multiply_reduce_fusion.1 = (f32[256]{0:T(256)S(1)}, f32[4,256]{1,0:T(4,128)S(1)}) fusion(f32[4,256]{1,0:T(4,128)S(1)} %dynamic_update_slice.51, f32[256,256]{1,0:T(8,128)} %inverse.5), kind=kOutput, calls=%fused_computation.70 | convolution fusion | flops 3147520 | bytes 271360 | tf_op jit(solution)/shard_map/dot_general | solution.py:15
  114.7 0.6 fusion.26
  (76 shorter events, 1.6 us)
Async XLA Ops:
  0.6 0.7 copy-start.3
  3.8 1.0 copy-start
  3.9 2.0 %copy-start.1 = (f32[128,256]{1,0:T(8,128)S(1)}, f32[128,256]{1,0:T(8,128)}, u32[]{:S(2)}) copy-start(f32[128,256]{1,0:T(8,128)} %param.4) | copy-start | bytes 393220
  3.9 12.9 %collective-permute-start = (f32[256,256]{1,0:T(8,128)S(1)}, f32[256,256]{1,0:T(8,128)S(1)}, u32[]{:S(2)}, u32[]{:S(2)}) collective-permute-start(f32[256,256]{1,0:T(8,128)S(1)} %bitcast.75), channel_id=1, source_target_pairs={{0,4},{4,0},{1,5},{5,1},{2,6},{6,2},{3,7},{7,3},{8,12},{12,8},{9,1... | collective-permute-start | bytes 786440 | tf_op jit(solution)/shard_map/ppermute | solution.py:94
  5.4 8.4 %collective-permute-start.1 = (f32[512]{0:T(512)S(1)}, f32[512]{0:T(512)S(1)}, u32[]{:S(2)}, u32[]{:S(2)}) collective-permute-start(f32[512]{0:T(512)S(1)} %get-tuple-element.8), channel_id=1, source_target_pairs={{0,4},{4,0},{1,5},{5,1},{2,6},{6,2},{3,7},{7,3},{8,12},{12,8},{9,1... | collective-permute-start | bytes 6152 | tf_op jit(solution)/shard_map/ppermute | solution.py:94
  6.8 4.1 %collective-permute-start.5 = (f32[385]{0:T(512)S(1)}, f32[385]{0:T(512)S(1)}, u32[]{:S(2)}, u32[]{:S(2)}) collective-permute-start(f32[385]{0:T(512)S(1)} %pad_maximum_fusion.8), channel_id=1, source_target_pairs={{0,8},{8,0},{16,24},{24,16},{1,9},{9,1},{17,25},{25,17},{2,10},{10... | collective-permute-start | bytes 4628 | tf_op jit(solution)/shard_map/ppermute | solution.py:94
  9.7 23.0 %collective-permute-start.12 = (f32[256,256]{1,0:T(8,128)S(1)}, f32[256,256]{1,0:T(8,128)S(1)}, u32[]{:S(2)}, u32[]{:S(2)}) collective-permute-start(f32[256,256]{1,0:T(8,128)S(1)} %fusion.34), channel_id=1, source_target_pairs={{0,4},{4,0},{1,5},{5,1},{2,6},{6,2},{3,7},{7,3},{8,12},{12,8},{9,1... | collective-permute-start | bytes 786440 | tf_op jit(solution)/shard_map/ppermute | solution.py:94
  11.6 3.6 %collective-permute-start.6 = (f32[385]{0:T(512)S(1)}, f32[385]{0:T(512)S(1)}, u32[]{:S(2)}, u32[]{:S(2)}) collective-permute-start(f32[385]{0:T(512)S(1)} %fusion.30), channel_id=1, source_target_pairs={{0,16},{8,24},{16,0},{24,8},{1,17},{9,25},{17,1},{25,9},{2,18},{10... | collective-permute-start | bytes 4628 | tf_op jit(solution)/shard_map/ppermute | solution.py:94
  15.2 1.2 %collective-permute-start.7 = (f32[257]{0:T(512)S(1)}, f32[257]{0:T(512)S(1)}, u32[]{:S(2)}, u32[]{:S(2)}) collective-permute-start(f32[257]{0:T(512)S(1)} %bitcast.81), channel_id=1, source_target_pairs={{0,4},{4,0},{1,5},{5,1},{2,6},{6,2},{3,7},{7,3},{8,12},{12,8},{9,1... | collective-permute-start | bytes 3092 | tf_op jit(solution)/shard_map/ppermute | solution.py:94
  17.0 5.4 %collective-permute-start.2 = (f32[67,256]{1,0:T(8,128)S(1)}, f32[67,256]{1,0:T(8,128)S(1)}, u32[]{:S(2)}, u32[]{:S(2)}) collective-permute-start(f32[67,256]{1,0:T(8,128)S(1)} %get-tuple-element.28), channel_id=1, source_target_pairs={{0,1},{1,0},{2,3},{3,2},{4,5},{5,4},{6,7},{7,6},{8,9},{9,8},{10,11... | collective-permute-start | bytes 205832 | tf_op jit(solution)/shard_map/ppermute | solution.py:94
  19.1 8.9 %collective-permute-start.3 = (f32[67,256]{1,0:T(8,128)S(1)}, f32[67,256]{1,0:T(8,128)S(1)}, u32[]{:S(2)}, u32[]{:S(2)}) collective-permute-start(f32[67,256]{1,0:T(8,128)S(1)} %get-tuple-element.27), channel_id=1, source_target_pairs={{0,2},{1,3},{2,0},{3,1},{4,6},{5,7},{6,4},{7,5},{8,10},{9,11},{10,... | collective-permute-start | bytes 205832 | tf_op jit(solution)/shard_map/ppermute | solution.py:94
  21.7 6.3 %collective-permute-start.4 = (f32[67,256]{1,0:T(8,128)S(1)}, f32[67,256]{1,0:T(8,128)S(1)}, u32[]{:S(2)}, u32[]{:S(2)}) collective-permute-start(f32[67,256]{1,0:T(8,128)S(1)} %get-tuple-element.26), channel_id=1, source_target_pairs={{0,3},{1,2},{2,1},{3,0},{4,7},{5,6},{6,5},{7,4},{8,11},{9,10},{10,... | collective-permute-start | bytes 205832 | tf_op jit(solution)/shard_map/ppermute | solution.py:94
  28.0 6.4 %collective-permute-start.8 = (f32[65,256]{1,0:T(8,128)S(1)}, f32[65,256]{1,0:T(8,128)S(1)}, u32[]{:S(2)}, u32[]{:S(2)}) collective-permute-start(f32[65,256]{1,0:T(8,128)S(1)} %pad_maximum_fusion.7), channel_id=1, source_target_pairs={{0,1},{1,0},{2,3},{3,2},{4,5},{5,4},{6,7},{7,6},{8,9},{9,8},{10,11... | collective-permute-start | bytes 199688 | tf_op jit(solution)/shard_map/ppermute | solution.py:94
  29.5 8.1 %collective-permute-start.9 = (f32[65,256]{1,0:T(8,128)S(1)}, f32[65,256]{1,0:T(8,128)S(1)}, u32[]{:S(2)}, u32[]{:S(2)}) collective-permute-start(f32[65,256]{1,0:T(8,128)S(1)} %pad_maximum_fusion.7), channel_id=1, source_target_pairs={{0,2},{1,3},{2,0},{3,1},{4,6},{5,7},{6,4},{7,5},{8,10},{9,11},{10,... | collective-permute-start | bytes 199688 | tf_op jit(solution)/shard_map/ppermute | solution.py:94
  31.2 6.4 %collective-permute-start.10 = (f32[65,256]{1,0:T(8,128)S(1)}, f32[65,256]{1,0:T(8,128)S(1)}, u32[]{:S(2)}, u32[]{:S(2)}) collective-permute-start(f32[65,256]{1,0:T(8,128)S(1)} %pad_maximum_fusion.7), channel_id=1, source_target_pairs={{0,3},{1,2},{2,1},{3,0},{4,7},{5,6},{6,5},{7,4},{8,11},{9,10},{10,... | collective-permute-start | bytes 199688 | tf_op jit(solution)/shard_map/ppermute | solution.py:94
  37.7 13.0 %collective-permute-start.11 = (f32[256,256]{1,0:T(8,128)S(1)}, f32[256,256]{1,0:T(8,128)S(1)}, u32[]{:S(2)}, u32[]{:S(2)}) collective-permute-start(f32[256,256]{1,0:T(8,128)S(1)} %bitcast.74), channel_id=1, source_target_pairs={{0,4},{4,0},{1,5},{5,1},{2,6},{6,2},{3,7},{7,3},{8,12},{12,8},{9,1... | collective-permute-start | bytes 786440 | tf_op jit(solution)/shard_map/ppermute | solution.py:94
  50.7 1.0 copy-start.2
  52.8 6.0 %collective-permute-start.13 = (f32[128,256]{1,0:T(8,128)S(1)}, f32[128,256]{1,0:T(8,128)S(1)}, u32[]{:S(2)}, u32[]{:S(2)}) collective-permute-start(f32[128,256]{1,0:T(8,128)S(1)} %fusion.6), channel_id=1, source_target_pairs={{0,8},{8,0},{16,24},{24,16},{1,9},{9,1},{17,25},{25,17},{2,10},{10... | collective-permute-start | bytes 393224 | tf_op jit(solution)/shard_map/ppermute | solution.py:94
  58.8 5.1 %collective-permute-start.14 = (f32[128,256]{1,0:T(8,128)S(1)}, f32[128,256]{1,0:T(8,128)S(1)}, u32[]{:S(2)}, u32[]{:S(2)}) collective-permute-start(f32[128,256]{1,0:T(8,128)S(1)} %add.150), channel_id=1, source_target_pairs={{0,16},{8,24},{16,0},{24,8},{1,17},{9,25},{17,1},{25,9},{2,18},{10... | collective-permute-start | bytes 393224 | tf_op jit(solution)/shard_map/ppermute | solution.py:94
  61.1 5.0 %collective-permute-start.16 = (f32[128,256]{1,0:T(8,128)S(1)}, f32[128,256]{1,0:T(8,128)S(1)}, u32[]{:S(2)}, u32[]{:S(2)}) collective-permute-start(f32[128,256]{1,0:T(8,128)S(1)} %fusion.4), channel_id=1, source_target_pairs={{0,8},{8,0},{16,24},{24,16},{1,9},{9,1},{17,25},{25,17},{2,10},{10... | collective-permute-start | bytes 393224 | tf_op jit(solution)/shard_map/ppermute | solution.py:94
  64.0 2.8 %collective-permute-start.15 = (f32[128,256]{1,0:T(8,128)S(1)}, f32[128,256]{1,0:T(8,128)S(1)}, u32[]{:S(2)}, u32[]{:S(2)}) collective-permute-start(f32[128,256]{1,0:T(8,128)S(1)} %add.151), channel_id=1, source_target_pairs={{0,4},{4,0},{1,5},{5,1},{2,6},{6,2},{3,7},{7,3},{8,12},{12,8},{9,1... | collective-permute-start | bytes 393224 | tf_op jit(solution)/shard_map/ppermute | solution.py:94
  66.2 5.0 %collective-permute-start.17 = (f32[128,256]{1,0:T(8,128)S(1)}, f32[128,256]{1,0:T(8,128)S(1)}, u32[]{:S(2)}, u32[]{:S(2)}) collective-permute-start(f32[128,256]{1,0:T(8,128)S(1)} %add.153), channel_id=1, source_target_pairs={{0,16},{8,24},{16,0},{24,8},{1,17},{9,25},{17,1},{25,9},{2,18},{10... | collective-permute-start | bytes 393224 | tf_op jit(solution)/shard_map/ppermute | solution.py:94
  71.2 6.1 %collective-permute-start.18 = (f32[128,256]{1,0:T(8,128)S(1)}, f32[128,256]{1,0:T(8,128)S(1)}, u32[]{:S(2)}, u32[]{:S(2)}) collective-permute-start(f32[128,256]{1,0:T(8,128)S(1)} %broadcast_multiply_fusion), channel_id=1, source_target_pairs={{0,1},{1,0},{2,3},{3,2},{4,5},{5,4},{6,7},{7,6},{8,9},{9,8},{10,11... | collective-permute-start | bytes 393224 | tf_op jit(solution)/shard_map/ppermute | solution.py:94
  77.3 13.7 %collective-permute-start.19 = (f32[128,256]{1,0:T(8,128)S(1)}, f32[128,256]{1,0:T(8,128)S(1)}, u32[]{:S(2)}, u32[]{:S(2)}) collective-permute-start(f32[128,256]{1,0:T(8,128)S(1)} %add.155), channel_id=1, source_target_pairs={{0,2},{1,3},{2,0},{3,1},{4,6},{5,7},{6,4},{7,5},{8,10},{9,11},{10,... | collective-permute-start | bytes 393224 | tf_op jit(solution)/shard_map/ppermute | solution.py:94
  92.7 1.6 %collective-permute-start.20 = (f32[256,256]{1,0:T(8,128)S(1)}, f32[256,256]{1,0:T(8,128)S(1)}, u32[]{:S(2)}, u32[]{:S(2)}) collective-permute-start(f32[256,256]{1,0:T(8,128)S(1)} %fusion.35), channel_id=1, source_target_pairs={{0,4},{4,0},{1,5},{5,1},{2,6},{6,2},{3,7},{7,3},{8,12},{12,8},{9,1... | collective-permute-start | bytes 786440 | tf_op jit(solution)/shard_map/ppermute | solution.py:94
  95.1 1.5 %collective-permute-start.21 = (f32[1,256]{1,0:T(1,128)S(1)}, f32[1,256]{1,0:T(1,128)S(1)}, u32[]{:S(2)}, u32[]{:S(2)}) collective-permute-start(f32[1,256]{1,0:T(1,128)S(1)} %bitcast.82), channel_id=1, source_target_pairs={{0,4},{4,0},{1,5},{5,1},{2,6},{6,2},{3,7},{7,3},{8,12},{12,8},{9,1... | collective-permute-start | bytes 3080 | tf_op jit(solution)/shard_map/ppermute | solution.py:94
  96.7 16.7 %collective-permute-start.22 = (f32[1,256]{1,0:T(1,128)S(1)}, f32[1,256]{1,0:T(1,128)S(1)}, u32[]{:S(2)}, u32[]{:S(2)}) collective-permute-start(f32[1,256]{1,0:T(1,128)S(1)} %add.161), channel_id=1, source_target_pairs={{0,1},{1,0},{2,3},{3,2},{4,5},{5,4},{6,7},{7,6},{8,9},{9,8},{10,11... | collective-permute-start | bytes 3080 | tf_op jit(solution)/shard_map/ppermute | solution.py:94
  97.8 15.6 %collective-permute-start.23 = (f32[1,256]{1,0:T(1,128)S(1)}, f32[1,256]{1,0:T(1,128)S(1)}, u32[]{:S(2)}, u32[]{:S(2)}) collective-permute-start(f32[1,256]{1,0:T(1,128)S(1)} %add.161), channel_id=1, source_target_pairs={{0,2},{1,3},{2,0},{3,1},{4,6},{5,7},{6,4},{7,5},{8,10},{9,11},{10,... | collective-permute-start | bytes 3080 | tf_op jit(solution)/shard_map/ppermute | solution.py:94
  99.4 14.1 %collective-permute-start.24 = (f32[1,256]{1,0:T(1,128)S(1)}, f32[1,256]{1,0:T(1,128)S(1)}, u32[]{:S(2)}, u32[]{:S(2)}) collective-permute-start(f32[1,256]{1,0:T(1,128)S(1)} %add.161), channel_id=1, source_target_pairs={{0,3},{1,2},{2,1},{3,0},{4,7},{5,6},{6,5},{7,4},{8,11},{9,10},{10,... | collective-permute-start | bytes 3080 | tf_op jit(solution)/shard_map/ppermute | solution.py:94
where the time goes:
time: 116 us; the launch traced here: 115 us
  Pallas kernels  34.6 us (30%)
  starting transfers between devices  28 us (24%)
  waiting for transfers between devices  27.4 us (24%)
  other arithmetic  9.81 us (8%)
  matrix products  8.59 us (7%)
  local copies, waits for them, and re-layouts  3.91 us (3%)
  between operations  3.08 us (3%)
    pallas_call x3, Pallas kernels, inverse(): pl.pallas_call(inverse_kernel, out_shape=jax.ShapeDtypeStruct((n, n), jnp...  34.6 us
    ppermute x25, starting transfers between devices, swap(): return lax.ppermute(x, axis, [(i, i ^ bit) for i in range(n)])  28 us
    ppermute x25, waiting for transfers between devices, swap(): return lax.ppermute(x, axis, [(i, i ^ bit) for i in range(n)])  27.4 us
    dot_general x11, matrix products, dot(): return jnp.dot(a, b, precision=hp, preferred_element_type=jnp.float32)  8.59 us
  transfers between devices with their start and end apart: 25, of which 11 were waited for; matrix products, arithmetic and copies ran while one was open for 11% of the time, Pallas kernels for 30%

commit v1 on v0

v1 whole, which is shorter than its diff:
```python
import jax
import jax.numpy as jnp
from jax import lax
from jax.experimental import pallas as pl
from jax.experimental.pallas import tpu as pltpu
from jax.sharding import PartitionSpec as P


ridge = 0.2
eps = 1e-06
hp = lax.Precision.HIGHEST
block = 32


def dot(a, b):
    return jnp.dot(a, b, precision=hp, preferred_element_type=jnp.float32)


def pivot_panel(panel):
    groups, tiles = len(panel), len(panel[0])
    lane = lax.broadcasted_iota(jnp.int32, (8, 128), 1)
    sub = lax.broadcasted_iota(jnp.int32, (8, 128), 0)
    part = [list(r) for r in panel]
    for g in range(groups):
        cols = [
            [jnp.broadcast_to(part[h][0][:, 8 * g + q : 8 * g + q + 1], (8, 128)) for h in range(groups)]
            for q in range(8)
        ]
        for q in range(8):
            col = cols[q]
            inv = 1.0 / jnp.broadcast_to(col[g][q : q + 1, :], (8, 128))
            here = lane == 8 * g + q
            this = sub == q
            rows = []
            for t in range(tiles):
                row = jnp.broadcast_to(part[g][t][q : q + 1, :], (8, 128))
                if t == 0:
                    row = jnp.where(here, 1.0, row)
                rows.append(row * inv)
            for h in range(groups):
                for t in range(tiles):
                    base = jnp.where(here, 0.0, part[h][t]) if t == 0 else part[h][t]
                    new = base - col[h] * rows[t]
                    part[h][t] = jnp.where(this, rows[t], new) if h == g else new
            for q2 in range(q + 1, 8):
                factor = jnp.broadcast_to(cols[q2][g][q : q + 1, :], (8, 128)) * inv
                for h in range(groups):
                    new = cols[q2][h] - col[h] * factor
                    cols[q2][h] = jnp.where(this, factor, new) if h == g else new
    return jnp.concatenate([jnp.concatenate(r, axis=1) for r in part], axis=0)


def eliminate(a_ref, count):
    n = a_ref.shape[0]

    def step(_, carry):
        panel = [
            [a_ref[8 * g : 8 * g + 8, 128 * t : 128 * t + 128] for t in range(n // 128)]
            for g in range(block // 8)
        ]
        top = pivot_panel(panel)
        rest = a_ref[block:, :]
        lane = lax.broadcasted_iota(jnp.int32, rest.shape, 1)
        new = jnp.where(lane < block, 0.0, rest) - dot(rest[:, :block], top)
        a_ref[: n - block, :] = pltpu.roll(new, n - block, 1)
        a_ref[n - block :, :] = pltpu.roll(top, n - block, 1)
        return carry

    lax.fori_loop(0, count, step, 0)


def near(x):
    return pltpu.with_memory_space_constraint(x, pltpu.VMEM)


def call(kernel, outs, *args, smem=0, scratch=()):
    specs = [pl.BlockSpec(memory_space=pltpu.SMEM)] * smem
    specs += [pl.BlockSpec(memory_space=pltpu.VMEM)] * (len(args) - smem)
    many = isinstance(outs, list)
    shapes = [pltpu.VMEM(s, jnp.float32) for s in (outs if many else [outs])]
    vmem = [pl.BlockSpec(memory_space=pltpu.VMEM)] * len(shapes)
    return pl.pallas_call(
        kernel,
        out_shape=shapes if many else shapes[0],
        in_specs=specs,
        out_specs=vmem if many else vmem[0],
        scratch_shapes=scratch,
    )(*args[:smem], *[near(a) for a in args[smem:]])


def inverse_piece(state, count):
    def kernel(v_ref, o_ref):
        o_ref[...] = v_ref[...]
        eliminate(o_ref, count)

    return call(kernel, state.shape, state)


def inverse_and_unit(state, count, raw, scale):
    def kernel(v_ref, raw_ref, scale_ref, o_ref, unit_ref, buf, sem):
        buf[...] = raw_ref[...] / scale_ref[...]
        copy = pltpu.make_async_copy(buf, unit_ref, sem)
        copy.start()
        o_ref[...] = v_ref[...]
        eliminate(o_ref, count)
        copy.wait()

    vmem = pl.BlockSpec(memory_space=pltpu.VMEM)
    return pl.pallas_call(
        kernel,
        out_shape=[pltpu.VMEM(state.shape, jnp.float32), jax.ShapeDtypeStruct(raw.shape, jnp.float32)],
        in_specs=[vmem] * 3,
        out_specs=[vmem, pl.BlockSpec(memory_space=pl.ANY)],
        scratch_shapes=[pltpu.VMEM(raw.shape, jnp.float32), pltpu.SemaphoreType.DMA(())],
        name="inverse_unit",
    )(near(state), near(raw), near(scale))


def eye(n):
    return lax.broadcasted_iota(jnp.int32, (n, n), 0) == lax.broadcasted_iota(jnp.int32, (n, n), 1)


def outer(a, b):
    return lax.dot_general(a, b, (((0,), (0,)), ((), ())), precision=hp, preferred_element_type=jnp.float32)


def ridged(h):
    n = h.shape[0]
    on = eye(n)
    diag = jnp.where(on, h, 0.0)
    trace = jnp.sum(jnp.sum(diag, axis=0, keepdims=True), axis=1, keepdims=True)
    return h + jnp.where(on, trace * (ridge / n), 0.0)


def normalised(gram, count):
    diag = jnp.where(eye(gram.shape[0]), gram, 0.0)
    one = jnp.sqrt(jnp.sum(diag, axis=0, keepdims=True) / count + eps)
    two = jnp.sqrt(jnp.sum(diag, axis=1, keepdims=True) / count + eps)
    return one, gram * (1.0 / two) * (1.0 / one)


def after(x, *deps):
    return lax.optimization_barrier((x,) + deps)[0]


def swap(x, axis, bit):
    n = lax.axis_size(axis)
    return lax.ppermute(x, axis, [(i, i ^ bit) for i in range(n)])


def bits(axis):
    n = lax.axis_size(axis)
    return [1 << b for b in range(n.bit_length() - 1)]


def total(x, axis, some=None):
    for bit in bits(axis) if some is None else some:
        x = x + swap(x, axis, bit)
    return x


def total_crossed(x, axis, side):
    n, m = lax.axis_size(axis), lax.axis_size(side)
    order = bits(axis)
    for one, two in zip(order, reversed(order)):
        pairs = [(i * m + j, (i ^ (two if j & 1 else one)) * m + j) for i in range(n) for j in range(m)]
        x = x + lax.ppermute(x, (axis, side), pairs)
    return x


def gather_rows(x, axis):
    me = lax.axis_index(axis)
    for bit in bits(axis):
        other = swap(x, axis, bit)
        mine = (me & bit) != 0
        x = jnp.concatenate([jnp.where(mine, other, x), jnp.where(mine, x, other)], axis=0)
    return x


def open_kernel(pick_ref, f_ref, b_ref, w_ref, give_ref, row_ref, f_out_ref, b_out_ref, w_out_ref):
    f = f_ref[...]
    half = f.shape[0] // 2
    at = pl.multiple_of(pick_ref[0] * half, half)
    give_ref[:half, :] = dot(f_ref[pl.ds(at, half), :], b_ref[...] * w_ref[...])
    row = lax.dot_general(
        jnp.ones((8, f.shape[1]), jnp.float32), f, (((1,), (1,)), ((), ())), precision=hp, preferred_element_type=jnp.float32
    )[:1]
    row_ref[...] = row
    rank = give_ref.shape[1]
    give_ref[half:, :] = jnp.zeros_like(give_ref[half:, :])
    for n in range(f.shape[0] // rank):
        give_ref[half + n : half + n + 1, :] = row[:, n * rank : (n + 1) * rank]
    f_out_ref[...] = f
    b_out_ref[...] = b_ref[...]
    w_out_ref[...] = w_ref[...]


def rest_kernel(pick_ref, f_ref, b_ref, w_ref, keep_ref, small_ref, gram_ref):
    b = b_ref[...]
    half, cols = f_ref.shape[0] // 2, f_ref.shape[1]
    at = pl.multiple_of(pick_ref[0] * half, half)
    keep_ref[...] = dot(f_ref[pl.ds(at, half), :], b * w_ref[...])
    col = jnp.sum(f_ref[...], axis=0, keepdims=True)
    small_ref[...] = jnp.zeros_like(small_ref)
    small_ref[0:1, :] = dot(jnp.broadcast_to(col, (8, cols)), b)[:1]
    small_ref[1:2, :cols] = col
    small_ref[2:3, :] = jnp.broadcast_to(jnp.sum(col, axis=1, keepdims=True), (1, small_ref.shape[1]))
    gram_ref[...] = outer(b, b)


def cut_kernel(me_ref, own_ref, got_ref, row_ref, w_ref, *gives):
    half, rank = own_ref.shape
    chunk = half // len(gives)
    row = row_ref[...] + jnp.concatenate(
        [got_ref[half + n : half + n + 1, :] for n in range(row_ref.shape[1] // rank)], axis=1
    )
    for d, give in enumerate(gives):
        at = pl.multiple_of((me_ref[0] ^ d) * chunk, chunk)
        give[:chunk, :] = own_ref[pl.ds(at, chunk), :] + got_ref[pl.ds(at, chunk), :]
        give[chunk:, :] = jnp.zeros_like(give[chunk:, :])
        give[chunk : chunk + 1, :] = w_ref[...]
        for n in range(row_ref.shape[1] // rank):
            give[chunk + 1 + n : chunk + 2 + n, :] = row[:, n * rank : (n + 1) * rank]


def fold_kernel(*refs):
    *parts, heads_ref, small_ref, w_ref, give_ref, col_ref = refs
    chunk = give_ref.shape[0] - 8
    acc = parts[0][:chunk, :]
    for part in parts[1:]:
        acc = acc + part[:chunk, :]
    give_ref[:chunk, :] = acc
    grand = heads_ref[2:3, :]
    give_ref[chunk:, :] = jnp.zeros_like(give_ref[chunk:, :])
    give_ref[chunk : chunk + 1, :] = w_ref[...] * (heads_ref[0:1, :] / grand)
    cols = col_ref.shape[1]
    col_ref[...] = small_ref[1:2, :cols] / grand[:, :cols]


def first_kernel(me_ref, own_ref, other_ref, *refs):
    *parts, v_ref, gram_ref, row_ref, w_ref = refs
    rank = w_ref.shape[1]
    w_ref[...] = jnp.zeros_like(w_ref)
    row_ref[...] = jnp.zeros_like(row_ref)
    for d, part in enumerate(parts):
        chunk = part.shape[0] - 8
        at = me_ref[0] ^ d
        w_ref[pl.ds(at, 1), :] = part[chunk : chunk + 1, :]
        for n in range(row_ref.shape[1] // rank):
            row_ref[pl.ds(at, 1), n * rank : (n + 1) * rank] = part[chunk + 1 + n : chunk + 2 + n, :]
    gram = outer(w_ref[...], w_ref[...])
    gram_ref[...] = gram
    v_ref[...] = ridged((own_ref[...] + other_ref[...]) * gram)


def rows_kernel(me_ref, *refs):
    *parts, m_ref, shift_ref = refs
    shift_ref[...] = jnp.zeros_like(shift_ref)
    for d, part in enumerate(parts):
        chunk = part.shape[0] - 8
        at = me_ref[0] ^ d
        m_ref[pl.ds(pl.multiple_of(at * chunk, chunk), chunk), :] = part[:chunk, :]
        shift_ref[pl.ds(at, 1), :] = part[chunk : chunk + 1, :]


def exporter_kernel(
    me_ref, top_ref, own_ref, other_ref, row_all_ref, shift_ref, inv_ref, f_ref, col_ref, raw_ref, both_ref, m_ref, s_ref
):
    half = own_ref.shape[0]
    m_ref[pl.ds(pl.multiple_of(top_ref[0] * half, half), half), :] = own_ref[...]
    m_ref[pl.ds(pl.multiple_of((1 - top_ref[0]) * half, half), half), :] = other_ref[...]
    rank, cols = shift_ref.shape[1], f_ref.shape[1]
    s_ref[:, :rank] = shift_ref[...]
    week = lax.broadcasted_iota(jnp.int32, (s_ref.shape[0], cols), 0)
    s_ref[:, rank:] = jnp.where(week == me_ref[0], col_ref[...], 0.0)
    terms = outer(row_all_ref[...], s_ref[...])
    raw = dot(m_ref[...] - terms[:, :rank], inv_ref[...])
    raw_ref[...] = raw
    grams = both_ref.shape[0] - cols
    at = pl.multiple_of(top_ref[0] * grams, grams) if grams < rank else 0
    left = jnp.concatenate([raw_ref[:, pl.ds(at, grams)], f_ref[...] - terms[:, rank:]], axis=1)
    both_ref[...] = outer(left, raw)


def second_kernel(count, steps, g_ref, gram_c_ref, v_ref, gram_ref, scale_ref):
    scale, gram = normalised(g_ref[...], count)
    scale_ref[...] = scale
    gram_ref[...] = gram
    v_ref[...] = ridged(gram * gram_c_ref[...])
    eliminate(v_ref, steps)


def importer_kernel(own_ref, other_ref, scale_ref, inv_ref, t_ref, raw_ref, both_ref):
    raw = dot((own_ref[...] + other_ref[...]) / scale_ref[...], inv_ref[...])
    raw_ref[...] = raw
    rank = raw.shape[1]
    both_ref[:rank, :] = outer(raw, raw)
    both_ref[rank:, :] = jnp.zeros_like(both_ref[rank:, :])
    both_ref[rank : rank + 1, :] = jnp.sum(raw * t_ref[...], axis=0, keepdims=True)


def third_kernel(count, own_ref, other_ref, gram_a_ref, v_ref, scale_ref):
    rank = own_ref.shape[1]
    scale, gram = normalised(own_ref[:rank, :] + other_ref[:rank, :], count)
    scale_ref[...] = scale
    v_ref[...] = ridged(gram * gram_a_ref[...])


def week_kernel(*refs):
    *parts, scale_a_ref, scale_b_ref, inv_ref, o_ref, s_ref = refs
    s_ref[...] = jnp.zeros_like(s_ref)
    for i, part in enumerate(parts):
        s_ref[i : i + 1, :] = part[...] / scale_a_ref[...] / scale_b_ref[...]
    raw = dot(s_ref[...], inv_ref[...])
    scale = jnp.sqrt(jnp.sum(raw * raw, axis=0, keepdims=True) / len(parts) + eps)
    o_ref[...] = raw[:1] / scale


def shares(f, b, w, top, ni):
    rows, rank = f.shape[0], w.shape[1]
    if ni == 2 and rows % rank == 0 and rows // rank <= 7:
        give, row, f, b, w = pl.pallas_call(
            open_kernel,
            out_shape=[
                pltpu.VMEM(s, jnp.float32) for s in ((rows // 2 + 8, rank), (1, rows), f.shape, b.shape, w.shape)
            ],
            in_specs=[pl.BlockSpec(memory_space=pltpu.SMEM)] + [pl.BlockSpec(memory_space=pltpu.VMEM)] * 3,
            out_specs=[pl.BlockSpec(memory_space=pltpu.VMEM)] * 5,
            name="open",
        )(1 - top, f, b, w)
        got = swap(give, "imp", 1)
        keep, small, gram = call(rest_kernel, [(rows // 2, rank), (8, rank), (rank, rank)], top, f, b, w, smem=1)
        other = swap(gram, "imp", 1)
        return f, w, keep, got, row, small, gram, other
    low = bits("imp")[:-1]
    sums = jnp.sum(f, 1)[None]
    part = jnp.concatenate([dot(f, b * w).reshape(2, rows // 2, rank), jnp.zeros((2, 8, rank))], axis=1)
    part = total(part.at[:, rows // 2 : rows // 2 + rows // rank].set(sums.reshape(-1, rank)), "imp", low)
    keep = lax.dynamic_index_in_dim(part, top[0], 0, keepdims=False)[: rows // 2]
    got = swap(lax.dynamic_index_in_dim(part, 1 - top[0], 0, keepdims=False), "imp", ni // 2)
    row = part[0, rows // 2 : rows // 2 + rows // rank].reshape(1, rows)
    col = jnp.sum(f, 0)[None]
    wide = jnp.pad(col, ((0, 0), (0, rank - col.shape[1])))
    small = jnp.concatenate([dot(col, b), wide, jnp.full((1, rank), jnp.sum(col)), jnp.zeros((5, rank))], axis=0)
    gram = total(dot(b.T, b), "imp", low)
    return f, w, keep, got, row, small, gram, swap(gram, "imp", ni // 2)


def per_device(flows, importer_factor, week_factor):
    f = flows[0]
    w = week_factor
    rank = w.shape[1]
    rows, cols = f.shape
    weeks, ni, ne = lax.axis_size("wk"), lax.axis_size("imp"), lax.axis_size("exp")
    me_k = lax.axis_index("wk").astype(jnp.int32)[None]
    top = jnp.where((lax.axis_index("imp") & (ni // 2)) != 0, 1, 0).astype(jnp.int32)[None]
    steps = rank // block

    f, w, keep, got, row, small, gram_own, gram_other = shares(f, importer_factor, w, top, ni)
    small = small + swap(small, "exp", 1)

    chunk = keep.shape[0] // weeks
    gives = call(cut_kernel, [(chunk + 8, rank)] * weeks, me_k, keep, got, row, w, smem=1)
    got = [swap(g, "wk", d) if d else g for d, g in enumerate(gives)]
    for bit in bits("exp")[1:]:
        small = small + swap(small, "exp", bit)
    heads = total(small, "imp")
    give, col_mean = call(fold_kernel, [(chunk + 8, rank), (1, cols)], *got, heads, small, w)
    gathered = [swap(give, "wk", d) if d else give for d in range(weeks)]

    state, gram_c, row_all = call(
        first_kernel,
        [(rank, rank), (rank, rank), (-(-weeks // 8) * 8, rows)],
        me_k, after(gram_own, give), gram_other, *got,
        smem=1, scratch=[pltpu.VMEM((-(-weeks // 8) * 8, rank), jnp.float32)],
    )
    state = inverse_piece(state, steps // 2)
    *gathered, state = lax.optimization_barrier((*gathered, state))
    m_rows, shifts = call(rows_kernel, [(chunk * weeks, rank), (-(-weeks // 8) * 8, rank)], me_k, *gathered, smem=1)
    m_other = swap(m_rows, "imp", ni // 2)
    inv_a = inverse_piece(state, steps - steps // 2)

    grams = rank // 2 if ni == 2 and rank % 256 == 0 else rank
    raw_a, both = call(
        exporter_kernel,
        [(rows, rank), (grams + cols, rank)],
        me_k, top, m_rows, m_other, row_all, shifts, inv_a, f, col_mean,
        smem=2, scratch=[pltpu.VMEM((rows, rank), jnp.float32), pltpu.VMEM((-(-weeks // 8) * 8, rank + cols), jnp.float32)],
    )
    both = total_crossed(both, "exp", "imp")
    t = both[grams:]
    g_a = gather_rows(both[:grams], "imp") if grams < rank else both[:grams]

    def second(*refs):
        second_kernel(rows * ne, steps // 4, *refs)

    m_own = t * w
    m_got = swap(m_own, "wk", 1)
    state, gram_a, scale_a = call(second, [(rank, rank), (rank, rank), (1, rank)], g_a, gram_c)
    for bit in bits("wk")[1:]:
        state = inverse_piece(state, steps // 4)
        m_got, state = lax.optimization_barrier((m_got, state))
        m_own = m_own + m_got
        m_got = swap(m_own, "wk", bit)
    inv_b, fac_a = inverse_and_unit(after(state, m_own), steps - steps // 4 * len(bits("wk")), raw_a, scale_a)
    raw_b, both = call(importer_kernel, [(cols, rank), (rank + 8, rank)], m_own, m_got, scale_a, inv_b, t)
    for bit in bits("imp")[:-1]:
        both = both + swap(both, "imp", bit)
    got = swap(both, "imp", ni // 2)
    m_mine = both[rank : rank + 1] + got[rank : rank + 1]
    m_all = [m_mine] + [swap(m_mine, "wk", d) for d in range(1, weeks)]

    def third(*refs):
        third_kernel(cols * ni, *refs)

    state, scale_b = call(third, [(rank, rank), (1, rank)], both, got, after(gram_a, m_mine))
    inv_c, fac_b = inverse_and_unit(state, steps, raw_b, scale_b)
    scratch = [pltpu.VMEM((-(-weeks // 8) * 8, rank), jnp.float32)]
    fac_c = call(week_kernel, (1, rank), *m_all, scale_a, scale_b, inv_c, scratch=scratch)
    return (fac_a, fac_b, fac_c)


def solution(mesh):
    in_specs = (P("wk", "exp", "imp"), P("imp", None), P("wk", None))
    out_specs = (P("exp", None), P("imp", None), P("wk", None))

    return jax.shard_map(per_device, mesh=mesh, in_specs=in_specs, out_specs=out_specs, check_vma=False)
```

time: 116 us -> 84.3 us (0.73)
  other arithmetic: 9.81 us -> 0.16 us
  matrix products: 8.59 us -> 0 us
  waiting for transfers between devices: 27.4 us -> 18.9 us
  local copies, waits for them, and re-layouts: 3.91 us -> 0.58 us
  Pallas kernels: 34.6 us -> 37 us
  between operations: 3.08 us -> 0.88 us
  starting transfers between devices: 28 us -> 26.7 us
    ppermute x25 -> x19, waiting for transfers between devices: 27.4 us -> 9.42 us  [swap(): return lax.ppermute(x, axis, [(i, i ^ bit) for i in range(n)])]
    ppermute x0 -> x2, waiting for transfers between devices: none -> 9.46 us  [total_crossed(): x = x + lax.ppermute(x, (axis, side), pairs)]
    dot_general x11 -> x0, matrix products: 8.59 us -> none  [dot(): return jnp.dot(a, b, precision=hp, preferred_element_type=jnp.float32)]
    ppermute x25 -> x19, starting transfers between devices: 28 us -> 23.3 us  [swap(): return lax.ppermute(x, axis, [(i, i ^ bit) for i in range(n)])]
    ppermute x0 -> x2, starting transfers between devices: none -> 3.42 us  [total_crossed(): x = x + lax.ppermute(x, (axis, side), pairs)]
    reduce_sum x6 -> x0, other arithmetic: 3.07 us -> none  [the longest x2 1.47 us: ridge_inverse(): return inverse(h + ridge * jnp.trace(h) / n * eye)]
    div x4 -> x0, other arithmetic: 2.77 us -> none  [the longest x1 0.84 us: per_device(): fac_a = raw_a / scale_a]
    pallas_call x3 -> x16, Pallas kernels: 34.6 us -> 37 us  [the longest x13 20.5 us: call(): pl.pallas_call(kernel, out_shape=shapes if many else shapes[0], in_specs=...]
  transfers between devices with their start and end apart: 25 -> 21, of which waited for: 11 -> 9; matrix products, arithmetic and copies ran while one was open for 11% -> 0% of each run, Pallas kernels for 30% -> 38%
where the time goes in v1:
time: 84.3 us; the launch traced here: 84.1 us
  Pallas kernels  37 us (44%)
  starting transfers between devices  26.7 us (32%)
  waiting for transfers between devices  18.9 us (22%)
  between operations  0.88 us (1%)
    ppermute x19, starting transfers between devices, swap(): return lax.ppermute(x, axis, [(i, i ^ bit) for i in range(n)])  23.3 us
    pallas_call x13, Pallas kernels, call(): pl.pallas_call(kernel, out_shape=shapes if many else shapes[0], in_specs=...  20.5 us
    pallas_call x2, Pallas kernels, inverse_and_unit(): pl.pallas_call(kernel, out_shape=[pltpu.VMEM(state.shape, jnp.float32), j...  14.9 us
    ppermute x2, waiting for transfers between devices, total_crossed(): x = x + lax.ppermute(x, (axis, side), pairs)  9.46 us
    ppermute x19, waiting for transfers between devices, swap(): return lax.ppermute(x, axis, [(i, i ^ bit) for i in range(n)])  9.42 us
    ppermute x2, starting transfers between devices, total_crossed(): x = x + lax.ppermute(x, (axis, side), pairs)  3.42 us
  transfers between devices with their start and end apart: 21, of which 9 were waited for; matrix products, arithmetic and copies ran while one was open for 0% of the time, Pallas kernels for 38%

profile of v1, /device:TPU:0, one launch (start us, length us, event | category | flops | bytes accessed | tf_op | source)
XLA Modules:
  0.0 84.1 jit_solution(9474721703052604918)
XLA Ops:
  0.6 1.6 %open.1 = (f32[264,256]{1,0:T(8,128)S(1)}, f32[1,512]{1,0:T(1,128)S(1)}, f32[512,128]{1,0:T(8,128)S(1)}, f32[128,256]{1,0:T(8,128)S(1)}, f32[1,256]{1,0:T(1,128)S(1)}) custom-call(s32[1]{0:T(128)S(6)} %sub.3.pick_ref, f32[512,128]{1,0:T(8,128)} %bitcast.5, f32[128,256]{1,0:T(8,128)} %b_ref.1, f32[1,256]{1,0:T(1,128)} %w_ref.1), custom_call_target="tpu_custom_call" | custom-call | tf_op jit(solution)/shard_map/open/pallas_call | solution.py:322
  2.2 0.6 collective-permute-start
  2.8 0.7 shard_map.58
  3.5 0.1 collective-permute-start.10
  3.6 0.4 collective-permute-done.got_ref
  4.0 3.0 %collective-permute-start.1 = (f32[72,256]{1,0:T(8,128)S(1)}, f32[72,256]{1,0:T(8,128)S(1)}, u32[]{:S(2)}, u32[]{:S(2)}) collective-permute-start(f32[72,256]{1,0:T(8,128)S(1)} %get-tuple-element.52), channel_id=1, source_target_pairs={{0,1},{1,0},{2,3},{3,2},{4,5},{5,4},{6,7},{7,6},{8,9},{9,8},{10,11... | collective-permute-start | bytes 221192 | tf_op jit(solution)/shard_map/ppermute | solution.py:148
  7.0 2.6 %collective-permute-start.2 = (f32[72,256]{1,0:T(8,128)S(1)}, f32[72,256]{1,0:T(8,128)S(1)}, u32[]{:S(2)}, u32[]{:S(2)}) collective-permute-start(f32[72,256]{1,0:T(8,128)S(1)} %get-tuple-element.53), channel_id=1, source_target_pairs={{0,2},{1,3},{2,0},{3,1},{4,6},{5,7},{6,4},{7,5},{8,10},{9,11},{10,... | collective-permute-start | bytes 221192 | tf_op jit(solution)/shard_map/ppermute | solution.py:148
  9.6 0.0 collective-permute-start.3
  9.6 1.7 %collective-permute-start.4 = (f32[8,256]{1,0:T(8,128)S(1)}, f32[8,256]{1,0:T(8,128)S(1)}, u32[]{:S(2)}, u32[]{:S(2)}) collective-permute-start(f32[8,256]{1,0:T(8,128)S(1)} %get-tuple-element.55), channel_id=1, source_target_pairs={{0,8},{8,0},{16,24},{24,16},{1,9},{9,1},{17,25},{25,17},{2,10},{10... | collective-permute-start | bytes 24584 | tf_op jit(solution)/shard_map/ppermute | solution.py:148
  11.3 1.9 %collective-permute-done.4 = f32[8,256]{1,0:T(8,128)S(1)} collective-permute-done((f32[8,256]{1,0:T(8,128)S(1)}, f32[8,256]{1,0:T(8,128)S(1)}, u32[]{:S(2)}, u32[]{:S(2)}) %collective-permute-start.4) | collective-permute-done | bytes 8224 | tf_op jit(solution)/shard_map/ppermute | solution.py:148
  13.3 1.7 %collective-permute-start.5 = (f32[8,256]{1,0:T(8,128)S(1)}, f32[8,256]{1,0:T(8,128)S(1)}, u32[]{:S(2)}, u32[]{:S(2)}) collective-permute-start(f32[8,256]{1,0:T(8,128)S(1)} %add.21), channel_id=1, source_target_pairs={{0,16},{8,24},{16,0},{24,8},{1,17},{9,25},{17,1},{25,9},{2,18},{10... | collective-permute-start | bytes 24584 | tf_op jit(solution)/shard_map/ppermute | solution.py:148
  15.0 1.9 %collective-permute-done.5 = f32[8,256]{1,0:T(8,128)S(1)} collective-permute-done((f32[8,256]{1,0:T(8,128)S(1)}, f32[8,256]{1,0:T(8,128)S(1)}, u32[]{:S(2)}, u32[]{:S(2)}) %collective-permute-start.5) | collective-permute-done | bytes 8224 | tf_op jit(solution)/shard_map/ppermute | solution.py:148
  16.9 0.0 collective-permute-start.6
  16.9 1.2 %collective-permute-done.6 = f32[8,256]{1,0:T(8,128)S(1)} collective-permute-done((f32[8,256]{1,0:T(8,128)S(1)}, f32[8,256]{1,0:T(8,128)S(1)}, u32[]{:S(2)}, u32[]{:S(2)}) %collective-permute-start.6) | collective-permute-done | bytes 8224 | tf_op jit(solution)/shard_map/ppermute | solution.py:148
  18.1 0.0 collective-permute-done.1.refs_1_
  18.1 0.0 collective-permute-done.2.refs_2_
  18.1 0.0 collective-permute-done.3.refs_3_
  18.1 3.9 %collective-permute-start.9 = (f32[72,256]{1,0:T(8,128)S(1)}, f32[72,256]{1,0:T(8,128)S(1)}, u32[]{:S(2)}, u32[]{:S(2)}) collective-permute-start(f32[72,256]{1,0:T(8,128)S(1)} %get-tuple-element.60.refs_0_), channel_id=1, source_target_pairs={{0,3},{1,2},{2,1},{3,0},{4,7},{5,6},{6,5},{7,4},{8,11},{9,10},{10,... | collective-permute-start | bytes 221192 | tf_op jit(solution)/shard_map/ppermute | solution.py:148
  22.0 0.0 collective-permute-start.8
  22.0 0.6 collective-permute-start.7
  22.7 0.0 collective-permute-done.10.other_ref
  22.7 0.5 shard_map.61
  23.2 4.9 %shard_map.62.v_ref = f32[256,256]{1,0:T(8,128)S(1)} custom-call(f32[256,256]{1,0:T(8,128)S(1)} %get-tuple-element.59.v_ref), custom_call_target="tpu_custom_call" | custom-call | tf_op jit(solution)/shard_map/pallas_call | solution.py:82
  28.2 0.0 collective-permute-done.9.refs_3_
  28.2 0.0 collective-permute-done.8.refs_2_
  28.2 0.0 collective-permute-done.7.refs_1_
  28.2 0.1 collective-permute-start.11
  28.3 4.9 %shard_map.64.inv_ref = f32[256,256]{1,0:T(8,128)S(1)} custom-call(f32[256,256]{1,0:T(8,128)S(1)} %shard_map.62.v_ref), custom_call_target="tpu_custom_call" | custom-call | tf_op jit(solution)/shard_map/pallas_call | solution.py:82
  33.3 0.0 collective-permute-done.11.other_ref
  33.3 2.7 %shard_map.65 = (f32[512,256]{1,0:T(8,128)S(1)}, f32[256,256]{1,0:T(8,128)S(1)}) custom-call(s32[1]{0:T(128)} %bitcast.me_ref, s32[1]{0:T(128)} %bitcast.1.pick_ref.top_ref, f32[256,256]{1,0:T(8,128)S(1)} %get-tuple-element.64.own_ref, f32[256,256]{1,0:T(8,128)S(1)} %collective-permute-done.11.other_ref, f32[8,512]{1,0:T(8,128)S(1)} %get-tuple-element.65.row_all_ref, ...), custom_call_target="tpu_custom_call" | custom-call | tf_op jit(solution)/shard_map/pallas_call | solution.py:82
  36.0 1.7 %collective-permute-start.12 = (f32[256,256]{1,0:T(8,128)S(1)}, f32[256,256]{1,0:T(8,128)S(1)}, u32[]{:S(2)}, u32[]{:S(2)}) collective-permute-start(f32[256,256]{1,0:T(8,128)S(1)} %get-tuple-element.69), channel_id=1, source_target_pairs={{0,8},{4,20},{8,0},{12,28},{16,24},{20,4},{24,16},{28,12},{1,9},{5... | collective-permute-start | bytes 786440 | tf_op jit(solution)/shard_map/ppermute | solution.py:167
  37.6 4.7 %collective-permute-done.12 = f32[256,256]{1,0:T(8,128)S(1)} collective-permute-done((f32[256,256]{1,0:T(8,128)S(1)}, f32[256,256]{1,0:T(8,128)S(1)}, u32[]{:S(2)}, u32[]{:S(2)}) %collective-permute-start.12) | collective-permute-done | bytes 262176 | tf_op jit(solution)/shard_map/ppermute | solution.py:167
  42.4 1.7 %collective-permute-start.13 = (f32[256,256]{1,0:T(8,128)S(1)}, f32[256,256]{1,0:T(8,128)S(1)}, u32[]{:S(2)}, u32[]{:S(2)}) collective-permute-start(f32[256,256]{1,0:T(8,128)S(1)} %add.24), channel_id=1, source_target_pairs={{0,16},{4,12},{8,24},{12,4},{16,0},{20,28},{24,8},{28,20},{1,17},{... | collective-permute-start | bytes 786440 | tf_op jit(solution)/shard_map/ppermute | solution.py:167
  44.1 4.7 %collective-permute-done.13 = f32[256,256]{1,0:T(8,128)S(1)} collective-permute-done((f32[256,256]{1,0:T(8,128)S(1)}, f32[256,256]{1,0:T(8,128)S(1)}, u32[]{:S(2)}, u32[]{:S(2)}) %collective-permute-start.13) | collective-permute-done | bytes 262176 | tf_op jit(solution)/shard_map/ppermute | solution.py:167
  48.9 0.1 collective-permute-start.15
  49.0 1.3 %collective-permute-done.15 = f32[128,256]{1,0:T(8,128)S(1)} collective-permute-done((f32[128,256]{1,0:T(8,128)S(1)}, f32[128,256]{1,0:T(8,128)S(1)}, u32[]{:S(2)}, u32[]{:S(2)}) %collective-permute-start.15) | collective-permute-done | bytes 131104 | tf_op jit(solution)/shard_map/ppermute | solution.py:148
  50.4 1.4 %collective-permute-start.14 = (f32[128,256]{1,0:T(8,128)S(1)}, f32[128,256]{1,0:T(8,128)S(1)}, u32[]{:S(2)}, u32[]{:S(2)}) collective-permute-start(f32[128,256]{1,0:T(8,128)S(1)} %get-tuple-element.90), channel_id=1, source_target_pairs={{0,1},{1,0},{2,3},{3,2},{4,5},{5,4},{6,7},{7,6},{8,9},{9,8},{10,11... | collective-permute-start | bytes 393224 | tf_op jit(solution)/shard_map/ppermute | solution.py:148
  51.8 2.7 %shard_map.66 = (f32[256,256]{1,0:T(8,128)S(1)}, f32[256,256]{1,0:T(8,128)S(1)}, f32[1,256]{1,0:T(1,128)S(1)}) custom-call(f32[256,256]{1,0:T(8,128)S(1)} %pad_maximum_fusion.refs_0_, f32[256,256]{1,0:T(8,128)S(1)} %get-tuple-element.70.refs_1_), custom_call_target="tpu_custom_call" | custom-call | tf_op jit(solution)/shard_map/pallas_call | solution.py:82
  54.6 2.5 %shard_map.67.v_ref = f32[256,256]{1,0:T(8,128)S(1)} custom-call(f32[256,256]{1,0:T(8,128)S(1)} %get-tuple-element.71.v_ref), custom_call_target="tpu_custom_call" | custom-call | tf_op jit(solution)/shard_map/pallas_call | solution.py:82
  57.1 0.0 collective-permute-done.14
  57.1 3.0 %collective-permute-start.16 = (f32[128,256]{1,0:T(8,128)S(1)}, f32[128,256]{1,0:T(8,128)S(1)}, u32[]{:S(2)}, u32[]{:S(2)}) collective-permute-start(f32[128,256]{1,0:T(8,128)S(1)} %add.26.own_ref), channel_id=1, source_target_pairs={{0,2},{1,3},{2,0},{3,1},{4,6},{5,7},{6,4},{7,5},{8,10},{9,11},{10,... | collective-permute-start | bytes 393224 | tf_op jit(solution)/shard_map/ppermute | solution.py:148
  60.1 5.0 %inverse_unit.2 = (f32[256,256]{1,0:T(8,128)S(1)}, f32[512,256]{1,0:T(8,128)}) custom-call(f32[256,256]{1,0:T(8,128)S(1)} %shard_map.67.v_ref, f32[512,256]{1,0:T(8,128)S(1)} %get-tuple-element.75.raw_ref, f32[1,256]{1,0:T(1,128)S(1)} %get-tuple-element.76.scale_ref.refs_4_), custom_call_target="tpu_custom_call" | custom-call | tf_op jit(solution)/shard_map/inverse_unit/pallas_call | solution.py:109
  65.1 1.1 %collective-permute-done.16.other_ref = f32[128,256]{1,0:T(8,128)S(1)} collective-permute-done((f32[128,256]{1,0:T(8,128)S(1)}, f32[128,256]{1,0:T(8,128)S(1)}, u32[]{:S(2)}, u32[]{:S(2)}) %collective-permute-start.16) | collective-permute-done | bytes 131104 | tf_op jit(solution)/shard_map/ppermute | solution.py:148
  66.2 0.9 %shard_map.68 = (f32[128,256]{1,0:T(8,128)S(1)}, f32[264,256]{1,0:T(8,128)S(1)}) custom-call(f32[128,256]{1,0:T(8,128)S(1)} %add.26.own_ref, f32[128,256]{1,0:T(8,128)S(1)} %collective-permute-done.16.other_ref, f32[1,256]{1,0:T(1,128)S(1)} %get-tuple-element.76.scale_ref.refs_4_, f32[256,256]{1,0:T(8,128)S(1)} %get-tuple-element.78.inv_ref, ...), custom_call_target="tpu_custom_call" | custom-call | tf_op jit(solution)/shard_map/pallas_call | solution.py:82
  67.1 0.1 collective-permute-start.17
  67.2 1.5 %collective-permute-done.17.refs_1_ = f32[264,256]{1,0:T(8,128)S(1)} collective-permute-done((f32[264,256]{1,0:T(8,128)S(1)}, f32[264,256]{1,0:T(8,128)S(1)}, u32[]{:S(2)}, u32[]{:S(2)}) %collective-permute-start.17) | collective-permute-done | bytes 270368 | tf_op jit(solution)/shard_map/ppermute | solution.py:148
  68.7 2.6 %collective-permute-start.20 = (f32[1,256]{1,0:T(1,128)S(1)}, f32[1,256]{1,0:T(1,128)S(1)}, u32[]{:S(2)}, u32[]{:S(2)}) collective-permute-start(f32[1,256]{1,0:T(1,128)S(1)} %slice_add_fusion.refs_0_), channel_id=1, source_target_pairs={{0,3},{1,2},{2,1},{3,0},{4,7},{5,6},{6,5},{7,4},{8,11},{9,10},{10,... | collective-permute-start | bytes 3080 | tf_op jit(solution)/shard_map/ppermute | solution.py:148
  71.3 0.0 collective-permute-start.19
  71.3 1.8 %collective-permute-start.18 = (f32[1,256]{1,0:T(1,128)S(1)}, f32[1,256]{1,0:T(1,128)S(1)}, u32[]{:S(2)}, u32[]{:S(2)}) collective-permute-start(f32[1,256]{1,0:T(1,128)S(1)} %slice_add_fusion.refs_0_), channel_id=1, source_target_pairs={{0,1},{1,0},{2,3},{3,2},{4,5},{5,4},{6,7},{7,6},{8,9},{9,8},{10,11... | collective-permute-start | bytes 3080 | tf_op jit(solution)/shard_map/ppermute | solution.py:148
  73.1 0.3 shard_map.69
  73.4 9.9 %inverse_unit.3 = (f32[256,256]{1,0:T(8,128)S(1)}, f32[128,256]{1,0:T(8,128)}) custom-call(f32[256,256]{1,0:T(8,128)S(1)} %get-tuple-element.82.v_ref, f32[128,256]{1,0:T(8,128)S(1)} %get-tuple-element.83.raw_ref, f32[1,256]{1,0:T(1,128)S(1)} %get-tuple-element.84.scale_ref.refs_5_), custom_call_target="tpu_custom_call" | custom-call | tf_op jit(solution)/shard_map/inverse_unit/pallas_call | solution.py:109
  83.3 0.0 collective-permute-done.20.refs_3_
  83.3 0.0 collective-permute-done.19.refs_2_
  83.3 0.0 collective-permute-done.18.refs_1_
  83.3 0.2 shard_map.70
  83.6 0.6 copy.6
  (13 shorter events, 0.3 us)
Async XLA Ops:
  2.2 1.7 %collective-permute-start = (f32[264,256]{1,0:T(8,128)S(1)}, f32[264,256]{1,0:T(8,128)S(1)}, u32[]{:S(2)}, u32[]{:S(2)}) collective-permute-start(f32[264,256]{1,0:T(8,128)S(1)} %get-tuple-element.49), channel_id=1, source_target_pairs={{0,4},{4,0},{1,5},{5,1},{2,6},{6,2},{3,7},{7,3},{8,12},{12,8},{9,1... | collective-permute-start | bytes 811016 | tf_op jit(solution)/shard_map/ppermute | solution.py:148
  3.5 19.2 %collective-permute-start.10 = (f32[256,256]{1,0:T(8,128)S(1)}, f32[256,256]{1,0:T(8,128)S(1)}, u32[]{:S(2)}, u32[]{:S(2)}) collective-permute-start(f32[256,256]{1,0:T(8,128)S(1)} %get-tuple-element.58.own_ref), channel_id=1, source_target_pairs={{0,4},{4,0},{1,5},{5,1},{2,6},{6,2},{3,7},{7,3},{8,12},{12,8},{9,1... | collective-permute-start | bytes 786440 | tf_op jit(solution)/shard_map/ppermute | solution.py:148
  4.0 14.1 %collective-permute-start.1 = (f32[72,256]{1,0:T(8,128)S(1)}, f32[72,256]{1,0:T(8,128)S(1)}, u32[]{:S(2)}, u32[]{:S(2)}) collective-permute-start(f32[72,256]{1,0:T(8,128)S(1)} %get-tuple-element.52), channel_id=1, source_target_pairs={{0,1},{1,0},{2,3},{3,2},{4,5},{5,4},{6,7},{7,6},{8,9},{9,8},{10,11... | collective-permute-start | bytes 221192 | tf_op jit(solution)/shard_map/ppermute | solution.py:148
  7.0 11.1 %collective-permute-start.2 = (f32[72,256]{1,0:T(8,128)S(1)}, f32[72,256]{1,0:T(8,128)S(1)}, u32[]{:S(2)}, u32[]{:S(2)}) collective-permute-start(f32[72,256]{1,0:T(8,128)S(1)} %get-tuple-element.53), channel_id=1, source_target_pairs={{0,2},{1,3},{2,0},{3,1},{4,6},{5,7},{6,4},{7,5},{8,10},{9,11},{10,... | collective-permute-start | bytes 221192 | tf_op jit(solution)/shard_map/ppermute | solution.py:148
  9.6 8.5 %collective-permute-start.3 = (f32[72,256]{1,0:T(8,128)S(1)}, f32[72,256]{1,0:T(8,128)S(1)}, u32[]{:S(2)}, u32[]{:S(2)}) collective-permute-start(f32[72,256]{1,0:T(8,128)S(1)} %get-tuple-element.54), channel_id=1, source_target_pairs={{0,3},{1,2},{2,1},{3,0},{4,7},{5,6},{6,5},{7,4},{8,11},{9,10},{10,... | collective-permute-start | bytes 221192 | tf_op jit(solution)/shard_map/ppermute | solution.py:148
  9.6 3.7 %collective-permute-start.4 = (f32[8,256]{1,0:T(8,128)S(1)}, f32[8,256]{1,0:T(8,128)S(1)}, u32[]{:S(2)}, u32[]{:S(2)}) collective-permute-start(f32[8,256]{1,0:T(8,128)S(1)} %get-tuple-element.55), channel_id=1, source_target_pairs={{0,8},{8,0},{16,24},{24,16},{1,9},{9,1},{17,25},{25,17},{2,10},{10... | collective-permute-start | bytes 24584 | tf_op jit(solution)/shard_map/ppermute | solution.py:148
  13.3 3.7 %collective-permute-start.5 = (f32[8,256]{1,0:T(8,128)S(1)}, f32[8,256]{1,0:T(8,128)S(1)}, u32[]{:S(2)}, u32[]{:S(2)}) collective-permute-start(f32[8,256]{1,0:T(8,128)S(1)} %add.21), channel_id=1, source_target_pairs={{0,16},{8,24},{16,0},{24,8},{1,17},{9,25},{17,1},{25,9},{2,18},{10... | collective-permute-start | bytes 24584 | tf_op jit(solution)/shard_map/ppermute | solution.py:148
  16.9 1.2 %collective-permute-start.6 = (f32[8,256]{1,0:T(8,128)S(1)}, f32[8,256]{1,0:T(8,128)S(1)}, u32[]{:S(2)}, u32[]{:S(2)}) collective-permute-start(f32[8,256]{1,0:T(8,128)S(1)} %add.22.refs_5_), channel_id=1, source_target_pairs={{0,4},{4,0},{1,5},{5,1},{2,6},{6,2},{3,7},{7,3},{8,12},{12,8},{9,1... | collective-permute-start | bytes 24584 | tf_op jit(solution)/shard_map/ppermute | solution.py:148
  18.1 10.0 %collective-permute-start.9 = (f32[72,256]{1,0:T(8,128)S(1)}, f32[72,256]{1,0:T(8,128)S(1)}, u32[]{:S(2)}, u32[]{:S(2)}) collective-permute-start(f32[72,256]{1,0:T(8,128)S(1)} %get-tuple-element.60.refs_0_), channel_id=1, source_target_pairs={{0,3},{1,2},{2,1},{3,0},{4,7},{5,6},{6,5},{7,4},{8,11},{9,10},{10,... | collective-permute-start | bytes 221192 | tf_op jit(solution)/shard_map/ppermute | solution.py:148
  22.0 6.2 %collective-permute-start.8 = (f32[72,256]{1,0:T(8,128)S(1)}, f32[72,256]{1,0:T(8,128)S(1)}, u32[]{:S(2)}, u32[]{:S(2)}) collective-permute-start(f32[72,256]{1,0:T(8,128)S(1)} %get-tuple-element.60.refs_0_), channel_id=1, source_target_pairs={{0,2},{1,3},{2,0},{3,1},{4,6},{5,7},{6,4},{7,5},{8,10},{9,11},{10,... | collective-permute-start | bytes 221192 | tf_op jit(solution)/shard_map/ppermute | solution.py:148
  22.0 6.2 %collective-permute-start.7 = (f32[72,256]{1,0:T(8,128)S(1)}, f32[72,256]{1,0:T(8,128)S(1)}, u32[]{:S(2)}, u32[]{:S(2)}) collective-permute-start(f32[72,256]{1,0:T(8,128)S(1)} %get-tuple-element.60.refs_0_), channel_id=1, source_target_pairs={{0,1},{1,0},{2,3},{3,2},{4,5},{5,4},{6,7},{7,6},{8,9},{9,8},{10,11... | collective-permute-start | bytes 221192 | tf_op jit(solution)/shard_map/ppermute | solution.py:148
  28.2 5.0 %collective-permute-start.11 = (f32[256,256]{1,0:T(8,128)S(1)}, f32[256,256]{1,0:T(8,128)S(1)}, u32[]{:S(2)}, u32[]{:S(2)}) collective-permute-start(f32[256,256]{1,0:T(8,128)S(1)} %get-tuple-element.64.own_ref), channel_id=1, source_target_pairs={{0,4},{4,0},{1,5},{5,1},{2,6},{6,2},{3,7},{7,3},{8,12},{12,8},{9,1... | collective-permute-start | bytes 786440 | tf_op jit(solution)/shard_map/ppermute | solution.py:148
  36.0 6.4 %collective-permute-start.12 = (f32[256,256]{1,0:T(8,128)S(1)}, f32[256,256]{1,0:T(8,128)S(1)}, u32[]{:S(2)}, u32[]{:S(2)}) collective-permute-start(f32[256,256]{1,0:T(8,128)S(1)} %get-tuple-element.69), channel_id=1, source_target_pairs={{0,8},{4,20},{8,0},{12,28},{16,24},{20,4},{24,16},{28,12},{1,9},{5... | collective-permute-start | bytes 786440 | tf_op jit(solution)/shard_map/ppermute | solution.py:167
  42.4 6.4 %collective-permute-start.13 = (f32[256,256]{1,0:T(8,128)S(1)}, f32[256,256]{1,0:T(8,128)S(1)}, u32[]{:S(2)}, u32[]{:S(2)}) collective-permute-start(f32[256,256]{1,0:T(8,128)S(1)} %add.24), channel_id=1, source_target_pairs={{0,16},{4,12},{8,24},{12,4},{16,0},{20,28},{24,8},{28,20},{1,17},{... | collective-permute-start | bytes 786440 | tf_op jit(solution)/shard_map/ppermute | solution.py:167
  48.9 1.4 %collective-permute-start.15 = (f32[128,256]{1,0:T(8,128)S(1)}, f32[128,256]{1,0:T(8,128)S(1)}, u32[]{:S(2)}, u32[]{:S(2)}) collective-permute-start(f32[128,256]{1,0:T(8,128)S(1)} %slice.17), channel_id=1, source_target_pairs={{0,4},{4,0},{1,5},{5,1},{2,6},{6,2},{3,7},{7,3},{8,12},{12,8},{9,1... | collective-permute-start | bytes 393224 | tf_op jit(solution)/shard_map/ppermute | solution.py:148
  50.4 6.7 %collective-permute-start.14 = (f32[128,256]{1,0:T(8,128)S(1)}, f32[128,256]{1,0:T(8,128)S(1)}, u32[]{:S(2)}, u32[]{:S(2)}) collective-permute-start(f32[128,256]{1,0:T(8,128)S(1)} %get-tuple-element.90), channel_id=1, source_target_pairs={{0,1},{1,0},{2,3},{3,2},{4,5},{5,4},{6,7},{7,6},{8,9},{9,8},{10,11... | collective-permute-start | bytes 393224 | tf_op jit(solution)/shard_map/ppermute | solution.py:148
  57.1 9.1 %collective-permute-start.16 = (f32[128,256]{1,0:T(8,128)S(1)}, f32[128,256]{1,0:T(8,128)S(1)}, u32[]{:S(2)}, u32[]{:S(2)}) collective-permute-start(f32[128,256]{1,0:T(8,128)S(1)} %add.26.own_ref), channel_id=1, source_target_pairs={{0,2},{1,3},{2,0},{3,1},{4,6},{5,7},{6,4},{7,5},{8,10},{9,11},{10,... | collective-permute-start | bytes 393224 | tf_op jit(solution)/shard_map/ppermute | solution.py:148
  67.1 1.6 %collective-permute-start.17 = (f32[264,256]{1,0:T(8,128)S(1)}, f32[264,256]{1,0:T(8,128)S(1)}, u32[]{:S(2)}, u32[]{:S(2)}) collective-permute-start(f32[264,256]{1,0:T(8,128)S(1)} %get-tuple-element.79.refs_0_), channel_id=1, source_target_pairs={{0,4},{4,0},{1,5},{5,1},{2,6},{6,2},{3,7},{7,3},{8,12},{12,8},{9,1... | collective-permute-start | bytes 811016 | tf_op jit(solution)/shard_map/ppermute | solution.py:148
  68.7 14.6 %collective-permute-start.20 = (f32[1,256]{1,0:T(1,128)S(1)}, f32[1,256]{1,0:T(1,128)S(1)}, u32[]{:S(2)}, u32[]{:S(2)}) collective-permute-start(f32[1,256]{1,0:T(1,128)S(1)} %slice_add_fusion.refs_0_), channel_id=1, source_target_pairs={{0,3},{1,2},{2,1},{3,0},{4,7},{5,6},{6,5},{7,4},{8,11},{9,10},{10,... | collective-permute-start | bytes 3080 | tf_op jit(solution)/shard_map/ppermute | solution.py:148
  71.3 12.0 %collective-permute-start.19 = (f32[1,256]{1,0:T(1,128)S(1)}, f32[1,256]{1,0:T(1,128)S(1)}, u32[]{:S(2)}, u32[]{:S(2)}) collective-permute-start(f32[1,256]{1,0:T(1,128)S(1)} %slice_add_fusion.refs_0_), channel_id=1, source_target_pairs={{0,2},{1,3},{2,0},{3,1},{4,6},{5,7},{6,4},{7,5},{8,10},{9,11},{10,... | collective-permute-start | bytes 3080 | tf_op jit(solution)/shard_map/ppermute | solution.py:148
  71.3 12.0 %collective-permute-start.18 = (f32[1,256]{1,0:T(1,128)S(1)}, f32[1,256]{1,0:T(1,128)S(1)}, u32[]{:S(2)}, u32[]{:S(2)}) collective-permute-start(f32[1,256]{1,0:T(1,128)S(1)} %slice_add_fusion.refs_0_), channel_id=1, source_target_pairs={{0,1},{1,0},{2,3},{3,2},{4,5},{5,4},{6,7},{7,6},{8,9},{9,8},{10,11... | collective-permute-start | bytes 3080 | tf_op jit(solution)/shard_map/ppermute | solution.py:148

commit v2 on v1

--- a/solution.py
+++ b/solution.py
@@ -16,57 +16,131 @@
     return jnp.dot(a, b, precision=hp, preferred_element_type=jnp.float32)
 
 
-def pivot_panel(panel):
-    groups, tiles = len(panel), len(panel[0])
+def spread(x, axis, i):
+    return jnp.broadcast_to(x[:, i : i + 1] if axis else x[i : i + 1, :], x.shape)
+
+
+def pivot_group(rows, tile, at):
     lane = lax.broadcasted_iota(jnp.int32, (8, 128), 1)
     sub = lax.broadcasted_iota(jnp.int32, (8, 128), 0)
-    part = [list(r) for r in panel]
-    for g in range(groups):
-        cols = [
-            [jnp.broadcast_to(part[h][0][:, 8 * g + q : 8 * g + q + 1], (8, 128)) for h in range(groups)]
-            for q in range(8)
-        ]
-        for q in range(8):
-            col = cols[q]
-            inv = 1.0 / jnp.broadcast_to(col[g][q : q + 1, :], (8, 128))
-            here = lane == 8 * g + q
-            this = sub == q
-            rows = []
-            for t in range(tiles):
-                row = jnp.broadcast_to(part[g][t][q : q + 1, :], (8, 128))
-                if t == 0:
-                    row = jnp.where(here, 1.0, row)
-                rows.append(row * inv)
-            for h in range(groups):
-                for t in range(tiles):
-                    base = jnp.where(here, 0.0, part[h][t]) if t == 0 else part[h][t]
-                    new = base - col[h] * rows[t]
-                    part[h][t] = jnp.where(this, rows[t], new) if h == g else new
-            for q2 in range(q + 1, 8):
-                factor = jnp.broadcast_to(cols[q2][g][q : q + 1, :], (8, 128)) * inv
-                for h in range(groups):
-                    new = cols[q2][h] - col[h] * factor
-                    cols[q2][h] = jnp.where(this, factor, new) if h == g else new
-    return jnp.concatenate([jnp.concatenate(r, axis=1) for r in part], axis=0)
-
-
-def eliminate(a_ref, count):
-    n = a_ref.shape[0]
-
-    def step(_, carry):
-        panel = [
-            [a_ref[8 * g : 8 * g + 8, 128 * t : 128 * t + 128] for t in range(n // 128)]
-            for g in range(block // 8)
-        ]
-        top = pivot_panel(panel)
-        rest = a_ref[block:, :]
-        lane = lax.broadcasted_iota(jnp.int32, rest.shape, 1)
-        new = jnp.where(lane < block, 0.0, rest) - dot(rest[:, :block], top)
-        a_ref[: n - block, :] = pltpu.roll(new, n - block, 1)
-        a_ref[n - block :, :] = pltpu.roll(top, n - block, 1)
+    part = list(rows)
+    own = [spread(part[tile], 1, at + q) for q in range(8)]
+    raw = list(own)
+    for q in range(0, 8, 2):
+        c0, c1 = own[q], own[q + 1]
+        a, b = spread(raw[q], 0, q), spread(raw[q + 1], 0, q)
+        c, d = spread(raw[q], 0, q + 1), spread(raw[q + 1], 0, q + 1)
+        inv = 1.0 / (a * d - b * c)
+        t0, t1 = sub == q, sub == q + 1
+
+        def solve(x, y, a=a, b=b, c=c, d=d, inv=inv):
+            return (d * x - b * y) * inv, (a * y - c * x) * inv
+
+        for q2 in range(q + 2, 8):
+            f0, f1 = solve(spread(raw[q2], 0, q), spread(raw[q2], 0, q + 1))
+            raw[q2] = (own[q2] - c0 * f0) - c1 * f1
+            own[q2] = jnp.where(t0, f0, jnp.where(t1, f1, raw[q2]))
+        h0, h1 = lane == at + q, lane == at + q + 1
+        for t in range(len(part)):
+            x, y, base = spread(part[t], 0, q), spread(part[t], 0, q + 1), part[t]
+            if t == tile:
+                x = jnp.where(h0, 1.0, jnp.where(h1, 0.0, x))
+                y = jnp.where(h1, 1.0, jnp.where(h0, 0.0, y))
+                base = jnp.where(h0 | h1, 0.0, base)
+            f0, f1 = solve(x, y)
+            part[t] = jnp.where(t0, f0, jnp.where(t1, f1, (base - c0 * f0) - c1 * f1))
+    return part
+
+
+def apply_group(target, tile, at, rows):
+    lane = lax.broadcasted_iota(jnp.int32, (8, 128), 1)
+    inside = (lane >= at) & (lane < at + 8)
+    cols = [spread(target[tile], 1, at + q) for q in range(8)]
+    out = []
+    for t in range(len(target)):
+        base = jnp.where(inside, 0.0, target[t]) if t == tile else target[t]
+        e = [cols[q] * spread(rows[t], 0, q) for q in range(8)]
+        out.append(base - (((e[0] + e[1]) + (e[2] + e[3])) + ((e[4] + e[5]) + (e[6] + e[7]))))
+    return out
+
+
+def apply_block(rows, width, top):
+    lane = lax.broadcasted_iota(jnp.int32, rows.shape, 1)
+    return jnp.where(lane < width, 0.0, rows) - dot(rows[:, :width], top)
+
+
+def split(x):
+    return [[x[8 * i : 8 * i + 8, 128 * t : 128 * t + 128] for t in range(x.shape[1] // 128)] for i in range(x.shape[0] // 8)]
+
+
+def join(rows):
+    return jnp.concatenate([jnp.concatenate(r, axis=1) for r in rows], axis=0)
+
+
+def invert_square(s_ref, r_ref, t_ref):
+    n, per, early = s_ref.shape[0], block // 8, 2
+
+    def back(x):
+        return pltpu.roll(x, n - block, 1)
+
+    r_ref[...] = pltpu.roll(s_ref[block : n - block, :], block, 1)
+    t_ref[...] = pltpu.roll(s_ref[n - block :, :], block, 1)
+
+    def flush(live):
+        old, top = r_ref[...], t_ref[...]
+        out = lax.broadcasted_iota(jnp.int32, old.shape, 1) < jnp.where(live, block, 0)
+        u = dot(jnp.where(out, old, 0.0)[:, :block], top)
+        return back(jnp.where(out, 0.0, old) - u), back(top)
+
+    def step(p, panel):
+        rest, last = flush(p > 0)
+        part = split(panel)
+        for g in range(per):
+            if g == early:
+                ahead = split(apply_block(rest[:block], 8 * early, join(part[:early])))
+            part[g] = pivot_group(part[g], 0, 8 * g)
+            if g >= early:
+                ahead = [apply_group(r, 0, 8 * g, part[g]) for r in ahead]
+            for h in ([g + 1] if g + 1 < per else []) + [h for h in range(per) if h not in (g, g + 1)]:
+                part[h] = apply_group(part[h], 0, 8 * g, part[g])
+        r_ref[: n - 3 * block, :] = rest[block:]
+        r_ref[n - 3 * block :, :] = last
+        t_ref[...] = join(part)
+        return back(join(ahead))
+
+    panel = lax.fori_loop(0, n // block, step, s_ref[:block, :])
+    rest, last = flush(True)
+    s_ref[:block, :] = panel
+    s_ref[block : n - block, :] = rest
+    s_ref[n - block :, :] = last
+
+
+square = [pltpu.VMEM((128, 128), jnp.float32), pltpu.VMEM((128 - 2 * block, 128), jnp.float32), pltpu.VMEM((block, 128), jnp.float32)]
+
+
+def eliminate(a_ref, begin, end, *scratch):
+    count = a_ref.shape[0] // 128
+
+    def at(i):
+        return pl.ds(pl.multiple_of(128 * i, 128), 128)
+
+    def step(b, carry):
+        scratch[0][...] = a_ref[at(b), at(b)]
+        invert_square(*scratch)
+        d = scratch[0][...]
+        others = [lax.rem(b + i, count) for i in range(1, count)]
+        rows = [dot(d, a_ref[at(b), at(j)]) for j in others]
+        for i in others:
+            left = a_ref[at(i), at(b)]
+            for j, row in zip(others, rows):
+                a_ref[at(i), at(j)] = a_ref[at(i), at(j)] - dot(left, row)
+            a_ref[at(i), at(b)] = -dot(left, d)
+        for j, row in zip(others, rows):
+            a_ref[at(b), at(j)] = row
+        a_ref[at(b), at(b)] = d
         return carry
 
-    lax.fori_loop(0, count, step, 0)
+    lax.fori_loop(begin, end, step, 0)
 
 
 def near(x):
@@ -88,21 +162,21 @@
     )(*args[:smem], *[near(a) for a in args[smem:]])
 
 
-def inverse_piece(state, count):
-    def kernel(v_ref, o_ref):
+def inverse_piece(state, begin, end):
+    def kernel(v_ref, o_ref, *scratch):
         o_ref[...] = v_ref[...]
-        eliminate(o_ref, count)
-
-    return call(kernel, state.shape, state)
-
-
-def inverse_and_unit(state, count, raw, scale):
-    def kernel(v_ref, raw_ref, scale_ref, o_ref, unit_ref, buf, sem):
+        eliminate(o_ref, begin, end, *scratch)
+
+    return call(kernel, state.shape, state, scratch=square)
+
+
+def inverse_and_unit(state, begin, end, raw, scale):
+    def kernel(v_ref, raw_ref, scale_ref, o_ref, unit_ref, buf, sem, *scratch):
         buf[...] = raw_ref[...] / scale_ref[...]
         copy = pltpu.make_async_copy(buf, unit_ref, sem)
         copy.start()
         o_ref[...] = v_ref[...]
-        eliminate(o_ref, count)
+        eliminate(o_ref, begin, end, *scratch)
         copy.wait()
 
     vmem = pl.BlockSpec(memory_space=pltpu.VMEM)
@@ -111,7 +185,7 @@
         out_shape=[pltpu.VMEM(state.shape, jnp.float32), jax.ShapeDtypeStruct(raw.shape, jnp.float32)],
         in_specs=[vmem] * 3,
         out_specs=[vmem, pl.BlockSpec(memory_space=pl.ANY)],
-        scratch_shapes=[pltpu.VMEM(raw.shape, jnp.float32), pltpu.SemaphoreType.DMA(())],
+        scratch_shapes=[pltpu.VMEM(raw.shape, jnp.float32), pltpu.SemaphoreType.DMA(()), *square],
         name="inverse_unit",
     )(near(state), near(raw), near(scale))
 
@@ -159,13 +233,11 @@
     return x
 
 
-def total_crossed(x, axis, side):
+def crossed(x, axis, side, i):
     n, m = lax.axis_size(axis), lax.axis_size(side)
-    order = bits(axis)
-    for one, two in zip(order, reversed(order)):
-        pairs = [(i * m + j, (i ^ (two if j & 1 else one)) * m + j) for i in range(n) for j in range(m)]
-        x = x + lax.ppermute(x, (axis, side), pairs)
-    return x
+    one, two = bits(axis)[i], bits(axis)[-1 - i]
+    pairs = [(k * m + j, (k ^ (two if j & 1 else one)) * m + j) for k in range(n) for j in range(m)]
+    return lax.ppermute(x, (axis, side), pairs)
 
 
 def gather_rows(x, axis):
@@ -264,7 +336,7 @@
 
 
 def exporter_kernel(
-    me_ref, top_ref, own_ref, other_ref, row_all_ref, shift_ref, inv_ref, f_ref, col_ref, raw_ref, both_ref, m_ref, s_ref
+    me_ref, top_ref, own_ref, other_ref, row_all_ref, shift_ref, inv_ref, f_ref, col_ref, raw_ref, t_ref, m_ref, s_ref
 ):
     half = own_ref.shape[0]
     m_ref[pl.ds(pl.multiple_of(top_ref[0] * half, half), half), :] = own_ref[...]
@@ -276,18 +348,21 @@
     terms = outer(row_all_ref[...], s_ref[...])
     raw = dot(m_ref[...] - terms[:, :rank], inv_ref[...])
     raw_ref[...] = raw
-    grams = both_ref.shape[0] - cols
+    t_ref[...] = outer(f_ref[...] - terms[:, rank:], raw)
+
+
+def gram_kernel(top_ref, raw_ref, g_ref):
+    grams, rank = g_ref.shape
     at = pl.multiple_of(top_ref[0] * grams, grams) if grams < rank else 0
-    left = jnp.concatenate([raw_ref[:, pl.ds(at, grams)], f_ref[...] - terms[:, rank:]], axis=1)
-    both_ref[...] = outer(left, raw)
-
-
-def second_kernel(count, steps, g_ref, gram_c_ref, v_ref, gram_ref, scale_ref):
+    g_ref[...] = outer(raw_ref[:, pl.ds(at, grams)], raw_ref[...])
+
+
+def second_kernel(count, end, g_ref, gram_c_ref, v_ref, gram_ref, scale_ref, *scratch):
     scale, gram = normalised(g_ref[...], count)
     scale_ref[...] = scale
     gram_ref[...] = gram
     v_ref[...] = ridged(gram * gram_c_ref[...])
-    eliminate(v_ref, steps)
+    eliminate(v_ref, 0, end, *scratch)
 
 
 def importer_kernel(own_ref, other_ref, scale_ref, inv_ref, t_ref, raw_ref, both_ref):
@@ -354,7 +429,7 @@
     weeks, ni, ne = lax.axis_size("wk"), lax.axis_size("imp"), lax.axis_size("exp")
     me_k = lax.axis_index("wk").astype(jnp.int32)[None]
     top = jnp.where((lax.axis_index("imp") & (ni // 2)) != 0, 1, 0).astype(jnp.int32)[None]
-    steps = rank // block
+    steps = rank // 128
 
     f, w, keep, got, row, small, gram_own, gram_other = shares(f, importer_factor, w, top, ni)
     small = small + swap(small, "exp", 1)
@@ -374,47 +449,64 @@
         me_k, after(gram_own, give), gram_other, *got,
         smem=1, scratch=[pltpu.VMEM((-(-weeks // 8) * 8, rank), jnp.float32)],
     )
-    state = inverse_piece(state, steps // 2)
+    state = inverse_piece(state, 0, steps // 2)
     *gathered, state = lax.optimization_barrier((*gathered, state))
     m_rows, shifts = call(rows_kernel, [(chunk * weeks, rank), (-(-weeks // 8) * 8, rank)], me_k, *gathered, smem=1)
     m_other = swap(m_rows, "imp", ni // 2)
-    inv_a = inverse_piece(state, steps - steps // 2)
+    inv_a = inverse_piece(state, steps // 2, steps)
 
     grams = rank // 2 if ni == 2 and rank % 256 == 0 else rank
-    raw_a, both = call(
+    raw_a, t = call(
         exporter_kernel,
-        [(rows, rank), (grams + cols, rank)],
+        [(rows, rank), (cols, rank)],
         me_k, top, m_rows, m_other, row_all, shifts, inv_a, f, col_mean,
         smem=2, scratch=[pltpu.VMEM((rows, rank), jnp.float32), pltpu.VMEM((-(-weeks // 8) * 8, rank + cols), jnp.float32)],
     )
-    both = total_crossed(both, "exp", "imp")
-    t = both[grams:]
-    g_a = gather_rows(both[:grams], "imp") if grams < rank else both[:grams]
-
-    def second(*refs):
-        second_kernel(rows * ne, steps // 4, *refs)
-
+    g_a = call(gram_kernel, (grams, rank), top, after(raw_a, t), smem=1)
+    for i, bit in enumerate(bits("exp")):
+        t_got = crossed(t, "exp", "imp", i)
+        g_got = crossed(g_a, "exp", "imp", i)
+        t = t + t_got
+        g_a = g_a + g_got
     m_own = t * w
     m_got = swap(m_own, "wk", 1)
-    state, gram_a, scale_a = call(second, [(rank, rank), (rank, rank), (1, rank)], g_a, gram_c)
+    g_a = gather_rows(g_a, "imp") if grams < rank else g_a
+
+    def second(*refs):
+        second_kernel(rows * ne, steps // 2, *refs)
+
     for bit in bits("wk")[1:]:
-        state = inverse_piece(state, steps // 4)
-        m_got, state = lax.optimization_barrier((m_got, state))
+        m_got, g_a = lax.optimization_barrier((m_got, g_a))
         m_own = m_own + m_got
         m_got = swap(m_own, "wk", bit)
-    inv_b, fac_a = inverse_and_unit(after(state, m_own), steps - steps // 4 * len(bits("wk")), raw_a, scale_a)
+    state, gram_a, scale_a = call(
+        second, [(rank, rank), (rank, rank), (1, rank)], after(g_a, m_own), gram_c, scratch=square
+    )
+    inv_b, fac_a = inverse_and_unit(state, steps // 2, steps, raw_a, scale_a)
     raw_b, both = call(importer_kernel, [(cols, rank), (rank + 8, rank)], m_own, m_got, scale_a, inv_b, t)
     for bit in bits("imp")[:-1]:
         both = both + swap(both, "imp", bit)
     got = swap(both, "imp", ni // 2)
     m_mine = both[rank : rank + 1] + got[rank : rank + 1]
-    m_all = [m_mine] + [swap(m_mine, "wk", d) for d in range(1, weeks)]
+    paired = weeks == 4 and ni == 2
+    if paired:
+        pairs = [(j * 4 + k, j * 4 + (k ^ (1 + j))) for k in range(4) for j in range(2)]
+        near_row = lax.ppermute(m_mine, ("imp", "wk"), pairs)
+        far_row = swap(m_mine, "wk", 3)
+    else:
+        m_all = [m_mine] + [swap(m_mine, "wk", d) for d in range(1, weeks)]
 
     def third(*refs):
         third_kernel(cols * ni, *refs)
 
     state, scale_b = call(third, [(rank, rank), (1, rank)], both, got, after(gram_a, m_mine))
-    inv_c, fac_b = inverse_and_unit(state, steps, raw_b, scale_b)
+    state = inverse_piece(state, 0, steps // 2)
+    if paired:
+        near_row, state = lax.optimization_barrier((near_row, state))
+        side_row = swap(near_row, "imp", 1)
+        low = lax.axis_index("imp") == 0
+        m_all = [m_mine, jnp.where(low, near_row, side_row), jnp.where(low, side_row, near_row), far_row]
+    inv_c, fac_b = inverse_and_unit(state, steps // 2, steps, raw_b, scale_b)
     scratch = [pltpu.VMEM((-(-weeks // 8) * 8, rank), jnp.float32)]
     fac_c = call(week_kernel, (1, rank), *m_all, scale_a, scale_b, inv_c, scratch=scratch)
     return (fac_a, fac_b, fac_c)

time: 84.3 us -> 78.5 us (0.931)
  Pallas kernels: 37 us -> 32.2 us
  waiting for transfers between devices: 18.9 us -> 17.3 us
    pallas_call x2, Pallas kernels: 14.9 us -> 8.28 us  [inverse_and_unit(): pl.pallas_call(kernel, out_shape=[pltpu.VMEM(state.shape, jnp.float32), j...]
    ppermute x2 -> x5, starting transfers between devices: 3.42 us -> 7.27 us  [the longest x4 5.25 us: crossed(): return lax.ppermute(x, (axis, side), pairs)]
    ppermute x19 -> x18, starting transfers between devices: 23.3 us -> 20 us  [swap(): return lax.ppermute(x, axis, [(i, i ^ bit) for i in range(n)])]
    ppermute x2 -> x5, waiting for transfers between devices: 9.46 us -> 6.41 us  [the longest x4 6.41 us: crossed(): return lax.ppermute(x, (axis, side), pairs)]
    pallas_call x13 -> x14, Pallas kernels: 20.5 us -> 22.3 us  [call(): pl.pallas_call(kernel, out_shape=shapes if many else shapes[0], in_specs=...]
    ppermute x19 -> x18, waiting for transfers between devices: 9.42 us -> 10.9 us  [swap(): return lax.ppermute(x, axis, [(i, i ^ bit) for i in range(n)])]
  transfers between devices with their start and end apart: 21 -> 23, of which waited for: 9 -> 11; matrix products, arithmetic and copies ran while one was open for 0% -> 0% of each run, Pallas kernels for 38% -> 34%
where the time goes in v2:
time: 78.5 us; the launch traced here: 78.4 us
  Pallas kernels  32.2 us (41%)
  starting transfers between devices  27.3 us (35%)
  waiting for transfers between devices  17.3 us (22%)
  between operations  0.9 us (1%)
    pallas_call x14, Pallas kernels, call(): pl.pallas_call(kernel, out_shape=shapes if many else shapes[0], in_specs=...  22.3 us
    ppermute x18, starting transfers between devices, swap(): return lax.ppermute(x, axis, [(i, i ^ bit) for i in range(n)])  20 us
    ppermute x18, waiting for transfers between devices, swap(): return lax.ppermute(x, axis, [(i, i ^ bit) for i in range(n)])  10.9 us
    pallas_call x2, Pallas kernels, inverse_and_unit(): pl.pallas_call(kernel, out_shape=[pltpu.VMEM(state.shape, jnp.float32), j...  8.28 us
    ppermute x4, waiting for transfers between devices, crossed(): return lax.ppermute(x, (axis, side), pairs)  6.41 us
    ppermute x4, starting transfers between devices, crossed(): return lax.ppermute(x, (axis, side), pairs)  5.25 us
    ppermute x1, starting transfers between devices, per_device(): near_row = lax.ppermute(m_mine, ('imp', 'wk'), pairs)  2.02 us
    pallas_call x1, Pallas kernels, shares(): pl.pallas_call(open_kernel, out_shape=[pltpu.VMEM(s, jnp.float32) for s i...  1.58 us
  transfers between devices with their start and end apart: 23, of which 11 were waited for; matrix products, arithmetic and copies ran while one was open for 0% of the time, Pallas kernels for 34%

profile of v2, /device:TPU:0, one launch (start us, length us, event | category | flops | bytes accessed | tf_op | source)
XLA Modules:
  0.0 78.4 jit_solution(12123264654221184339)
XLA Ops:
  0.6 1.6 %open.1 = (f32[264,256]{1,0:T(8,128)S(1)}, f32[1,512]{1,0:T(1,128)S(1)}, f32[512,128]{1,0:T(8,128)S(1)}, f32[128,256]{1,0:T(8,128)S(1)}, f32[1,256]{1,0:T(1,128)S(1)}) custom-call(s32[1]{0:T(128)S(6)} %sub.3.pick_ref, f32[512,128]{1,0:T(8,128)} %bitcast.5, f32[128,256]{1,0:T(8,128)} %b_ref.1, f32[1,256]{1,0:T(1,128)} %w_ref.1), custom_call_target="tpu_custom_call" | custom-call | tf_op jit(solution)/shard_map/open/pallas_call | solution.py:397
  2.2 0.6 collective-permute-start
  2.8 0.7 shard_map.58
  3.5 0.1 collective-permute-start.10
  3.6 0.4 collective-permute-done.got_ref
  4.0 3.0 %collective-permute-start.1 = (f32[72,256]{1,0:T(8,128)S(1)}, f32[72,256]{1,0:T(8,128)S(1)}, u32[]{:S(2)}, u32[]{:S(2)}) collective-permute-start(f32[72,256]{1,0:T(8,128)S(1)} %get-tuple-element.55), channel_id=1, source_target_pairs={{0,1},{1,0},{2,3},{3,2},{4,5},{5,4},{6,7},{7,6},{8,9},{9,8},{10,11... | collective-permute-start | bytes 221192 | tf_op jit(solution)/shard_map/ppermute | solution.py:222
  7.0 2.6 %collective-permute-start.2 = (f32[72,256]{1,0:T(8,128)S(1)}, f32[72,256]{1,0:T(8,128)S(1)}, u32[]{:S(2)}, u32[]{:S(2)}) collective-permute-start(f32[72,256]{1,0:T(8,128)S(1)} %get-tuple-element.56), channel_id=1, source_target_pairs={{0,2},{1,3},{2,0},{3,1},{4,6},{5,7},{6,4},{7,5},{8,10},{9,11},{10,... | collective-permute-start | bytes 221192 | tf_op jit(solution)/shard_map/ppermute | solution.py:222
  9.6 0.0 collective-permute-start.3
  9.6 1.7 %collective-permute-start.4 = (f32[8,256]{1,0:T(8,128)S(1)}, f32[8,256]{1,0:T(8,128)S(1)}, u32[]{:S(2)}, u32[]{:S(2)}) collective-permute-start(f32[8,256]{1,0:T(8,128)S(1)} %get-tuple-element.58), channel_id=1, source_target_pairs={{0,8},{8,0},{16,24},{24,16},{1,9},{9,1},{17,25},{25,17},{2,10},{10... | collective-permute-start | bytes 24584 | tf_op jit(solution)/shard_map/ppermute | solution.py:222
  11.3 1.9 %collective-permute-done.4 = f32[8,256]{1,0:T(8,128)S(1)} collective-permute-done((f32[8,256]{1,0:T(8,128)S(1)}, f32[8,256]{1,0:T(8,128)S(1)}, u32[]{:S(2)}, u32[]{:S(2)}) %collective-permute-start.4) | collective-permute-done | bytes 8224 | tf_op jit(solution)/shard_map/ppermute | solution.py:222
  13.2 1.7 %collective-permute-start.5 = (f32[8,256]{1,0:T(8,128)S(1)}, f32[8,256]{1,0:T(8,128)S(1)}, u32[]{:S(2)}, u32[]{:S(2)}) collective-permute-start(f32[8,256]{1,0:T(8,128)S(1)} %add.27), channel_id=1, source_target_pairs={{0,16},{8,24},{16,0},{24,8},{1,17},{9,25},{17,1},{25,9},{2,18},{10... | collective-permute-start | bytes 24584 | tf_op jit(solution)/shard_map/ppermute | solution.py:222
  15.0 1.9 %collective-permute-done.5 = f32[8,256]{1,0:T(8,128)S(1)} collective-permute-done((f32[8,256]{1,0:T(8,128)S(1)}, f32[8,256]{1,0:T(8,128)S(1)}, u32[]{:S(2)}, u32[]{:S(2)}) %collective-permute-start.5) | collective-permute-done | bytes 8224 | tf_op jit(solution)/shard_map/ppermute | solution.py:222
  16.9 0.0 collective-permute-start.6
  16.9 1.2 %collective-permute-done.6 = f32[8,256]{1,0:T(8,128)S(1)} collective-permute-done((f32[8,256]{1,0:T(8,128)S(1)}, f32[8,256]{1,0:T(8,128)S(1)}, u32[]{:S(2)}, u32[]{:S(2)}) %collective-permute-start.6) | collective-permute-done | bytes 8224 | tf_op jit(solution)/shard_map/ppermute | solution.py:222
  18.1 0.0 collective-permute-done.1.refs_1_
  18.1 0.0 collective-permute-done.2.refs_2_
  18.1 0.0 collective-permute-done.3.refs_3_
  18.1 3.9 %collective-permute-start.9 = (f32[72,256]{1,0:T(8,128)S(1)}, f32[72,256]{1,0:T(8,128)S(1)}, u32[]{:S(2)}, u32[]{:S(2)}) collective-permute-start(f32[72,256]{1,0:T(8,128)S(1)} %get-tuple-element.63.refs_0_), channel_id=1, source_target_pairs={{0,3},{1,2},{2,1},{3,0},{4,7},{5,6},{6,5},{7,4},{8,11},{9,10},{10,... | collective-permute-start | bytes 221192 | tf_op jit(solution)/shard_map/ppermute | solution.py:222
  22.0 0.0 collective-permute-start.8
  22.0 0.6 collective-permute-start.7
  22.7 0.0 collective-permute-done.10.other_ref
  22.7 0.5 shard_map.61
  23.2 4.2 %shard_map.62.v_ref = f32[256,256]{1,0:T(8,128)S(1)} custom-call(f32[256,256]{1,0:T(8,128)S(1)} %get-tuple-element.62.v_ref), custom_call_target="tpu_custom_call" | custom-call | tf_op jit(solution)/shard_map/pallas_call | solution.py:156
  27.5 0.0 collective-permute-done.9.refs_3_
  27.5 0.4 collective-permute-done.8.refs_2_
  27.9 0.1 collective-permute-done.7.refs_1_
  28.0 0.1 collective-permute-start.11
  28.1 4.1 %shard_map.64.inv_ref = f32[256,256]{1,0:T(8,128)S(1)} custom-call(f32[256,256]{1,0:T(8,128)S(1)} %shard_map.62.v_ref), custom_call_target="tpu_custom_call" | custom-call | tf_op jit(solution)/shard_map/pallas_call | solution.py:156
  32.2 0.0 collective-permute-done.11.other_ref
  32.2 2.3 %shard_map.65 = (f32[512,256]{1,0:T(8,128)S(1)}, f32[128,256]{1,0:T(8,128)S(1)}) custom-call(s32[1]{0:T(128)} %bitcast.me_ref, s32[1]{0:T(128)} %bitcast.1.pick_ref.top_ref, f32[256,256]{1,0:T(8,128)S(1)} %get-tuple-element.67.own_ref, f32[256,256]{1,0:T(8,128)S(1)} %collective-permute-done.11.other_ref, f32[8,512]{1,0:T(8,128)S(1)} %get-tuple-element.68.row_all_ref, ...), custom_call_target="tpu_custom_call" | custom-call | tf_op jit(solution)/shard_map/pallas_call | solution.py:156
  34.5 0.5 shard_map.66
  35.0 1.7 %collective-permute-start.15 = (f32[128,256]{1,0:T(8,128)S(1)}, f32[128,256]{1,0:T(8,128)S(1)}, u32[]{:S(2)}, u32[]{:S(2)}) collective-permute-start(f32[128,256]{1,0:T(8,128)S(1)} %shard_map.66), channel_id=1, source_target_pairs={{0,8},{4,20},{8,0},{12,28},{16,24},{20,4},{24,16},{28,12},{1,9},{5... | collective-permute-start | bytes 393224 | tf_op jit(solution)/shard_map/ppermute | solution.py:240
  36.6 0.4 collective-permute-start.12
  37.1 2.9 %collective-permute-done.15 = f32[128,256]{1,0:T(8,128)S(1)} collective-permute-done((f32[128,256]{1,0:T(8,128)S(1)}, f32[128,256]{1,0:T(8,128)S(1)}, u32[]{:S(2)}, u32[]{:S(2)}) %collective-permute-start.15) | collective-permute-done | bytes 131104 | tf_op jit(solution)/shard_map/ppermute | solution.py:240
  40.0 1.7 %collective-permute-start.16 = (f32[128,256]{1,0:T(8,128)S(1)}, f32[128,256]{1,0:T(8,128)S(1)}, u32[]{:S(2)}, u32[]{:S(2)}) collective-permute-start(f32[128,256]{1,0:T(8,128)S(1)} %add.32), channel_id=1, source_target_pairs={{0,16},{4,12},{8,24},{12,4},{16,0},{20,28},{24,8},{28,20},{1,17},{... | collective-permute-start | bytes 393224 | tf_op jit(solution)/shard_map/ppermute | solution.py:240
  41.7 0.0 collective-permute-done.12
  41.8 1.5 %collective-permute-start.13 = (f32[128,256]{1,0:T(8,128)S(1)}, f32[128,256]{1,0:T(8,128)S(1)}, u32[]{:S(2)}, u32[]{:S(2)}) collective-permute-start(f32[128,256]{1,0:T(8,128)S(1)} %add.30), channel_id=1, source_target_pairs={{0,16},{4,12},{8,24},{12,4},{16,0},{20,28},{24,8},{28,20},{1,17},{... | collective-permute-start | bytes 393224 | tf_op jit(solution)/shard_map/ppermute | solution.py:240
  43.2 1.8 %collective-permute-done.16 = f32[128,256]{1,0:T(8,128)S(1)} collective-permute-done((f32[128,256]{1,0:T(8,128)S(1)}, f32[128,256]{1,0:T(8,128)S(1)}, u32[]{:S(2)}, u32[]{:S(2)}) %collective-permute-start.16) | collective-permute-done | bytes 131104 | tf_op jit(solution)/shard_map/ppermute | solution.py:240
  45.1 0.1 collective-permute-start.17
  45.2 1.6 %collective-permute-done.13 = f32[128,256]{1,0:T(8,128)S(1)} collective-permute-done((f32[128,256]{1,0:T(8,128)S(1)}, f32[128,256]{1,0:T(8,128)S(1)}, u32[]{:S(2)}, u32[]{:S(2)}) %collective-permute-start.13) | collective-permute-done | bytes 131104 | tf_op jit(solution)/shard_map/ppermute | solution.py:240
  46.8 1.5 %collective-permute-start.14 = (f32[128,256]{1,0:T(8,128)S(1)}, f32[128,256]{1,0:T(8,128)S(1)}, u32[]{:S(2)}, u32[]{:S(2)}) collective-permute-start(f32[128,256]{1,0:T(8,128)S(1)} %get-tuple-element.92), channel_id=1, source_target_pairs={{0,1},{1,0},{2,3},{3,2},{4,5},{5,4},{6,7},{7,6},{8,9},{9,8},{10,11... | collective-permute-start | bytes 393224 | tf_op jit(solution)/shard_map/ppermute | solution.py:222
  48.3 0.0 collective-permute-done.17
  48.4 3.4 %collective-permute-done.14 = f32[128,256]{1,0:T(8,128)S(1)} collective-permute-done((f32[128,256]{1,0:T(8,128)S(1)}, f32[128,256]{1,0:T(8,128)S(1)}, u32[]{:S(2)}, u32[]{:S(2)}) %collective-permute-start.14) | collective-permute-done | bytes 131104 | tf_op jit(solution)/shard_map/ppermute | solution.py:222
  51.9 1.8 %collective-permute-start.18 = (f32[128,256]{1,0:T(8,128)S(1)}, f32[128,256]{1,0:T(8,128)S(1)}, u32[]{:S(2)}, u32[]{:S(2)}) collective-permute-start(f32[128,256]{1,0:T(8,128)S(1)} %add.34.own_ref), channel_id=1, source_target_pairs={{0,2},{1,3},{2,0},{3,1},{4,6},{5,7},{6,4},{7,5},{8,10},{9,11},{10,... | collective-permute-start | bytes 393224 | tf_op jit(solution)/shard_map/ppermute | solution.py:222
  53.6 4.4 %shard_map.67 = (f32[256,256]{1,0:T(8,128)S(1)}, f32[256,256]{1,0:T(8,128)S(1)}, f32[1,256]{1,0:T(1,128)S(1)}) custom-call(f32[256,256]{1,0:T(8,128)S(1)} %pad_maximum_fusion.refs_0_, f32[256,256]{1,0:T(8,128)S(1)} %get-tuple-element.77.refs_1_), custom_call_target="tpu_custom_call" | custom-call | tf_op jit(solution)/shard_map/pallas_call | solution.py:156
  58.0 4.1 %inverse_unit.2 = (f32[256,256]{1,0:T(8,128)S(1)}, f32[512,256]{1,0:T(8,128)}) custom-call(f32[256,256]{1,0:T(8,128)S(1)} %get-tuple-element.78.v_ref, f32[512,256]{1,0:T(8,128)S(1)} %get-tuple-element.73.raw_ref, f32[1,256]{1,0:T(1,128)S(1)} %get-tuple-element.79.scale_ref.refs_4_), custom_call_target="tpu_custom_call" | custom-call | tf_op jit(solution)/shard_map/inverse_unit/pallas_call | solution.py:183
  62.2 0.0 collective-permute-done.18.other_ref
  62.2 0.9 %shard_map.68 = (f32[128,256]{1,0:T(8,128)S(1)}, f32[264,256]{1,0:T(8,128)S(1)}) custom-call(f32[128,256]{1,0:T(8,128)S(1)} %add.34.own_ref, f32[128,256]{1,0:T(8,128)S(1)} %collective-permute-done.18.other_ref, f32[1,256]{1,0:T(1,128)S(1)} %get-tuple-element.79.scale_ref.refs_4_, f32[256,256]{1,0:T(8,128)S(1)} %get-tuple-element.81.inv_ref, ...), custom_call_target="tpu_custom_call" | custom-call | tf_op jit(solution)/shard_map/pallas_call | solution.py:156
  63.0 0.1 collective-permute-start.19
  63.1 1.5 %collective-permute-done.19.refs_1_ = f32[264,256]{1,0:T(8,128)S(1)} collective-permute-done((f32[264,256]{1,0:T(8,128)S(1)}, f32[264,256]{1,0:T(8,128)S(1)}, u32[]{:S(2)}, u32[]{:S(2)}) %collective-permute-start.19) | collective-permute-done | bytes 270368 | tf_op jit(solution)/shard_map/ppermute | solution.py:222
  64.7 2.0 %collective-permute-start.20 = (f32[1,256]{1,0:T(1,128)S(1)}, f32[1,256]{1,0:T(1,128)S(1)}, u32[]{:S(2)}, u32[]{:S(2)}) collective-permute-start(f32[1,256]{1,0:T(1,128)S(1)} %slice_add_fusion.refs_0_), channel_id=1, source_target_pairs={{0,1},{4,6},{1,0},{5,7},{2,3},{6,4},{3,2},{7,5},{8,9},{12,14},{9,8... | collective-permute-start | bytes 3080 | tf_op jit(solution)/shard_map/ppermute | solution.py:494
  66.7 0.3 shard_map.69
  67.0 4.1 %shard_map.70.v_ref = f32[256,256]{1,0:T(8,128)S(1)} custom-call(f32[256,256]{1,0:T(8,128)S(1)} %get-tuple-element.85.v_ref), custom_call_target="tpu_custom_call" | custom-call | tf_op jit(solution)/shard_map/pallas_call | solution.py:156
  71.1 0.0 collective-permute-done.20
  71.1 0.1 collective-permute-start.21
  71.2 2.2 %collective-permute-start.22 = (f32[1,256]{1,0:T(1,128)S(1)}, f32[1,256]{1,0:T(1,128)S(1)}, u32[]{:S(2)}, u32[]{:S(2)}) collective-permute-start(f32[1,256]{1,0:T(1,128)S(1)} %slice_add_fusion.refs_0_), channel_id=1, source_target_pairs={{0,3},{1,2},{2,1},{3,0},{4,7},{5,6},{6,5},{7,4},{8,11},{9,10},{10,... | collective-permute-start | bytes 3080 | tf_op jit(solution)/shard_map/ppermute | solution.py:222
  73.4 4.1 %inverse_unit.3 = (f32[256,256]{1,0:T(8,128)S(1)}, f32[128,256]{1,0:T(8,128)}) custom-call(f32[256,256]{1,0:T(8,128)S(1)} %shard_map.70.v_ref, f32[128,256]{1,0:T(8,128)S(1)} %get-tuple-element.87.raw_ref, f32[1,256]{1,0:T(1,128)S(1)} %get-tuple-element.88.scale_ref.refs_5_), custom_call_target="tpu_custom_call" | custom-call | tf_op jit(solution)/shard_map/inverse_unit/pallas_call | solution.py:183
  77.5 0.0 collective-permute-done.21
  77.6 0.0 collective-permute-done.22.refs_3_
  77.6 0.2 shard_map.71
  77.8 0.6 copy.6
  (15 shorter events, 0.2 us)
Async XLA Ops:
  2.2 1.7 %collective-permute-start = (f32[264,256]{1,0:T(8,128)S(1)}, f32[264,256]{1,0:T(8,128)S(1)}, u32[]{:S(2)}, u32[]{:S(2)}) collective-permute-start(f32[264,256]{1,0:T(8,128)S(1)} %get-tuple-element.52), channel_id=1, source_target_pairs={{0,4},{4,0},{1,5},{5,1},{2,6},{6,2},{3,7},{7,3},{8,12},{12,8},{9,1... | collective-permute-start | bytes 811016 | tf_op jit(solution)/shard_map/ppermute | solution.py:222
  3.5 19.2 %collective-permute-start.10 = (f32[256,256]{1,0:T(8,128)S(1)}, f32[256,256]{1,0:T(8,128)S(1)}, u32[]{:S(2)}, u32[]{:S(2)}) collective-permute-start(f32[256,256]{1,0:T(8,128)S(1)} %get-tuple-element.61.own_ref), channel_id=1, source_target_pairs={{0,4},{4,0},{1,5},{5,1},{2,6},{6,2},{3,7},{7,3},{8,12},{12,8},{9,1... | collective-permute-start | bytes 786440 | tf_op jit(solution)/shard_map/ppermute | solution.py:222
  4.0 14.1 %collective-permute-start.1 = (f32[72,256]{1,0:T(8,128)S(1)}, f32[72,256]{1,0:T(8,128)S(1)}, u32[]{:S(2)}, u32[]{:S(2)}) collective-permute-start(f32[72,256]{1,0:T(8,128)S(1)} %get-tuple-element.55), channel_id=1, source_target_pairs={{0,1},{1,0},{2,3},{3,2},{4,5},{5,4},{6,7},{7,6},{8,9},{9,8},{10,11... | collective-permute-start | bytes 221192 | tf_op jit(solution)/shard_map/ppermute | solution.py:222
  7.0 11.1 %collective-permute-start.2 = (f32[72,256]{1,0:T(8,128)S(1)}, f32[72,256]{1,0:T(8,128)S(1)}, u32[]{:S(2)}, u32[]{:S(2)}) collective-permute-start(f32[72,256]{1,0:T(8,128)S(1)} %get-tuple-element.56), channel_id=1, source_target_pairs={{0,2},{1,3},{2,0},{3,1},{4,6},{5,7},{6,4},{7,5},{8,10},{9,11},{10,... | collective-permute-start | bytes 221192 | tf_op jit(solution)/shard_map/ppermute | solution.py:222
  9.6 8.5 %collective-permute-start.3 = (f32[72,256]{1,0:T(8,128)S(1)}, f32[72,256]{1,0:T(8,128)S(1)}, u32[]{:S(2)}, u32[]{:S(2)}) collective-permute-start(f32[72,256]{1,0:T(8,128)S(1)} %get-tuple-element.57), channel_id=1, source_target_pairs={{0,3},{1,2},{2,1},{3,0},{4,7},{5,6},{6,5},{7,4},{8,11},{9,10},{10,... | collective-permute-start | bytes 221192 | tf_op jit(solution)/shard_map/ppermute | solution.py:222
  9.6 3.7 %collective-permute-start.4 = (f32[8,256]{1,0:T(8,128)S(1)}, f32[8,256]{1,0:T(8,128)S(1)}, u32[]{:S(2)}, u32[]{:S(2)}) collective-permute-start(f32[8,256]{1,0:T(8,128)S(1)} %get-tuple-element.58), channel_id=1, source_target_pairs={{0,8},{8,0},{16,24},{24,16},{1,9},{9,1},{17,25},{25,17},{2,10},{10... | collective-permute-start | bytes 24584 | tf_op jit(solution)/shard_map/ppermute | solution.py:222
  13.2 3.7 %collective-permute-start.5 = (f32[8,256]{1,0:T(8,128)S(1)}, f32[8,256]{1,0:T(8,128)S(1)}, u32[]{:S(2)}, u32[]{:S(2)}) collective-permute-start(f32[8,256]{1,0:T(8,128)S(1)} %add.27), channel_id=1, source_target_pairs={{0,16},{8,24},{16,0},{24,8},{1,17},{9,25},{17,1},{25,9},{2,18},{10... | collective-permute-start | bytes 24584 | tf_op jit(solution)/shard_map/ppermute | solution.py:222
  16.9 1.2 %collective-permute-start.6 = (f32[8,256]{1,0:T(8,128)S(1)}, f32[8,256]{1,0:T(8,128)S(1)}, u32[]{:S(2)}, u32[]{:S(2)}) collective-permute-start(f32[8,256]{1,0:T(8,128)S(1)} %add.28.refs_5_), channel_id=1, source_target_pairs={{0,4},{4,0},{1,5},{5,1},{2,6},{6,2},{3,7},{7,3},{8,12},{12,8},{9,1... | collective-permute-start | bytes 24584 | tf_op jit(solution)/shard_map/ppermute | solution.py:222
  18.1 9.3 %collective-permute-start.9 = (f32[72,256]{1,0:T(8,128)S(1)}, f32[72,256]{1,0:T(8,128)S(1)}, u32[]{:S(2)}, u32[]{:S(2)}) collective-permute-start(f32[72,256]{1,0:T(8,128)S(1)} %get-tuple-element.63.refs_0_), channel_id=1, source_target_pairs={{0,3},{1,2},{2,1},{3,0},{4,7},{5,6},{6,5},{7,4},{8,11},{9,10},{10,... | collective-permute-start | bytes 221192 | tf_op jit(solution)/shard_map/ppermute | solution.py:222
  22.0 5.9 %collective-permute-start.8 = (f32[72,256]{1,0:T(8,128)S(1)}, f32[72,256]{1,0:T(8,128)S(1)}, u32[]{:S(2)}, u32[]{:S(2)}) collective-permute-start(f32[72,256]{1,0:T(8,128)S(1)} %get-tuple-element.63.refs_0_), channel_id=1, source_target_pairs={{0,2},{1,3},{2,0},{3,1},{4,6},{5,7},{6,4},{7,5},{8,10},{9,11},{10,... | collective-permute-start | bytes 221192 | tf_op jit(solution)/shard_map/ppermute | solution.py:222
  22.0 6.0 %collective-permute-start.7 = (f32[72,256]{1,0:T(8,128)S(1)}, f32[72,256]{1,0:T(8,128)S(1)}, u32[]{:S(2)}, u32[]{:S(2)}) collective-permute-start(f32[72,256]{1,0:T(8,128)S(1)} %get-tuple-element.63.refs_0_), channel_id=1, source_target_pairs={{0,1},{1,0},{2,3},{3,2},{4,5},{5,4},{6,7},{7,6},{8,9},{9,8},{10,11... | collective-permute-start | bytes 221192 | tf_op jit(solution)/shard_map/ppermute | solution.py:222
  28.0 4.2 %collective-permute-start.11 = (f32[256,256]{1,0:T(8,128)S(1)}, f32[256,256]{1,0:T(8,128)S(1)}, u32[]{:S(2)}, u32[]{:S(2)}) collective-permute-start(f32[256,256]{1,0:T(8,128)S(1)} %get-tuple-element.67.own_ref), channel_id=1, source_target_pairs={{0,4},{4,0},{1,5},{5,1},{2,6},{6,2},{3,7},{7,3},{8,12},{12,8},{9,1... | collective-permute-start | bytes 786440 | tf_op jit(solution)/shard_map/ppermute | solution.py:222
  35.0 5.0 %collective-permute-start.15 = (f32[128,256]{1,0:T(8,128)S(1)}, f32[128,256]{1,0:T(8,128)S(1)}, u32[]{:S(2)}, u32[]{:S(2)}) collective-permute-start(f32[128,256]{1,0:T(8,128)S(1)} %shard_map.66), channel_id=1, source_target_pairs={{0,8},{4,20},{8,0},{12,28},{16,24},{20,4},{24,16},{28,12},{1,9},{5... | collective-permute-start | bytes 393224 | tf_op jit(solution)/shard_map/ppermute | solution.py:240
  36.6 5.1 %collective-permute-start.12 = (f32[128,256]{1,0:T(8,128)S(1)}, f32[128,256]{1,0:T(8,128)S(1)}, u32[]{:S(2)}, u32[]{:S(2)}) collective-permute-start(f32[128,256]{1,0:T(8,128)S(1)} %get-tuple-element.72), channel_id=1, source_target_pairs={{0,8},{4,20},{8,0},{12,28},{16,24},{20,4},{24,16},{28,12},{1,9},{5... | collective-permute-start | bytes 393224 | tf_op jit(solution)/shard_map/ppermute | solution.py:240
  40.0 5.0 %collective-permute-start.16 = (f32[128,256]{1,0:T(8,128)S(1)}, f32[128,256]{1,0:T(8,128)S(1)}, u32[]{:S(2)}, u32[]{:S(2)}) collective-permute-start(f32[128,256]{1,0:T(8,128)S(1)} %add.32), channel_id=1, source_target_pairs={{0,16},{4,12},{8,24},{12,4},{16,0},{20,28},{24,8},{28,20},{1,17},{... | collective-permute-start | bytes 393224 | tf_op jit(solution)/shard_map/ppermute | solution.py:240
  41.8 5.0 %collective-permute-start.13 = (f32[128,256]{1,0:T(8,128)S(1)}, f32[128,256]{1,0:T(8,128)S(1)}, u32[]{:S(2)}, u32[]{:S(2)}) collective-permute-start(f32[128,256]{1,0:T(8,128)S(1)} %add.30), channel_id=1, source_target_pairs={{0,16},{4,12},{8,24},{12,4},{16,0},{20,28},{24,8},{28,20},{1,17},{... | collective-permute-start | bytes 393224 | tf_op jit(solution)/shard_map/ppermute | solution.py:240
  45.1 3.3 %collective-permute-start.17 = (f32[128,256]{1,0:T(8,128)S(1)}, f32[128,256]{1,0:T(8,128)S(1)}, u32[]{:S(2)}, u32[]{:S(2)}) collective-permute-start(f32[128,256]{1,0:T(8,128)S(1)} %add.33), channel_id=1, source_target_pairs={{0,4},{4,0},{1,5},{5,1},{2,6},{6,2},{3,7},{7,3},{8,12},{12,8},{9,1... | collective-permute-start | bytes 393224 | tf_op jit(solution)/shard_map/ppermute | solution.py:222
  46.8 5.0 %collective-permute-start.14 = (f32[128,256]{1,0:T(8,128)S(1)}, f32[128,256]{1,0:T(8,128)S(1)}, u32[]{:S(2)}, u32[]{:S(2)}) collective-permute-start(f32[128,256]{1,0:T(8,128)S(1)} %get-tuple-element.92), channel_id=1, source_target_pairs={{0,1},{1,0},{2,3},{3,2},{4,5},{5,4},{6,7},{7,6},{8,9},{9,8},{10,11... | collective-permute-start | bytes 393224 | tf_op jit(solution)/shard_map/ppermute | solution.py:222
  51.9 10.3 %collective-permute-start.18 = (f32[128,256]{1,0:T(8,128)S(1)}, f32[128,256]{1,0:T(8,128)S(1)}, u32[]{:S(2)}, u32[]{:S(2)}) collective-permute-start(f32[128,256]{1,0:T(8,128)S(1)} %add.34.own_ref), channel_id=1, source_target_pairs={{0,2},{1,3},{2,0},{3,1},{4,6},{5,7},{6,4},{7,5},{8,10},{9,11},{10,... | collective-permute-start | bytes 393224 | tf_op jit(solution)/shard_map/ppermute | solution.py:222
  63.0 1.6 %collective-permute-start.19 = (f32[264,256]{1,0:T(8,128)S(1)}, f32[264,256]{1,0:T(8,128)S(1)}, u32[]{:S(2)}, u32[]{:S(2)}) collective-permute-start(f32[264,256]{1,0:T(8,128)S(1)} %get-tuple-element.82.refs_0_), channel_id=1, source_target_pairs={{0,4},{4,0},{1,5},{5,1},{2,6},{6,2},{3,7},{7,3},{8,12},{12,8},{9,1... | collective-permute-start | bytes 811016 | tf_op jit(solution)/shard_map/ppermute | solution.py:222
  64.7 6.4 %collective-permute-start.20 = (f32[1,256]{1,0:T(1,128)S(1)}, f32[1,256]{1,0:T(1,128)S(1)}, u32[]{:S(2)}, u32[]{:S(2)}) collective-permute-start(f32[1,256]{1,0:T(1,128)S(1)} %slice_add_fusion.refs_0_), channel_id=1, source_target_pairs={{0,1},{4,6},{1,0},{5,7},{2,3},{6,4},{3,2},{7,5},{8,9},{12,14},{9,8... | collective-permute-start | bytes 3080 | tf_op jit(solution)/shard_map/ppermute | solution.py:494
  71.1 6.4 %collective-permute-start.21 = (f32[1,256]{1,0:T(1,128)S(1)}, f32[1,256]{1,0:T(1,128)S(1)}, u32[]{:S(2)}, u32[]{:S(2)}) collective-permute-start(f32[1,256]{1,0:T(1,128)S(1)} %collective-permute-done.20), channel_id=1, source_target_pairs={{0,4},{4,0},{1,5},{5,1},{2,6},{6,2},{3,7},{7,3},{8,12},{12,8},{9,1... | collective-permute-start | bytes 3080 | tf_op jit(solution)/shard_map/ppermute | solution.py:222
  71.2 6.4 %collective-permute-start.22 = (f32[1,256]{1,0:T(1,128)S(1)}, f32[1,256]{1,0:T(1,128)S(1)}, u32[]{:S(2)}, u32[]{:S(2)}) collective-permute-start(f32[1,256]{1,0:T(1,128)S(1)} %slice_add_fusion.refs_0_), channel_id=1, source_target_pairs={{0,3},{1,2},{2,1},{3,0},{4,7},{5,6},{6,5},{7,4},{8,11},{9,10},{10,... | collective-permute-start | bytes 3080 | tf_op jit(solution)/shard_map/ppermute | solution.py:222

commit v3 on v2

--- a/solution.py
+++ b/solution.py
@@ -77,23 +77,22 @@
     return jnp.concatenate([jnp.concatenate(r, axis=1) for r in rows], axis=0)
 
 
-def invert_square(s_ref, r_ref, t_ref):
-    n, per, early = s_ref.shape[0], block // 8, 2
-
-    def back(x):
-        return pltpu.roll(x, n - block, 1)
-
-    r_ref[...] = pltpu.roll(s_ref[block : n - block, :], block, 1)
-    t_ref[...] = pltpu.roll(s_ref[n - block :, :], block, 1)
-
-    def flush(live):
-        old, top = r_ref[...], t_ref[...]
-        out = lax.broadcasted_iota(jnp.int32, old.shape, 1) < jnp.where(live, block, 0)
-        u = dot(jnp.where(out, old, 0.0)[:, :block], top)
-        return back(jnp.where(out, 0.0, old) - u), back(top)
+def back(x):
+    return pltpu.roll(x, x.shape[1] - block, 1)
+
+
+def flush(r_ref, t_ref, live):
+    old, top = r_ref[...], t_ref[...]
+    out = lax.broadcasted_iota(jnp.int32, old.shape, 1) < jnp.where(live, block, 0)
+    u = dot(jnp.where(out, old, 0.0)[:, :block], top)
+    return back(jnp.where(out, 0.0, old) - u), back(top)
+
+
+def square_steps(r_ref, t_ref, panel, begin, end):
+    n, per, early = r_ref.shape[1], block // 8, 2
 
     def step(p, panel):
-        rest, last = flush(p > 0)
+        rest, last = flush(r_ref, t_ref, p > 0)
         part = split(panel)
         for g in range(per):
             if g == early:
@@ -108,39 +107,41 @@
         t_ref[...] = join(part)
         return back(join(ahead))
 
-    panel = lax.fori_loop(0, n // block, step, s_ref[:block, :])
-    rest, last = flush(True)
-    s_ref[:block, :] = panel
-    s_ref[block : n - block, :] = rest
-    s_ref[n - block :, :] = last
-
-
-square = [pltpu.VMEM((128, 128), jnp.float32), pltpu.VMEM((128 - 2 * block, 128), jnp.float32), pltpu.VMEM((block, 128), jnp.float32)]
-
-
-def eliminate(a_ref, begin, end, *scratch):
-    count = a_ref.shape[0] // 128
-
-    def at(i):
-        return pl.ds(pl.multiple_of(128 * i, 128), 128)
-
-    def step(b, carry):
-        scratch[0][...] = a_ref[at(b), at(b)]
-        invert_square(*scratch)
-        d = scratch[0][...]
-        others = [lax.rem(b + i, count) for i in range(1, count)]
-        rows = [dot(d, a_ref[at(b), at(j)]) for j in others]
+    return lax.fori_loop(begin, end, step, panel)
+
+
+side = 128
+each = side // block
+held = [(side - 2 * block, side), (block, side), (block, side)]
+
+
+def eliminate(a_ref, r_ref, t_ref, p_ref, begin, end):
+    count = a_ref.shape[0] // side
+    while begin < end:
+        b, first = divmod(begin, each)
+        last = min(each, first + end - begin)
+        begin += last - first
+        at = [slice(side * i, side * i + side) for i in range(count)]
+        if first == 0:
+            s = a_ref[at[b], at[b]]
+            p_ref[...] = s[:block]
+            r_ref[...] = pltpu.roll(s[block : side - block], block, 1)
+            t_ref[...] = pltpu.roll(s[side - block :], block, 1)
+        panel = square_steps(r_ref, t_ref, p_ref[...], first, last)
+        p_ref[...] = panel
+        if last < each:
+            continue
+        d = jnp.concatenate([panel, *flush(r_ref, t_ref, True)], axis=0)
+        others = [i for i in range(count) if i != b]
+        rows = [dot(d, a_ref[at[b], at[j]]) for j in others]
         for i in others:
-            left = a_ref[at(i), at(b)]
+            left = a_ref[at[i], at[b]]
             for j, row in zip(others, rows):
-                a_ref[at(i), at(j)] = a_ref[at(i), at(j)] - dot(left, row)
-            a_ref[at(i), at(b)] = -dot(left, d)
+                a_ref[at[i], at[j]] = a_ref[at[i], at[j]] - dot(left, row)
+            a_ref[at[i], at[b]] = -dot(left, d)
         for j, row in zip(others, rows):
-            a_ref[at(b), at(j)] = row
-        a_ref[at(b), at(b)] = d
-        return carry
-
-    lax.fori_loop(begin, end, step, 0)
+            a_ref[at[b], at[j]] = row
+        a_ref[at[b], at[b]] = d
 
 
 def near(x):
@@ -162,32 +163,42 @@
     )(*args[:smem], *[near(a) for a in args[smem:]])
 
 
-def inverse_piece(state, begin, end):
-    def kernel(v_ref, o_ref, *scratch):
-        o_ref[...] = v_ref[...]
-        eliminate(o_ref, begin, end, *scratch)
-
-    return call(kernel, state.shape, state, scratch=square)
-
-
-def inverse_and_unit(state, begin, end, raw, scale):
-    def kernel(v_ref, raw_ref, scale_ref, o_ref, unit_ref, buf, sem, *scratch):
-        buf[...] = raw_ref[...] / scale_ref[...]
-        copy = pltpu.make_async_copy(buf, unit_ref, sem)
-        copy.start()
-        o_ref[...] = v_ref[...]
-        eliminate(o_ref, begin, end, *scratch)
-        copy.wait()
+def inverse_piece(state, begin, end, unit=None):
+    ins, outs = len(state), 1 if end % each == 0 else 4
+
+    def kernel(*refs):
+        refs = list(refs)
+        got, refs = refs[:ins], refs[ins:]
+        if unit:
+            (raw_ref, scale_ref), refs = refs[:2], refs[2:]
+        work, refs = refs[:outs], refs[outs:]
+        if unit:
+            (unit_ref, buf, sem), refs = (refs[0], refs[-2], refs[-1]), refs[1:-2]
+            buf[...] = raw_ref[...] / scale_ref[...]
+            copy = pltpu.make_async_copy(buf, unit_ref, sem)
+            copy.start()
+        work = work + refs[: 4 - outs]
+        for i, o in zip(got, work):
+            o[...] = i[...]
+        eliminate(*work, begin, end)
+        if unit:
+            copy.wait()
 
     vmem = pl.BlockSpec(memory_space=pltpu.VMEM)
-    return pl.pallas_call(
-        kernel,
-        out_shape=[pltpu.VMEM(state.shape, jnp.float32), jax.ShapeDtypeStruct(raw.shape, jnp.float32)],
-        in_specs=[vmem] * 3,
-        out_specs=[vmem, pl.BlockSpec(memory_space=pl.ANY)],
-        scratch_shapes=[pltpu.VMEM(raw.shape, jnp.float32), pltpu.SemaphoreType.DMA(()), *square],
-        name="inverse_unit",
-    )(near(state), near(raw), near(scale))
+    sizes = [state[0].shape] + held
+    scratch = [pltpu.VMEM(x, jnp.float32) for x in sizes[outs:]]
+    shapes = [pltpu.VMEM(x, jnp.float32) for x in sizes[:outs]]
+    specs = [vmem] * outs
+    args = list(state)
+    if unit:
+        args += list(unit)
+        shapes.append(jax.ShapeDtypeStruct(unit[0].shape, jnp.float32))
+        specs.append(pl.BlockSpec(memory_space=pl.ANY))
+        scratch += [pltpu.VMEM(unit[0].shape, jnp.float32), pltpu.SemaphoreType.DMA(())]
+    done = pl.pallas_call(
+        kernel, out_shape=shapes, in_specs=[vmem] * len(args), out_specs=specs, scratch_shapes=scratch, name="inverse"
+    )(*[near(x) for x in args])
+    return (done[:outs], done[outs]) if unit else done
 
 
 def eye(n):
@@ -336,7 +347,7 @@
 
 
 def exporter_kernel(
-    me_ref, top_ref, own_ref, other_ref, row_all_ref, shift_ref, inv_ref, f_ref, col_ref, raw_ref, t_ref, m_ref, s_ref
+    me_ref, top_ref, own_ref, other_ref, row_all_ref, shift_ref, f_ref, col_ref, m_ref, t_ref, s_ref
 ):
     half = own_ref.shape[0]
     m_ref[pl.ds(pl.multiple_of(top_ref[0] * half, half), half), :] = own_ref[...]
@@ -346,23 +357,30 @@
     week = lax.broadcasted_iota(jnp.int32, (s_ref.shape[0], cols), 0)
     s_ref[:, rank:] = jnp.where(week == me_ref[0], col_ref[...], 0.0)
     terms = outer(row_all_ref[...], s_ref[...])
-    raw = dot(m_ref[...] - terms[:, :rank], inv_ref[...])
-    raw_ref[...] = raw
-    t_ref[...] = outer(f_ref[...] - terms[:, rank:], raw)
-
-
-def gram_kernel(top_ref, raw_ref, g_ref):
+    m = m_ref[...] - terms[:, :rank]
+    m_ref[...] = m
+    t_ref[...] = outer(f_ref[...] - terms[:, rank:], m)
+
+
+def raw_kernel(top_ref, m_ref, inv_ref, raw_ref, g_ref):
+    raw_ref[...] = dot(m_ref[...], inv_ref[...])
     grams, rank = g_ref.shape
     at = pl.multiple_of(top_ref[0] * grams, grams) if grams < rank else 0
     g_ref[...] = outer(raw_ref[:, pl.ds(at, grams)], raw_ref[...])
 
 
-def second_kernel(count, end, g_ref, gram_c_ref, v_ref, gram_ref, scale_ref, *scratch):
+def terms_kernel(own_ref, other_ref, inv_ref, w_ref, t_ref, m_ref):
+    t = dot(own_ref[...] + other_ref[...], inv_ref[...])
+    t_ref[...] = t
+    m_ref[...] = t * w_ref[...]
+
+
+def second_kernel(count, end, g_ref, gram_c_ref, v_ref, gram_ref, scale_ref, *held_refs):
     scale, gram = normalised(g_ref[...], count)
     scale_ref[...] = scale
     gram_ref[...] = gram
     v_ref[...] = ridged(gram * gram_c_ref[...])
-    eliminate(v_ref, 0, end, *scratch)
+    eliminate(v_ref, *held_refs, 0, end)
 
 
 def importer_kernel(own_ref, other_ref, scale_ref, inv_ref, t_ref, raw_ref, both_ref):
@@ -377,6 +395,18 @@
 def third_kernel(count, own_ref, other_ref, gram_a_ref, v_ref, scale_ref):
     rank = own_ref.shape[1]
     scale, gram = normalised(own_ref[:rank, :] + other_ref[:rank, :], count)
+    scale_ref[...] = scale
+    v_ref[...] = ridged(gram * gram_a_ref[...])
+
+
+def both_kernel(count, own_ref, side_ref, t_ref, t_side_ref, scale_a_ref, inv_ref, gram_a_ref, raw_ref, week_ref, v_ref, scale_ref):
+    raw = dot(own_ref[...] / scale_a_ref[...], inv_ref[...])
+    raw_side = dot(side_ref[...] / scale_a_ref[...], inv_ref[...])
+    raw_ref[...] = raw
+    week_ref[...] = jnp.sum(raw * t_ref[...], axis=0, keepdims=True) + jnp.sum(
+        raw_side * t_side_ref[...], axis=0, keepdims=True
+    )
+    scale, gram = normalised(outer(raw, raw) + outer(raw_side, raw_side), count)
     scale_ref[...] = scale
     v_ref[...] = ridged(gram * gram_a_ref[...])
 
@@ -429,7 +459,7 @@
     weeks, ni, ne = lax.axis_size("wk"), lax.axis_size("imp"), lax.axis_size("exp")
     me_k = lax.axis_index("wk").astype(jnp.int32)[None]
     top = jnp.where((lax.axis_index("imp") & (ni // 2)) != 0, 1, 0).astype(jnp.int32)[None]
-    steps = rank // 128
+    steps = rank // block
 
     f, w, keep, got, row, small, gram_own, gram_other = shares(f, importer_factor, w, top, ni)
     small = small + swap(small, "exp", 1)
@@ -449,27 +479,31 @@
         me_k, after(gram_own, give), gram_other, *got,
         smem=1, scratch=[pltpu.VMEM((-(-weeks // 8) * 8, rank), jnp.float32)],
     )
-    state = inverse_piece(state, 0, steps // 2)
-    *gathered, state = lax.optimization_barrier((*gathered, state))
+    state = inverse_piece([state], 0, steps // 2)
+    gathered, state = lax.optimization_barrier((gathered, state))
     m_rows, shifts = call(rows_kernel, [(chunk * weeks, rank), (-(-weeks // 8) * 8, rank)], me_k, *gathered, smem=1)
     m_other = swap(m_rows, "imp", ni // 2)
-    inv_a = inverse_piece(state, steps // 2, steps)
-
-    grams = rank // 2 if ni == 2 and rank % 256 == 0 else rank
-    raw_a, t = call(
+    state = inverse_piece(after(state, m_rows), steps // 2, steps * 3 // 4)
+    m_other, state = lax.optimization_barrier((m_other, state))
+    m_a, t = call(
         exporter_kernel,
         [(rows, rank), (cols, rank)],
-        me_k, top, m_rows, m_other, row_all, shifts, inv_a, f, col_mean,
-        smem=2, scratch=[pltpu.VMEM((rows, rank), jnp.float32), pltpu.VMEM((-(-weeks // 8) * 8, rank + cols), jnp.float32)],
+        me_k, top, m_rows, m_other, row_all, shifts, f, col_mean,
+        smem=2, scratch=[pltpu.VMEM((-(-weeks // 8) * 8, rank + cols), jnp.float32)],
     )
-    g_a = call(gram_kernel, (grams, rank), top, after(raw_a, t), smem=1)
-    for i, bit in enumerate(bits("exp")):
+    (inv_a,) = inverse_piece(after(state, t), steps * 3 // 4, steps)
+    grams = rank // 2 if ni == 2 and rank % 256 == 0 else rank
+    raw_a, g_a = call(raw_kernel, [(rows, rank), (grams, rank)], top, m_a, inv_a, smem=1)
+
+    turns = len(bits("exp"))
+    for i in range(turns):
         t_got = crossed(t, "exp", "imp", i)
-        g_got = crossed(g_a, "exp", "imp", i)
-        t = t + t_got
-        g_a = g_a + g_got
-    m_own = t * w
+        if i + 1 < turns:
+            t = t + t_got
+    t, m_own = call(terms_kernel, [(cols, rank), (cols, rank)], t, t_got, inv_a, w)
     m_got = swap(m_own, "wk", 1)
+    for i in range(turns):
+        g_a = g_a + crossed(g_a, "exp", "imp", i)
     g_a = gather_rows(g_a, "imp") if grams < rank else g_a
 
     def second(*refs):
@@ -480,33 +514,53 @@
         m_own = m_own + m_got
         m_got = swap(m_own, "wk", bit)
     state, gram_a, scale_a = call(
-        second, [(rank, rank), (rank, rank), (1, rank)], after(g_a, m_own), gram_c, scratch=square
+        second,
+        [(rank, rank), (rank, rank), (1, rank)],
+        after(g_a, m_own), gram_c,
+        scratch=[pltpu.VMEM(x, jnp.float32) for x in held],
     )
-    inv_b, fac_a = inverse_and_unit(state, steps // 2, steps, raw_a, scale_a)
-    raw_b, both = call(importer_kernel, [(cols, rank), (rank + 8, rank)], m_own, m_got, scale_a, inv_b, t)
-    for bit in bits("imp")[:-1]:
-        both = both + swap(both, "imp", bit)
-    got = swap(both, "imp", ni // 2)
-    m_mine = both[rank : rank + 1] + got[rank : rank + 1]
     paired = weeks == 4 and ni == 2
+    if ni == 2:
+        t_side = swap(t, "imp", 1)
+        state, fac_a = inverse_piece([state], steps // 2, steps - 1, unit=(raw_a, scale_a))
+        m_got, state = lax.optimization_barrier((m_got, state))
+        m_b = m_own + m_got
+        m_side = swap(m_b, "imp", 1)
+        (inv_b,) = inverse_piece(after(state, m_b), steps - 1, steps)
+
+        def both(*refs):
+            both_kernel(cols * ni, *refs)
+
+        raw_b, m_mine, state, scale_b = call(
+            both,
+            [(cols, rank), (1, rank), (rank, rank), (1, rank)],
+            m_b, m_side, t, t_side, scale_a, inv_b, gram_a,
+        )
+    else:
+        (inv_b,), fac_a = inverse_piece([state], steps // 2, steps, unit=(raw_a, scale_a))
+        raw_b, both = call(importer_kernel, [(cols, rank), (rank + 8, rank)], m_own, m_got, scale_a, inv_b, t)
+        for bit in bits("imp")[:-1]:
+            both = both + swap(both, "imp", bit)
+        got = swap(both, "imp", ni // 2)
+        m_mine = both[rank : rank + 1] + got[rank : rank + 1]
+
+        def third(*refs):
+            third_kernel(cols * ni, *refs)
+
+        state, scale_b = call(third, [(rank, rank), (1, rank)], both, got, gram_a)
     if paired:
         pairs = [(j * 4 + k, j * 4 + (k ^ (1 + j))) for k in range(4) for j in range(2)]
         near_row = lax.ppermute(m_mine, ("imp", "wk"), pairs)
         far_row = swap(m_mine, "wk", 3)
     else:
         m_all = [m_mine] + [swap(m_mine, "wk", d) for d in range(1, weeks)]
-
-    def third(*refs):
-        third_kernel(cols * ni, *refs)
-
-    state, scale_b = call(third, [(rank, rank), (1, rank)], both, got, after(gram_a, m_mine))
-    state = inverse_piece(state, 0, steps // 2)
+    state = inverse_piece([state], 0, steps // 2)
     if paired:
         near_row, state = lax.optimization_barrier((near_row, state))
         side_row = swap(near_row, "imp", 1)
         low = lax.axis_index("imp") == 0
         m_all = [m_mine, jnp.where(low, near_row, side_row), jnp.where(low, side_row, near_row), far_row]
-    inv_c, fac_b = inverse_and_unit(state, steps // 2, steps, raw_b, scale_b)
+    (inv_c,), fac_b = inverse_piece(state, steps // 2, steps, unit=(raw_b, scale_b))
     scratch = [pltpu.VMEM((-(-weeks // 8) * 8, rank), jnp.float32)]
     fac_c = call(week_kernel, (1, rank), *m_all, scale_a, scale_b, inv_c, scratch=scratch)
     return (fac_a, fac_b, fac_c)

time: 78.5 us -> 78 us (level)
  waiting for transfers between devices: 17.3 us -> 15.8 us
    pallas_call x2 -> x7, Pallas kernels: 8.28 us -> 20.9 us  [inverse_piece(): pl.pallas_call(kernel, out_shape=shapes, in_specs=[vmem] * len(args), out...]
    pallas_call x14 -> x11, Pallas kernels: 22.3 us -> 10.3 us  [call(): pl.pallas_call(kernel, out_shape=shapes if many else shapes[0], in_specs=...]
    ppermute x18 -> x19, waiting for transfers between devices: 10.9 us -> 9.39 us  [swap(): return lax.ppermute(x, axis, [(i, i ^ bit) for i in range(n)])]
    ppermute x18 -> x19, starting transfers between devices: 20 us -> 20.4 us  [swap(): return lax.ppermute(x, axis, [(i, i ^ bit) for i in range(n)])]
  transfers between devices with their start and end apart: 23 -> 24, of which waited for: 11 -> 10; matrix products, arithmetic and copies ran while one was open for 0% -> 0% of each run, Pallas kernels for 34% -> 31%
where the time goes in v3:
time: 78 us; the launch traced here: 77.9 us
  Pallas kernels  32.7 us (42%)
  starting transfers between devices  27.7 us (36%)
  waiting for transfers between devices  15.8 us (20%)
  between operations  0.92 us (1%)
    pallas_call x7, Pallas kernels, inverse_piece(): pl.pallas_call(kernel, out_shape=shapes, in_specs=[vmem] * len(args), out...  20.9 us
    ppermute x19, starting transfers between devices, swap(): return lax.ppermute(x, axis, [(i, i ^ bit) for i in range(n)])  20.4 us
    pallas_call x11, Pallas kernels, call(): pl.pallas_call(kernel, out_shape=shapes if many else shapes[0], in_specs=...  10.3 us
    ppermute x19, waiting for transfers between devices, swap(): return lax.ppermute(x, axis, [(i, i ^ bit) for i in range(n)])  9.39 us
    ppermute x4, waiting for transfers between devices, crossed(): return lax.ppermute(x, (axis, side), pairs)  6.41 us
    ppermute x4, starting transfers between devices, crossed(): return lax.ppermute(x, (axis, side), pairs)  5.25 us
    ppermute x1, starting transfers between devices, per_device(): near_row = lax.ppermute(m_mine, ('imp', 'wk'), pairs)  2.08 us
    pallas_call x1, Pallas kernels, shares(): pl.pallas_call(open_kernel, out_shape=[pltpu.VMEM(s, jnp.float32) for s i...  1.58 us
  transfers between devices with their start and end apart: 24, of which 10 were waited for; matrix products, arithmetic and copies ran while one was open for 0% of the time, Pallas kernels for 31%

profile of v3, /device:TPU:0, one launch (start us, length us, event | category | flops | bytes accessed | tf_op | source)
XLA Modules:
  0.0 77.9 jit_solution(6566087836068244048)
XLA Ops:
  0.6 1.6 %open.1 = (f32[264,256]{1,0:T(8,128)S(1)}, f32[1,512]{1,0:T(1,128)S(1)}, f32[512,128]{1,0:T(8,128)S(1)}, f32[128,256]{1,0:T(8,128)S(1)}, f32[1,256]{1,0:T(1,128)S(1)}) custom-call(s32[1]{0:T(128)S(6)} %sub.3.pick_ref, f32[512,128]{1,0:T(8,128)} %bitcast.3, f32[128,256]{1,0:T(8,128)} %b_ref.1, f32[1,256]{1,0:T(1,128)} %w_ref.1), custom_call_target="tpu_custom_call" | custom-call | tf_op jit(solution)/shard_map/open/pallas_call | solution.py:427
  2.2 0.6 collective-permute-start
  2.8 0.7 shard_map.58
  3.5 0.1 collective-permute-start.10
  3.6 0.4 collective-permute-done.got_ref
  4.0 3.0 %collective-permute-start.1 = (f32[72,256]{1,0:T(8,128)S(1)}, f32[72,256]{1,0:T(8,128)S(1)}, u32[]{:S(2)}, u32[]{:S(2)}) collective-permute-start(f32[72,256]{1,0:T(8,128)S(1)} %get-tuple-element.83), channel_id=1, source_target_pairs={{0,1},{1,0},{2,3},{3,2},{4,5},{5,4},{6,7},{7,6},{8,9},{9,8},{10,11... | collective-permute-start | bytes 221192 | tf_op jit(solution)/shard_map/ppermute | solution.py:233
  7.0 2.6 %collective-permute-start.2 = (f32[72,256]{1,0:T(8,128)S(1)}, f32[72,256]{1,0:T(8,128)S(1)}, u32[]{:S(2)}, u32[]{:S(2)}) collective-permute-start(f32[72,256]{1,0:T(8,128)S(1)} %get-tuple-element.84), channel_id=1, source_target_pairs={{0,2},{1,3},{2,0},{3,1},{4,6},{5,7},{6,4},{7,5},{8,10},{9,11},{10,... | collective-permute-start | bytes 221192 | tf_op jit(solution)/shard_map/ppermute | solution.py:233
  9.6 0.0 collective-permute-start.3
  9.6 1.7 %collective-permute-start.4 = (f32[8,256]{1,0:T(8,128)S(1)}, f32[8,256]{1,0:T(8,128)S(1)}, u32[]{:S(2)}, u32[]{:S(2)}) collective-permute-start(f32[8,256]{1,0:T(8,128)S(1)} %get-tuple-element.86), channel_id=1, source_target_pairs={{0,8},{8,0},{16,24},{24,16},{1,9},{9,1},{17,25},{25,17},{2,10},{10... | collective-permute-start | bytes 24584 | tf_op jit(solution)/shard_map/ppermute | solution.py:233
  11.3 1.9 %collective-permute-done.4 = f32[8,256]{1,0:T(8,128)S(1)} collective-permute-done((f32[8,256]{1,0:T(8,128)S(1)}, f32[8,256]{1,0:T(8,128)S(1)}, u32[]{:S(2)}, u32[]{:S(2)}) %collective-permute-start.4) | collective-permute-done | bytes 8224 | tf_op jit(solution)/shard_map/ppermute | solution.py:233
  13.2 1.7 %collective-permute-start.5 = (f32[8,256]{1,0:T(8,128)S(1)}, f32[8,256]{1,0:T(8,128)S(1)}, u32[]{:S(2)}, u32[]{:S(2)}) collective-permute-start(f32[8,256]{1,0:T(8,128)S(1)} %add.24), channel_id=1, source_target_pairs={{0,16},{8,24},{16,0},{24,8},{1,17},{9,25},{17,1},{25,9},{2,18},{10... | collective-permute-start | bytes 24584 | tf_op jit(solution)/shard_map/ppermute | solution.py:233
  15.0 1.9 %collective-permute-done.5 = f32[8,256]{1,0:T(8,128)S(1)} collective-permute-done((f32[8,256]{1,0:T(8,128)S(1)}, f32[8,256]{1,0:T(8,128)S(1)}, u32[]{:S(2)}, u32[]{:S(2)}) %collective-permute-start.5) | collective-permute-done | bytes 8224 | tf_op jit(solution)/shard_map/ppermute | solution.py:233
  16.9 0.0 collective-permute-start.6
  16.9 1.2 %collective-permute-done.6 = f32[8,256]{1,0:T(8,128)S(1)} collective-permute-done((f32[8,256]{1,0:T(8,128)S(1)}, f32[8,256]{1,0:T(8,128)S(1)}, u32[]{:S(2)}, u32[]{:S(2)}) %collective-permute-start.6) | collective-permute-done | bytes 8224 | tf_op jit(solution)/shard_map/ppermute | solution.py:233
  18.1 0.0 collective-permute-done.1.refs_1_
  18.1 0.0 collective-permute-done.2.refs_2_
  18.1 0.0 collective-permute-done.3.refs_3_
  18.1 3.9 %collective-permute-start.9 = (f32[72,256]{1,0:T(8,128)S(1)}, f32[72,256]{1,0:T(8,128)S(1)}, u32[]{:S(2)}, u32[]{:S(2)}) collective-permute-start(f32[72,256]{1,0:T(8,128)S(1)} %get-tuple-element.91.refs_0_), channel_id=1, source_target_pairs={{0,3},{1,2},{2,1},{3,0},{4,7},{5,6},{6,5},{7,4},{8,11},{9,10},{10,... | collective-permute-start | bytes 221192 | tf_op jit(solution)/shard_map/ppermute | solution.py:233
  22.0 0.0 collective-permute-start.8
  22.0 0.6 collective-permute-start.7
  22.7 0.0 collective-permute-done.10.other_ref
  22.7 0.5 shard_map.61
  23.2 4.2 %inverse.7.refs_0_ = f32[256,256]{1,0:T(8,128)S(1)} custom-call(f32[256,256]{1,0:T(8,128)S(1)} %get-tuple-element.90.refs_0_), custom_call_target="tpu_custom_call" | custom-call | tf_op jit(solution)/shard_map/inverse/pallas_call | solution.py:198
  27.5 0.0 collective-permute-done.9.refs_3_
  27.5 0.4 collective-permute-done.8.refs_2_
  27.9 0.1 collective-permute-done.7.refs_1_
  28.0 0.1 collective-permute-start.11
  28.1 1.8 %inverse.8 = (f32[256,256]{1,0:T(8,128)S(1)}, f32[64,128]{1,0:T(8,128)S(1)}, f32[32,128]{1,0:T(8,128)S(1)}, f32[32,128]{1,0:T(8,128)S(1)}) custom-call(f32[256,256]{1,0:T(8,128)S(1)} %inverse.7.refs_0_), custom_call_target="tpu_custom_call" | custom-call | tf_op jit(solution)/shard_map/inverse/pallas_call | solution.py:198
  29.9 0.0 collective-permute-done.11.other_ref
  29.9 1.5 %shard_map.63 = (f32[512,256]{1,0:T(8,128)S(1)}, f32[128,256]{1,0:T(8,128)S(1)}) custom-call(s32[1]{0:T(128)} %bitcast.me_ref, s32[1]{0:T(128)} %bitcast.1.pick_ref.top_ref, f32[256,256]{1,0:T(8,128)S(1)} %get-tuple-element.95.own_ref, f32[256,256]{1,0:T(8,128)S(1)} %collective-permute-done.11.other_ref, f32[8,512]{1,0:T(8,128)S(1)} %get-tuple-element.103.row_all_ref, ...), custom_call_target="tpu_custom_call" | custom-call | tf_op jit(solution)/shard_map/pallas_call | solution.py:157
  31.3 2.4 %inverse.9.inv_ref = f32[256,256]{1,0:T(8,128)S(1)} custom-call(f32[256,256]{1,0:T(8,128)S(1)} %get-tuple-element.111.refs_0_, f32[64,128]{1,0:T(8,128)S(1)} %get-tuple-element.112.refs_1_, f32[32,128]{1,0:T(8,128)S(1)} %get-tuple-element.113.refs_2_, f32[32,128]{1,0:T(8,128)S(1)} %get-tuple-element.114.refs_3_), custom_call_target="tpu_custom_call" | custom-call | tf_op jit(solution)/shard_map/inverse/pallas_call | solution.py:198
  33.7 1.4 %shard_map.65 = (f32[512,256]{1,0:T(8,128)S(1)}, f32[128,256]{1,0:T(8,128)S(1)}) custom-call(s32[1]{0:T(128)} %bitcast.1.pick_ref.top_ref, f32[512,256]{1,0:T(8,128)S(1)} %get-tuple-element.116.m_ref, f32[256,256]{1,0:T(8,128)S(1)} %inverse.9.inv_ref), custom_call_target="tpu_custom_call" | custom-call | tf_op jit(solution)/shard_map/pallas_call | solution.py:157
  35.1 1.7 %collective-permute-start.15 = (f32[128,256]{1,0:T(8,128)S(1)}, f32[128,256]{1,0:T(8,128)S(1)}, u32[]{:S(2)}, u32[]{:S(2)}) collective-permute-start(f32[128,256]{1,0:T(8,128)S(1)} %get-tuple-element.117), channel_id=1, source_target_pairs={{0,8},{4,20},{8,0},{12,28},{16,24},{20,4},{24,16},{28,12},{1,9},{5... | collective-permute-start | bytes 393224 | tf_op jit(solution)/shard_map/ppermute | solution.py:251
  36.8 0.4 collective-permute-start.12
  37.2 2.9 %collective-permute-done.15 = f32[128,256]{1,0:T(8,128)S(1)} collective-permute-done((f32[128,256]{1,0:T(8,128)S(1)}, f32[128,256]{1,0:T(8,128)S(1)}, u32[]{:S(2)}, u32[]{:S(2)}) %collective-permute-start.15) | collective-permute-done | bytes 131104 | tf_op jit(solution)/shard_map/ppermute | solution.py:251
  40.2 1.7 %collective-permute-start.16 = (f32[128,256]{1,0:T(8,128)S(1)}, f32[128,256]{1,0:T(8,128)S(1)}, u32[]{:S(2)}, u32[]{:S(2)}) collective-permute-start(f32[128,256]{1,0:T(8,128)S(1)} %add.28), channel_id=1, source_target_pairs={{0,16},{4,12},{8,24},{12,4},{16,0},{20,28},{24,8},{28,20},{1,17},{... | collective-permute-start | bytes 393224 | tf_op jit(solution)/shard_map/ppermute | solution.py:251
  41.9 0.0 collective-permute-done.12
  41.9 1.5 %collective-permute-start.13 = (f32[128,256]{1,0:T(8,128)S(1)}, f32[128,256]{1,0:T(8,128)S(1)}, u32[]{:S(2)}, u32[]{:S(2)}) collective-permute-start(f32[128,256]{1,0:T(8,128)S(1)} %add.27.own_ref), channel_id=1, source_target_pairs={{0,16},{4,12},{8,24},{12,4},{16,0},{20,28},{24,8},{28,20},{1,17},{... | collective-permute-start | bytes 393224 | tf_op jit(solution)/shard_map/ppermute | solution.py:251
  43.4 1.8 %collective-permute-done.16 = f32[128,256]{1,0:T(8,128)S(1)} collective-permute-done((f32[128,256]{1,0:T(8,128)S(1)}, f32[128,256]{1,0:T(8,128)S(1)}, u32[]{:S(2)}, u32[]{:S(2)}) %collective-permute-start.16) | collective-permute-done | bytes 131104 | tf_op jit(solution)/shard_map/ppermute | solution.py:251
  45.2 0.1 collective-permute-start.17
  45.3 1.6 %collective-permute-done.13.other_ref = f32[128,256]{1,0:T(8,128)S(1)} collective-permute-done((f32[128,256]{1,0:T(8,128)S(1)}, f32[128,256]{1,0:T(8,128)S(1)}, u32[]{:S(2)}, u32[]{:S(2)}) %collective-permute-start.13) | collective-permute-done | bytes 131104 | tf_op jit(solution)/shard_map/ppermute | solution.py:251
  46.9 0.3 shard_map.64
  47.2 1.5 %collective-permute-start.14 = (f32[128,256]{1,0:T(8,128)S(1)}, f32[128,256]{1,0:T(8,128)S(1)}, u32[]{:S(2)}, u32[]{:S(2)}) collective-permute-start(f32[128,256]{1,0:T(8,128)S(1)} %get-tuple-element.115), channel_id=1, source_target_pairs={{0,1},{1,0},{2,3},{3,2},{4,5},{5,4},{6,7},{7,6},{8,9},{9,8},{10,11... | collective-permute-start | bytes 393224 | tf_op jit(solution)/shard_map/ppermute | solution.py:233
  48.8 0.0 collective-permute-done.17
  48.8 3.4 %collective-permute-done.14 = f32[128,256]{1,0:T(8,128)S(1)} collective-permute-done((f32[128,256]{1,0:T(8,128)S(1)}, f32[128,256]{1,0:T(8,128)S(1)}, u32[]{:S(2)}, u32[]{:S(2)}) %collective-permute-start.14) | collective-permute-done | bytes 131104 | tf_op jit(solution)/shard_map/ppermute | solution.py:233
  52.3 1.8 %collective-permute-start.18 = (f32[128,256]{1,0:T(8,128)S(1)}, f32[128,256]{1,0:T(8,128)S(1)}, u32[]{:S(2)}, u32[]{:S(2)}) collective-permute-start(f32[128,256]{1,0:T(8,128)S(1)} %add.30), channel_id=1, source_target_pairs={{0,2},{1,3},{2,0},{3,1},{4,6},{5,7},{6,4},{7,5},{8,10},{9,11},{10,... | collective-permute-start | bytes 393224 | tf_op jit(solution)/shard_map/ppermute | solution.py:233
  54.0 0.0 collective-permute-start.20
  54.1 4.4 %shard_map.66 = (f32[256,256]{1,0:T(8,128)S(1)}, f32[256,256]{1,0:T(8,128)S(1)}, f32[1,256]{1,0:T(1,128)S(1)}) custom-call(f32[256,256]{1,0:T(8,128)S(1)} %pad_maximum_fusion.refs_0_, f32[256,256]{1,0:T(8,128)S(1)} %get-tuple-element.121.refs_1_), custom_call_target="tpu_custom_call" | custom-call | tf_op jit(solution)/shard_map/pallas_call | solution.py:157
  58.4 2.6 %inverse.10 = (f32[256,256]{1,0:T(8,128)S(1)}, f32[64,128]{1,0:T(8,128)S(1)}, f32[32,128]{1,0:T(8,128)S(1)}, f32[32,128]{1,0:T(8,128)S(1)}, f32[512,256]{1,0:T(8,128)}) custom-call(f32[256,256]{1,0:T(8,128)S(1)} %get-tuple-element.122.refs_0_, f32[512,256]{1,0:T(8,128)S(1)} %get-tuple-element.123.refs_1_, f32[1,256]{1,0:T(1,128)S(1)} %get-tuple-element.124.refs_2_.refs_4_), custom_call_target="tpu_custom_call" | custom-call | tf_op jit(solution)/shard_map/inverse/pallas_call | solution.py:198
  61.1 0.0 collective-permute-done.18
  61.1 0.6 collective-permute-start.19
  61.7 1.6 %inverse.11.refs_5_ = f32[256,256]{1,0:T(8,128)S(1)} custom-call(f32[256,256]{1,0:T(8,128)S(1)} %get-tuple-element.136.refs_0_, f32[64,128]{1,0:T(8,128)S(1)} %get-tuple-element.137.refs_1_, f32[32,128]{1,0:T(8,128)S(1)} %get-tuple-element.138.refs_2_, f32[32,128]{1,0:T(8,128)S(1)} %get-tuple-element.139.refs_3_), custom_call_target="tpu_custom_call" | custom-call | tf_op jit(solution)/shard_map/inverse/pallas_call | solution.py:198
  63.3 0.0 collective-permute-done.20.refs_3_
  63.3 0.0 collective-permute-done.19.refs_1_
  63.3 1.2 %shard_map.67 = (f32[128,256]{1,0:T(8,128)S(1)}, f32[1,256]{1,0:T(1,128)S(1)}, f32[256,256]{1,0:T(8,128)S(1)}, f32[1,256]{1,0:T(1,128)S(1)}) custom-call(f32[128,256]{1,0:T(8,128)S(1)} %add.31.refs_0_, f32[128,256]{1,0:T(8,128)S(1)} %collective-permute-done.19.refs_1_, f32[128,256]{1,0:T(8,128)S(1)} %get-tuple-element.131.refs_2_, ...), custom_call_target="tpu_custom_call" | custom-call | tf_op jit(solution)/shard_map/pallas_call | solution.py:157
  64.5 2.1 %collective-permute-start.21 = (f32[1,256]{1,0:T(1,128)S(1)}, f32[1,256]{1,0:T(1,128)S(1)}, u32[]{:S(2)}, u32[]{:S(2)}) collective-permute-start(f32[1,256]{1,0:T(1,128)S(1)} %get-tuple-element.141.refs_0_), channel_id=1, source_target_pairs={{0,1},{4,6},{1,0},{5,7},{2,3},{6,4},{3,2},{7,5},{8,9},{12,14},{9,8... | collective-permute-start | bytes 3080 | tf_op jit(solution)/shard_map/ppermute | solution.py:553
  66.6 4.1 %inverse.12.refs_0_ = f32[256,256]{1,0:T(8,128)S(1)} custom-call(f32[256,256]{1,0:T(8,128)S(1)} %get-tuple-element.142.refs_0_), custom_call_target="tpu_custom_call" | custom-call | tf_op jit(solution)/shard_map/inverse/pallas_call | solution.py:198
  70.7 0.0 collective-permute-done.21
  70.7 0.1 collective-permute-start.22
  70.8 2.1 %collective-permute-start.23 = (f32[1,256]{1,0:T(1,128)S(1)}, f32[1,256]{1,0:T(1,128)S(1)}, u32[]{:S(2)}, u32[]{:S(2)}) collective-permute-start(f32[1,256]{1,0:T(1,128)S(1)} %get-tuple-element.141.refs_0_), channel_id=1, source_target_pairs={{0,3},{1,2},{2,1},{3,0},{4,7},{5,6},{6,5},{7,4},{8,11},{9,10},{10,... | collective-permute-start | bytes 3080 | tf_op jit(solution)/shard_map/ppermute | solution.py:233
  72.9 4.1 %inverse.13 = (f32[256,256]{1,0:T(8,128)S(1)}, f32[128,256]{1,0:T(8,128)}) custom-call(f32[256,256]{1,0:T(8,128)S(1)} %inverse.12.refs_0_, f32[128,256]{1,0:T(8,128)S(1)} %get-tuple-element.144.refs_1_, f32[1,256]{1,0:T(1,128)S(1)} %get-tuple-element.145.refs_2_.refs_5_), custom_call_target="tpu_custom_call" | custom-call | tf_op jit(solution)/shard_map/inverse/pallas_call | solution.py:198
  77.1 0.0 collective-permute-done.23.refs_3_
  77.1 0.2 shard_map.68
  77.3 0.6 copy.6
  (15 shorter events, 0.2 us)
Async XLA Ops:
  2.2 1.7 %collective-permute-start = (f32[264,256]{1,0:T(8,128)S(1)}, f32[264,256]{1,0:T(8,128)S(1)}, u32[]{:S(2)}, u32[]{:S(2)}) collective-permute-start(f32[264,256]{1,0:T(8,128)S(1)} %get-tuple-element.80), channel_id=1, source_target_pairs={{0,4},{4,0},{1,5},{5,1},{2,6},{6,2},{3,7},{7,3},{8,12},{12,8},{9,1... | collective-permute-start | bytes 811016 | tf_op jit(solution)/shard_map/ppermute | solution.py:233
  3.5 19.2 %collective-permute-start.10 = (f32[256,256]{1,0:T(8,128)S(1)}, f32[256,256]{1,0:T(8,128)S(1)}, u32[]{:S(2)}, u32[]{:S(2)}) collective-permute-start(f32[256,256]{1,0:T(8,128)S(1)} %get-tuple-element.89.own_ref), channel_id=1, source_target_pairs={{0,4},{4,0},{1,5},{5,1},{2,6},{6,2},{3,7},{7,3},{8,12},{12,8},{9,1... | collective-permute-start | bytes 786440 | tf_op jit(solution)/shard_map/ppermute | solution.py:233
  4.0 14.1 %collective-permute-start.1 = (f32[72,256]{1,0:T(8,128)S(1)}, f32[72,256]{1,0:T(8,128)S(1)}, u32[]{:S(2)}, u32[]{:S(2)}) collective-permute-start(f32[72,256]{1,0:T(8,128)S(1)} %get-tuple-element.83), channel_id=1, source_target_pairs={{0,1},{1,0},{2,3},{3,2},{4,5},{5,4},{6,7},{7,6},{8,9},{9,8},{10,11... | collective-permute-start | bytes 221192 | tf_op jit(solution)/shard_map/ppermute | solution.py:233
  7.0 11.1 %collective-permute-start.2 = (f32[72,256]{1,0:T(8,128)S(1)}, f32[72,256]{1,0:T(8,128)S(1)}, u32[]{:S(2)}, u32[]{:S(2)}) collective-permute-start(f32[72,256]{1,0:T(8,128)S(1)} %get-tuple-element.84), channel_id=1, source_target_pairs={{0,2},{1,3},{2,0},{3,1},{4,6},{5,7},{6,4},{7,5},{8,10},{9,11},{10,... | collective-permute-start | bytes 221192 | tf_op jit(solution)/shard_map/ppermute | solution.py:233
  9.6 8.5 %collective-permute-start.3 = (f32[72,256]{1,0:T(8,128)S(1)}, f32[72,256]{1,0:T(8,128)S(1)}, u32[]{:S(2)}, u32[]{:S(2)}) collective-permute-start(f32[72,256]{1,0:T(8,128)S(1)} %get-tuple-element.85), channel_id=1, source_target_pairs={{0,3},{1,2},{2,1},{3,0},{4,7},{5,6},{6,5},{7,4},{8,11},{9,10},{10,... | collective-permute-start | bytes 221192 | tf_op jit(solution)/shard_map/ppermute | solution.py:233
  9.6 3.7 %collective-permute-start.4 = (f32[8,256]{1,0:T(8,128)S(1)}, f32[8,256]{1,0:T(8,128)S(1)}, u32[]{:S(2)}, u32[]{:S(2)}) collective-permute-start(f32[8,256]{1,0:T(8,128)S(1)} %get-tuple-element.86), channel_id=1, source_target_pairs={{0,8},{8,0},{16,24},{24,16},{1,9},{9,1},{17,25},{25,17},{2,10},{10... | collective-permute-start | bytes 24584 | tf_op jit(solution)/shard_map/ppermute | solution.py:233
  13.2 3.7 %collective-permute-start.5 = (f32[8,256]{1,0:T(8,128)S(1)}, f32[8,256]{1,0:T(8,128)S(1)}, u32[]{:S(2)}, u32[]{:S(2)}) collective-permute-start(f32[8,256]{1,0:T(8,128)S(1)} %add.24), channel_id=1, source_target_pairs={{0,16},{8,24},{16,0},{24,8},{1,17},{9,25},{17,1},{25,9},{2,18},{10... | collective-permute-start | bytes 24584 | tf_op jit(solution)/shard_map/ppermute | solution.py:233
  16.9 1.2 %collective-permute-start.6 = (f32[8,256]{1,0:T(8,128)S(1)}, f32[8,256]{1,0:T(8,128)S(1)}, u32[]{:S(2)}, u32[]{:S(2)}) collective-permute-start(f32[8,256]{1,0:T(8,128)S(1)} %add.25.refs_5_), channel_id=1, source_target_pairs={{0,4},{4,0},{1,5},{5,1},{2,6},{6,2},{3,7},{7,3},{8,12},{12,8},{9,1... | collective-permute-start | bytes 24584 | tf_op jit(solution)/shard_map/ppermute | solution.py:233
  18.1 9.3 %collective-permute-start.9 = (f32[72,256]{1,0:T(8,128)S(1)}, f32[72,256]{1,0:T(8,128)S(1)}, u32[]{:S(2)}, u32[]{:S(2)}) collective-permute-start(f32[72,256]{1,0:T(8,128)S(1)} %get-tuple-element.91.refs_0_), channel_id=1, source_target_pairs={{0,3},{1,2},{2,1},{3,0},{4,7},{5,6},{6,5},{7,4},{8,11},{9,10},{10,... | collective-permute-start | bytes 221192 | tf_op jit(solution)/shard_map/ppermute | solution.py:233
  22.0 5.9 %collective-permute-start.8 = (f32[72,256]{1,0:T(8,128)S(1)}, f32[72,256]{1,0:T(8,128)S(1)}, u32[]{:S(2)}, u32[]{:S(2)}) collective-permute-start(f32[72,256]{1,0:T(8,128)S(1)} %get-tuple-element.91.refs_0_), channel_id=1, source_target_pairs={{0,2},{1,3},{2,0},{3,1},{4,6},{5,7},{6,4},{7,5},{8,10},{9,11},{10,... | collective-permute-start | bytes 221192 | tf_op jit(solution)/shard_map/ppermute | solution.py:233
  22.0 6.0 %collective-permute-start.7 = (f32[72,256]{1,0:T(8,128)S(1)}, f32[72,256]{1,0:T(8,128)S(1)}, u32[]{:S(2)}, u32[]{:S(2)}) collective-permute-start(f32[72,256]{1,0:T(8,128)S(1)} %get-tuple-element.91.refs_0_), channel_id=1, source_target_pairs={{0,1},{1,0},{2,3},{3,2},{4,5},{5,4},{6,7},{7,6},{8,9},{9,8},{10,11... | collective-permute-start | bytes 221192 | tf_op jit(solution)/shard_map/ppermute | solution.py:233
  28.0 1.9 %collective-permute-start.11 = (f32[256,256]{1,0:T(8,128)S(1)}, f32[256,256]{1,0:T(8,128)S(1)}, u32[]{:S(2)}, u32[]{:S(2)}) collective-permute-start(f32[256,256]{1,0:T(8,128)S(1)} %get-tuple-element.95.own_ref), channel_id=1, source_target_pairs={{0,4},{4,0},{1,5},{5,1},{2,6},{6,2},{3,7},{7,3},{8,12},{12,8},{9,1... | collective-permute-start | bytes 786440 | tf_op jit(solution)/shard_map/ppermute | solution.py:233
  35.1 5.0 %collective-permute-start.15 = (f32[128,256]{1,0:T(8,128)S(1)}, f32[128,256]{1,0:T(8,128)S(1)}, u32[]{:S(2)}, u32[]{:S(2)}) collective-permute-start(f32[128,256]{1,0:T(8,128)S(1)} %get-tuple-element.117), channel_id=1, source_target_pairs={{0,8},{4,20},{8,0},{12,28},{16,24},{20,4},{24,16},{28,12},{1,9},{5... | collective-permute-start | bytes 393224 | tf_op jit(solution)/shard_map/ppermute | solution.py:251
  36.8 5.1 %collective-permute-start.12 = (f32[128,256]{1,0:T(8,128)S(1)}, f32[128,256]{1,0:T(8,128)S(1)}, u32[]{:S(2)}, u32[]{:S(2)}) collective-permute-start(f32[128,256]{1,0:T(8,128)S(1)} %get-tuple-element.106), channel_id=1, source_target_pairs={{0,8},{4,20},{8,0},{12,28},{16,24},{20,4},{24,16},{28,12},{1,9},{5... | collective-permute-start | bytes 393224 | tf_op jit(solution)/shard_map/ppermute | solution.py:251
  40.2 5.0 %collective-permute-start.16 = (f32[128,256]{1,0:T(8,128)S(1)}, f32[128,256]{1,0:T(8,128)S(1)}, u32[]{:S(2)}, u32[]{:S(2)}) collective-permute-start(f32[128,256]{1,0:T(8,128)S(1)} %add.28), channel_id=1, source_target_pairs={{0,16},{4,12},{8,24},{12,4},{16,0},{20,28},{24,8},{28,20},{1,17},{... | collective-permute-start | bytes 393224 | tf_op jit(solution)/shard_map/ppermute | solution.py:251
  41.9 5.0 %collective-permute-start.13 = (f32[128,256]{1,0:T(8,128)S(1)}, f32[128,256]{1,0:T(8,128)S(1)}, u32[]{:S(2)}, u32[]{:S(2)}) collective-permute-start(f32[128,256]{1,0:T(8,128)S(1)} %add.27.own_ref), channel_id=1, source_target_pairs={{0,16},{4,12},{8,24},{12,4},{16,0},{20,28},{24,8},{28,20},{1,17},{... | collective-permute-start | bytes 393224 | tf_op jit(solution)/shard_map/ppermute | solution.py:251
  45.2 3.5 %collective-permute-start.17 = (f32[128,256]{1,0:T(8,128)S(1)}, f32[128,256]{1,0:T(8,128)S(1)}, u32[]{:S(2)}, u32[]{:S(2)}) collective-permute-start(f32[128,256]{1,0:T(8,128)S(1)} %add.29), channel_id=1, source_target_pairs={{0,4},{4,0},{1,5},{5,1},{2,6},{6,2},{3,7},{7,3},{8,12},{12,8},{9,1... | collective-permute-start | bytes 393224 | tf_op jit(solution)/shard_map/ppermute | solution.py:233
  47.2 5.0 %collective-permute-start.14 = (f32[128,256]{1,0:T(8,128)S(1)}, f32[128,256]{1,0:T(8,128)S(1)}, u32[]{:S(2)}, u32[]{:S(2)}) collective-permute-start(f32[128,256]{1,0:T(8,128)S(1)} %get-tuple-element.115), channel_id=1, source_target_pairs={{0,1},{1,0},{2,3},{3,2},{4,5},{5,4},{6,7},{7,6},{8,9},{9,8},{10,11... | collective-permute-start | bytes 393224 | tf_op jit(solution)/shard_map/ppermute | solution.py:233
  52.3 8.8 %collective-permute-start.18 = (f32[128,256]{1,0:T(8,128)S(1)}, f32[128,256]{1,0:T(8,128)S(1)}, u32[]{:S(2)}, u32[]{:S(2)}) collective-permute-start(f32[128,256]{1,0:T(8,128)S(1)} %add.30), channel_id=1, source_target_pairs={{0,2},{1,3},{2,0},{3,1},{4,6},{5,7},{6,4},{7,5},{8,10},{9,11},{10,... | collective-permute-start | bytes 393224 | tf_op jit(solution)/shard_map/ppermute | solution.py:233
  54.0 9.2 %collective-permute-start.20 = (f32[128,256]{1,0:T(8,128)S(1)}, f32[128,256]{1,0:T(8,128)S(1)}, u32[]{:S(2)}, u32[]{:S(2)}) collective-permute-start(f32[128,256]{1,0:T(8,128)S(1)} %get-tuple-element.131.refs_2_), channel_id=1, source_target_pairs={{0,4},{4,0},{1,5},{5,1},{2,6},{6,2},{3,7},{7,3},{8,12},{12,8},{9,1... | collective-permute-start | bytes 393224 | tf_op jit(solution)/shard_map/ppermute | solution.py:233
  61.1 2.2 %collective-permute-start.19 = (f32[128,256]{1,0:T(8,128)S(1)}, f32[128,256]{1,0:T(8,128)S(1)}, u32[]{:S(2)}, u32[]{:S(2)}) collective-permute-start(f32[128,256]{1,0:T(8,128)S(1)} %add.31.refs_0_), channel_id=1, source_target_pairs={{0,4},{4,0},{1,5},{5,1},{2,6},{6,2},{3,7},{7,3},{8,12},{12,8},{9,1... | collective-permute-start | bytes 393224 | tf_op jit(solution)/shard_map/ppermute | solution.py:233
  64.5 6.2 %collective-permute-start.21 = (f32[1,256]{1,0:T(1,128)S(1)}, f32[1,256]{1,0:T(1,128)S(1)}, u32[]{:S(2)}, u32[]{:S(2)}) collective-permute-start(f32[1,256]{1,0:T(1,128)S(1)} %get-tuple-element.141.refs_0_), channel_id=1, source_target_pairs={{0,1},{4,6},{1,0},{5,7},{2,3},{6,4},{3,2},{7,5},{8,9},{12,14},{9,8... | collective-permute-start | bytes 3080 | tf_op jit(solution)/shard_map/ppermute | solution.py:553
  70.7 6.3 %collective-permute-start.22 = (f32[1,256]{1,0:T(1,128)S(1)}, f32[1,256]{1,0:T(1,128)S(1)}, u32[]{:S(2)}, u32[]{:S(2)}) collective-permute-start(f32[1,256]{1,0:T(1,128)S(1)} %collective-permute-done.21), channel_id=1, source_target_pairs={{0,4},{4,0},{1,5},{5,1},{2,6},{6,2},{3,7},{7,3},{8,12},{12,8},{9,1... | collective-permute-start | bytes 3080 | tf_op jit(solution)/shard_map/ppermute | solution.py:233
  70.8 6.2 %collective-permute-start.23 = (f32[1,256]{1,0:T(1,128)S(1)}, f32[1,256]{1,0:T(1,128)S(1)}, u32[]{:S(2)}, u32[]{:S(2)}) collective-permute-start(f32[1,256]{1,0:T(1,128)S(1)} %get-tuple-element.141.refs_0_), channel_id=1, source_target_pairs={{0,3},{1,2},{2,1},{3,0},{4,7},{5,6},{6,5},{7,4},{8,11},{9,10},{10,... | collective-permute-start | bytes 3080 | tf_op jit(solution)/shard_map/ppermute | solution.py:233

commit v4 on v3

--- a/solution.py
+++ b/solution.py
@@ -20,12 +20,11 @@
     return jnp.broadcast_to(x[:, i : i + 1] if axis else x[i : i + 1, :], x.shape)
 
 
-def pivot_group(rows, tile, at):
+def pivot_group(rows, tile, at, own):
     lane = lax.broadcasted_iota(jnp.int32, (8, 128), 1)
     sub = lax.broadcasted_iota(jnp.int32, (8, 128), 0)
     part = list(rows)
-    own = [spread(part[tile], 1, at + q) for q in range(8)]
-    raw = list(own)
+    own, raw = list(own), list(own)
     for q in range(0, 8, 2):
         c0, c1 = own[q], own[q + 1]
         a, b = spread(raw[q], 0, q), spread(raw[q + 1], 0, q)
@@ -91,13 +90,17 @@
 def square_steps(r_ref, t_ref, panel, begin, end):
     n, per, early = r_ref.shape[1], block // 8, 2
 
-    def step(p, panel):
+    def columns(rows, at):
+        return [spread(rows, 1, at + q) for q in range(8)]
+
+    def step(p, carry):
+        panel, *own = carry
         rest, last = flush(r_ref, t_ref, p > 0)
         part = split(panel)
         for g in range(per):
             if g == early:
                 ahead = split(apply_block(rest[:block], 8 * early, join(part[:early])))
-            part[g] = pivot_group(part[g], 0, 8 * g)
+            part[g] = pivot_group(part[g], 0, 8 * g, own if g == 0 else columns(part[g][0], 8 * g))
             if g >= early:
                 ahead = [apply_group(r, 0, 8 * g, part[g]) for r in ahead]
             for h in ([g + 1] if g + 1 < per else []) + [h for h in range(per) if h not in (g, g + 1)]:
@@ -105,9 +108,9 @@
         r_ref[: n - 3 * block, :] = rest[block:]
         r_ref[n - 3 * block :, :] = last
         t_ref[...] = join(part)
-        return back(join(ahead))
-
-    return lax.fori_loop(begin, end, step, panel)
+        return (back(join(ahead)), *columns(ahead[0][0], block))
+
+    return lax.fori_loop(begin, end, step, (panel, *columns(panel[:8], 0)))[0]
 
 
 side = 128
@@ -550,13 +553,13 @@
         state, scale_b = call(third, [(rank, rank), (1, rank)], both, got, gram_a)
     if paired:
         pairs = [(j * 4 + k, j * 4 + (k ^ (1 + j))) for k in range(4) for j in range(2)]
+        far_row = swap(m_mine, "wk", 3)
         near_row = lax.ppermute(m_mine, ("imp", "wk"), pairs)
-        far_row = swap(m_mine, "wk", 3)
     else:
         m_all = [m_mine] + [swap(m_mine, "wk", d) for d in range(1, weeks)]
     state = inverse_piece([state], 0, steps // 2)
     if paired:
-        near_row, state = lax.optimization_barrier((near_row, state))
+        near_row, far_row, state = lax.optimization_barrier((near_row, far_row, state))
         side_row = swap(near_row, "imp", 1)
         low = lax.axis_index("imp") == 0
         m_all = [m_mine, jnp.where(low, near_row, side_row), jnp.where(low, side_row, near_row), far_row]

time: 78 us -> 75.8 us (0.972)
  starting transfers between devices: 27.7 us -> 26.4 us
  Pallas kernels: 32.7 us -> 31.7 us
    ppermute x1, starting transfers between devices: 2.08 us -> 0.01 us  [per_device(): near_row = lax.ppermute(m_mine, ('imp', 'wk'), pairs)]
    pallas_call x7, Pallas kernels: 20.9 us -> 20 us  [inverse_piece(): pl.pallas_call(kernel, out_shape=shapes, in_specs=[vmem] * len(args), out...]
where the time goes in v4:
time: 75.8 us; the launch traced here: 75.6 us
  Pallas kernels  31.7 us (42%)
  starting transfers between devices  26.4 us (35%)
  waiting for transfers between devices  16 us (21%)
  between operations  0.9 us (1%)
    ppermute x19, starting transfers between devices, swap(): return lax.ppermute(x, axis, [(i, i ^ bit) for i in range(n)])  21.1 us
    pallas_call x7, Pallas kernels, inverse_piece(): pl.pallas_call(kernel, out_shape=shapes, in_specs=[vmem] * len(args), out...  20 us
    pallas_call x11, Pallas kernels, call(): pl.pallas_call(kernel, out_shape=shapes if many else shapes[0], in_specs=...  10.1 us
    ppermute x19, waiting for transfers between devices, swap(): return lax.ppermute(x, axis, [(i, i ^ bit) for i in range(n)])  9.54 us
    ppermute x4, waiting for transfers between devices, crossed(): return lax.ppermute(x, (axis, side), pairs)  6.41 us
    ppermute x4, starting transfers between devices, crossed(): return lax.ppermute(x, (axis, side), pairs)  5.25 us
    pallas_call x1, Pallas kernels, shares(): pl.pallas_call(open_kernel, out_shape=[pltpu.VMEM(s, jnp.float32) for s i...  1.58 us
  transfers between devices with their start and end apart: 24, of which 10 were waited for; matrix products, arithmetic and copies ran while one was open for 0% of the time, Pallas kernels for 31%

profile of v4, /device:TPU:0, one launch (start us, length us, event | category | flops | bytes accessed | tf_op | source)
XLA Modules:
  0.0 75.6 jit_solution(1355858735771332565)
XLA Ops:
  0.6 1.6 %open.1 = (f32[264,256]{1,0:T(8,128)S(1)}, f32[1,512]{1,0:T(1,128)S(1)}, f32[512,128]{1,0:T(8,128)S(1)}, f32[128,256]{1,0:T(8,128)S(1)}, f32[1,256]{1,0:T(1,128)S(1)}) custom-call(s32[1]{0:T(128)S(6)} %sub.3.pick_ref, f32[512,128]{1,0:T(8,128)} %bitcast.3, f32[128,256]{1,0:T(8,128)} %b_ref.1, f32[1,256]{1,0:T(1,128)} %w_ref.1), custom_call_target="tpu_custom_call" | custom-call | tf_op jit(solution)/shard_map/open/pallas_call | solution.py:430
  2.2 0.6 collective-permute-start
  2.8 0.7 shard_map.58
  3.5 0.1 collective-permute-start.10
  3.6 0.4 collective-permute-done.got_ref
  4.0 3.0 %collective-permute-start.1 = (f32[72,256]{1,0:T(8,128)S(1)}, f32[72,256]{1,0:T(8,128)S(1)}, u32[]{:S(2)}, u32[]{:S(2)}) collective-permute-start(f32[72,256]{1,0:T(8,128)S(1)} %get-tuple-element.84), channel_id=1, source_target_pairs={{0,1},{1,0},{2,3},{3,2},{4,5},{5,4},{6,7},{7,6},{8,9},{9,8},{10,11... | collective-permute-start | bytes 221192 | tf_op jit(solution)/shard_map/ppermute | solution.py:236
  7.0 2.6 %collective-permute-start.2 = (f32[72,256]{1,0:T(8,128)S(1)}, f32[72,256]{1,0:T(8,128)S(1)}, u32[]{:S(2)}, u32[]{:S(2)}) collective-permute-start(f32[72,256]{1,0:T(8,128)S(1)} %get-tuple-element.85), channel_id=1, source_target_pairs={{0,2},{1,3},{2,0},{3,1},{4,6},{5,7},{6,4},{7,5},{8,10},{9,11},{10,... | collective-permute-start | bytes 221192 | tf_op jit(solution)/shard_map/ppermute | solution.py:236
  9.6 0.0 collective-permute-start.3
  9.6 1.7 %collective-permute-start.4 = (f32[8,256]{1,0:T(8,128)S(1)}, f32[8,256]{1,0:T(8,128)S(1)}, u32[]{:S(2)}, u32[]{:S(2)}) collective-permute-start(f32[8,256]{1,0:T(8,128)S(1)} %get-tuple-element.87), channel_id=1, source_target_pairs={{0,8},{8,0},{16,24},{24,16},{1,9},{9,1},{17,25},{25,17},{2,10},{10... | collective-permute-start | bytes 24584 | tf_op jit(solution)/shard_map/ppermute | solution.py:236
  11.3 1.9 %collective-permute-done.4 = f32[8,256]{1,0:T(8,128)S(1)} collective-permute-done((f32[8,256]{1,0:T(8,128)S(1)}, f32[8,256]{1,0:T(8,128)S(1)}, u32[]{:S(2)}, u32[]{:S(2)}) %collective-permute-start.4) | collective-permute-done | bytes 8224 | tf_op jit(solution)/shard_map/ppermute | solution.py:236
  13.2 1.7 %collective-permute-start.5 = (f32[8,256]{1,0:T(8,128)S(1)}, f32[8,256]{1,0:T(8,128)S(1)}, u32[]{:S(2)}, u32[]{:S(2)}) collective-permute-start(f32[8,256]{1,0:T(8,128)S(1)} %add.24), channel_id=1, source_target_pairs={{0,16},{8,24},{16,0},{24,8},{1,17},{9,25},{17,1},{25,9},{2,18},{10... | collective-permute-start | bytes 24584 | tf_op jit(solution)/shard_map/ppermute | solution.py:236
  15.0 1.9 %collective-permute-done.5 = f32[8,256]{1,0:T(8,128)S(1)} collective-permute-done((f32[8,256]{1,0:T(8,128)S(1)}, f32[8,256]{1,0:T(8,128)S(1)}, u32[]{:S(2)}, u32[]{:S(2)}) %collective-permute-start.5) | collective-permute-done | bytes 8224 | tf_op jit(solution)/shard_map/ppermute | solution.py:236
  16.9 0.0 collective-permute-start.6
  16.9 1.2 %collective-permute-done.6 = f32[8,256]{1,0:T(8,128)S(1)} collective-permute-done((f32[8,256]{1,0:T(8,128)S(1)}, f32[8,256]{1,0:T(8,128)S(1)}, u32[]{:S(2)}, u32[]{:S(2)}) %collective-permute-start.6) | collective-permute-done | bytes 8224 | tf_op jit(solution)/shard_map/ppermute | solution.py:236
  18.1 0.0 collective-permute-done.1.refs_1_
  18.1 0.0 collective-permute-done.2.refs_2_
  18.1 0.0 collective-permute-done.3.refs_3_
  18.1 3.9 %collective-permute-start.9 = (f32[72,256]{1,0:T(8,128)S(1)}, f32[72,256]{1,0:T(8,128)S(1)}, u32[]{:S(2)}, u32[]{:S(2)}) collective-permute-start(f32[72,256]{1,0:T(8,128)S(1)} %get-tuple-element.92.refs_0_), channel_id=1, source_target_pairs={{0,3},{1,2},{2,1},{3,0},{4,7},{5,6},{6,5},{7,4},{8,11},{9,10},{10,... | collective-permute-start | bytes 221192 | tf_op jit(solution)/shard_map/ppermute | solution.py:236
  22.0 0.0 collective-permute-start.8
  22.0 0.6 collective-permute-start.7
  22.7 0.0 collective-permute-done.10.other_ref
  22.7 0.5 shard_map.61
  23.2 4.1 %inverse.7.refs_0_ = f32[256,256]{1,0:T(8,128)S(1)} custom-call(f32[256,256]{1,0:T(8,128)S(1)} %get-tuple-element.91.refs_0_), custom_call_target="tpu_custom_call" | custom-call | tf_op jit(solution)/shard_map/inverse/pallas_call | solution.py:201
  27.3 0.0 collective-permute-done.9.refs_3_
  27.3 0.6 collective-permute-done.8.refs_2_
  27.9 0.1 collective-permute-done.7.refs_1_
  28.0 0.1 collective-permute-start.11
  28.1 1.7 %inverse.8 = (f32[256,256]{1,0:T(8,128)S(1)}, f32[64,128]{1,0:T(8,128)S(1)}, f32[32,128]{1,0:T(8,128)S(1)}, f32[32,128]{1,0:T(8,128)S(1)}) custom-call(f32[256,256]{1,0:T(8,128)S(1)} %inverse.7.refs_0_), custom_call_target="tpu_custom_call" | custom-call | tf_op jit(solution)/shard_map/inverse/pallas_call | solution.py:201
  29.8 0.0 collective-permute-done.11.other_ref
  29.8 1.5 %shard_map.63 = (f32[512,256]{1,0:T(8,128)S(1)}, f32[128,256]{1,0:T(8,128)S(1)}) custom-call(s32[1]{0:T(128)} %bitcast.me_ref, s32[1]{0:T(128)} %bitcast.1.pick_ref.top_ref, f32[256,256]{1,0:T(8,128)S(1)} %get-tuple-element.96.own_ref, f32[256,256]{1,0:T(8,128)S(1)} %collective-permute-done.11.other_ref, f32[8,512]{1,0:T(8,128)S(1)} %get-tuple-element.104.row_all_ref, ...), custom_call_target="tpu_custom_call" | custom-call | tf_op jit(solution)/shard_map/pallas_call | solution.py:160
  31.2 2.3 %inverse.9.inv_ref = f32[256,256]{1,0:T(8,128)S(1)} custom-call(f32[256,256]{1,0:T(8,128)S(1)} %get-tuple-element.112.refs_0_, f32[64,128]{1,0:T(8,128)S(1)} %get-tuple-element.113.refs_1_, f32[32,128]{1,0:T(8,128)S(1)} %get-tuple-element.114.refs_2_, f32[32,128]{1,0:T(8,128)S(1)} %get-tuple-element.115.refs_3_), custom_call_target="tpu_custom_call" | custom-call | tf_op jit(solution)/shard_map/inverse/pallas_call | solution.py:201
  33.6 1.4 %shard_map.65 = (f32[512,256]{1,0:T(8,128)S(1)}, f32[128,256]{1,0:T(8,128)S(1)}) custom-call(s32[1]{0:T(128)} %bitcast.1.pick_ref.top_ref, f32[512,256]{1,0:T(8,128)S(1)} %get-tuple-element.117.m_ref, f32[256,256]{1,0:T(8,128)S(1)} %inverse.9.inv_ref), custom_call_target="tpu_custom_call" | custom-call | tf_op jit(solution)/shard_map/pallas_call | solution.py:160
  35.0 1.7 %collective-permute-start.15 = (f32[128,256]{1,0:T(8,128)S(1)}, f32[128,256]{1,0:T(8,128)S(1)}, u32[]{:S(2)}, u32[]{:S(2)}) collective-permute-start(f32[128,256]{1,0:T(8,128)S(1)} %get-tuple-element.118), channel_id=1, source_target_pairs={{0,8},{4,20},{8,0},{12,28},{16,24},{20,4},{24,16},{28,12},{1,9},{5... | collective-permute-start | bytes 393224 | tf_op jit(solution)/shard_map/ppermute | solution.py:254
  36.6 0.4 collective-permute-start.12
  37.1 2.9 %collective-permute-done.15 = f32[128,256]{1,0:T(8,128)S(1)} collective-permute-done((f32[128,256]{1,0:T(8,128)S(1)}, f32[128,256]{1,0:T(8,128)S(1)}, u32[]{:S(2)}, u32[]{:S(2)}) %collective-permute-start.15) | collective-permute-done | bytes 131104 | tf_op jit(solution)/shard_map/ppermute | solution.py:254
  40.0 1.7 %collective-permute-start.16 = (f32[128,256]{1,0:T(8,128)S(1)}, f32[128,256]{1,0:T(8,128)S(1)}, u32[]{:S(2)}, u32[]{:S(2)}) collective-permute-start(f32[128,256]{1,0:T(8,128)S(1)} %add.28), channel_id=1, source_target_pairs={{0,16},{4,12},{8,24},{12,4},{16,0},{20,28},{24,8},{28,20},{1,17},{... | collective-permute-start | bytes 393224 | tf_op jit(solution)/shard_map/ppermute | solution.py:254
  41.7 0.0 collective-permute-done.12
  41.8 1.5 %collective-permute-start.13 = (f32[128,256]{1,0:T(8,128)S(1)}, f32[128,256]{1,0:T(8,128)S(1)}, u32[]{:S(2)}, u32[]{:S(2)}) collective-permute-start(f32[128,256]{1,0:T(8,128)S(1)} %add.27.own_ref), channel_id=1, source_target_pairs={{0,16},{4,12},{8,24},{12,4},{16,0},{20,28},{24,8},{28,20},{1,17},{... | collective-permute-start | bytes 393224 | tf_op jit(solution)/shard_map/ppermute | solution.py:254
  43.2 1.8 %collective-permute-done.16 = f32[128,256]{1,0:T(8,128)S(1)} collective-permute-done((f32[128,256]{1,0:T(8,128)S(1)}, f32[128,256]{1,0:T(8,128)S(1)}, u32[]{:S(2)}, u32[]{:S(2)}) %collective-permute-start.16) | collective-permute-done | bytes 131104 | tf_op jit(solution)/shard_map/ppermute | solution.py:254
  45.1 0.1 collective-permute-start.17
  45.2 1.6 %collective-permute-done.13.other_ref = f32[128,256]{1,0:T(8,128)S(1)} collective-permute-done((f32[128,256]{1,0:T(8,128)S(1)}, f32[128,256]{1,0:T(8,128)S(1)}, u32[]{:S(2)}, u32[]{:S(2)}) %collective-permute-start.13) | collective-permute-done | bytes 131104 | tf_op jit(solution)/shard_map/ppermute | solution.py:254
  46.8 0.3 shard_map.64
  47.1 1.5 %collective-permute-start.14 = (f32[128,256]{1,0:T(8,128)S(1)}, f32[128,256]{1,0:T(8,128)S(1)}, u32[]{:S(2)}, u32[]{:S(2)}) collective-permute-start(f32[128,256]{1,0:T(8,128)S(1)} %get-tuple-element.116), channel_id=1, source_target_pairs={{0,1},{1,0},{2,3},{3,2},{4,5},{5,4},{6,7},{7,6},{8,9},{9,8},{10,11... | collective-permute-start | bytes 393224 | tf_op jit(solution)/shard_map/ppermute | solution.py:236
  48.6 0.0 collective-permute-done.17
  48.7 3.4 %collective-permute-done.14 = f32[128,256]{1,0:T(8,128)S(1)} collective-permute-done((f32[128,256]{1,0:T(8,128)S(1)}, f32[128,256]{1,0:T(8,128)S(1)}, u32[]{:S(2)}, u32[]{:S(2)}) %collective-permute-start.14) | collective-permute-done | bytes 131104 | tf_op jit(solution)/shard_map/ppermute | solution.py:236
  52.1 1.7 %collective-permute-start.18 = (f32[128,256]{1,0:T(8,128)S(1)}, f32[128,256]{1,0:T(8,128)S(1)}, u32[]{:S(2)}, u32[]{:S(2)}) collective-permute-start(f32[128,256]{1,0:T(8,128)S(1)} %add.30), channel_id=1, source_target_pairs={{0,2},{1,3},{2,0},{3,1},{4,6},{5,7},{6,4},{7,5},{8,10},{9,11},{10,... | collective-permute-start | bytes 393224 | tf_op jit(solution)/shard_map/ppermute | solution.py:236
  53.8 0.0 collective-permute-start.20
  53.8 4.2 %shard_map.66 = (f32[256,256]{1,0:T(8,128)S(1)}, f32[256,256]{1,0:T(8,128)S(1)}, f32[1,256]{1,0:T(1,128)S(1)}) custom-call(f32[256,256]{1,0:T(8,128)S(1)} %pad_maximum_fusion.refs_0_, f32[256,256]{1,0:T(8,128)S(1)} %get-tuple-element.122.refs_1_), custom_call_target="tpu_custom_call" | custom-call | tf_op jit(solution)/shard_map/pallas_call | solution.py:160
  58.0 2.5 %inverse.10 = (f32[256,256]{1,0:T(8,128)S(1)}, f32[64,128]{1,0:T(8,128)S(1)}, f32[32,128]{1,0:T(8,128)S(1)}, f32[32,128]{1,0:T(8,128)S(1)}, f32[512,256]{1,0:T(8,128)}) custom-call(f32[256,256]{1,0:T(8,128)S(1)} %get-tuple-element.123.refs_0_, f32[512,256]{1,0:T(8,128)S(1)} %get-tuple-element.124.refs_1_, f32[1,256]{1,0:T(1,128)S(1)} %get-tuple-element.125.refs_2_.refs_4_), custom_call_target="tpu_custom_call" | custom-call | tf_op jit(solution)/shard_map/inverse/pallas_call | solution.py:201
  60.4 0.0 collective-permute-done.18
  60.5 0.6 collective-permute-start.19
  61.1 1.6 %inverse.11.refs_5_ = f32[256,256]{1,0:T(8,128)S(1)} custom-call(f32[256,256]{1,0:T(8,128)S(1)} %get-tuple-element.137.refs_0_, f32[64,128]{1,0:T(8,128)S(1)} %get-tuple-element.138.refs_1_, f32[32,128]{1,0:T(8,128)S(1)} %get-tuple-element.139.refs_2_, f32[32,128]{1,0:T(8,128)S(1)} %get-tuple-element.140.refs_3_), custom_call_target="tpu_custom_call" | custom-call | tf_op jit(solution)/shard_map/inverse/pallas_call | solution.py:201
  62.6 0.0 collective-permute-done.20.refs_3_
  62.6 0.0 collective-permute-done.19.refs_1_
  62.7 1.2 %shard_map.67 = (f32[128,256]{1,0:T(8,128)S(1)}, f32[1,256]{1,0:T(1,128)S(1)}, f32[256,256]{1,0:T(8,128)S(1)}, f32[1,256]{1,0:T(1,128)S(1)}) custom-call(f32[128,256]{1,0:T(8,128)S(1)} %add.31.refs_0_, f32[128,256]{1,0:T(8,128)S(1)} %collective-permute-done.19.refs_1_, f32[128,256]{1,0:T(8,128)S(1)} %get-tuple-element.132.refs_2_, ...), custom_call_target="tpu_custom_call" | custom-call | tf_op jit(solution)/shard_map/pallas_call | solution.py:160
  63.9 2.3 %collective-permute-start.22 = (f32[1,256]{1,0:T(1,128)S(1)}, f32[1,256]{1,0:T(1,128)S(1)}, u32[]{:S(2)}, u32[]{:S(2)}) collective-permute-start(f32[1,256]{1,0:T(1,128)S(1)} %get-tuple-element.142.refs_0_), channel_id=1, source_target_pairs={{0,3},{1,2},{2,1},{3,0},{4,7},{5,6},{6,5},{7,4},{8,11},{9,10},{10,... | collective-permute-start | bytes 3080 | tf_op jit(solution)/shard_map/ppermute | solution.py:236
  66.2 0.0 collective-permute-start.21
  66.2 3.9 %inverse.12.refs_0_ = f32[256,256]{1,0:T(8,128)S(1)} custom-call(f32[256,256]{1,0:T(8,128)S(1)} %get-tuple-element.143.refs_0_), custom_call_target="tpu_custom_call" | custom-call | tf_op jit(solution)/shard_map/inverse/pallas_call | solution.py:201
  70.1 0.0 collective-permute-done.22.refs_3_
  70.1 0.0 collective-permute-done.21
  70.1 0.7 collective-permute-start.23
  70.9 3.9 %inverse.13 = (f32[256,256]{1,0:T(8,128)S(1)}, f32[128,256]{1,0:T(8,128)}) custom-call(f32[256,256]{1,0:T(8,128)S(1)} %inverse.12.refs_0_, f32[128,256]{1,0:T(8,128)S(1)} %get-tuple-element.145.refs_1_, f32[1,256]{1,0:T(1,128)S(1)} %get-tuple-element.146.refs_2_.refs_5_), custom_call_target="tpu_custom_call" | custom-call | tf_op jit(solution)/shard_map/inverse/pallas_call | solution.py:201
  74.8 0.2 shard_map.68
  75.1 0.6 copy.6
  (15 shorter events, 0.2 us)
Async XLA Ops:
  2.2 1.7 %collective-permute-start = (f32[264,256]{1,0:T(8,128)S(1)}, f32[264,256]{1,0:T(8,128)S(1)}, u32[]{:S(2)}, u32[]{:S(2)}) collective-permute-start(f32[264,256]{1,0:T(8,128)S(1)} %get-tuple-element.81), channel_id=1, source_target_pairs={{0,4},{4,0},{1,5},{5,1},{2,6},{6,2},{3,7},{7,3},{8,12},{12,8},{9,1... | collective-permute-start | bytes 811016 | tf_op jit(solution)/shard_map/ppermute | solution.py:236
  3.5 19.2 %collective-permute-start.10 = (f32[256,256]{1,0:T(8,128)S(1)}, f32[256,256]{1,0:T(8,128)S(1)}, u32[]{:S(2)}, u32[]{:S(2)}) collective-permute-start(f32[256,256]{1,0:T(8,128)S(1)} %get-tuple-element.90.own_ref), channel_id=1, source_target_pairs={{0,4},{4,0},{1,5},{5,1},{2,6},{6,2},{3,7},{7,3},{8,12},{12,8},{9,1... | collective-permute-start | bytes 786440 | tf_op jit(solution)/shard_map/ppermute | solution.py:236
  4.0 14.1 %collective-permute-start.1 = (f32[72,256]{1,0:T(8,128)S(1)}, f32[72,256]{1,0:T(8,128)S(1)}, u32[]{:S(2)}, u32[]{:S(2)}) collective-permute-start(f32[72,256]{1,0:T(8,128)S(1)} %get-tuple-element.84), channel_id=1, source_target_pairs={{0,1},{1,0},{2,3},{3,2},{4,5},{5,4},{6,7},{7,6},{8,9},{9,8},{10,11... | collective-permute-start | bytes 221192 | tf_op jit(solution)/shard_map/ppermute | solution.py:236
  7.0 11.1 %collective-permute-start.2 = (f32[72,256]{1,0:T(8,128)S(1)}, f32[72,256]{1,0:T(8,128)S(1)}, u32[]{:S(2)}, u32[]{:S(2)}) collective-permute-start(f32[72,256]{1,0:T(8,128)S(1)} %get-tuple-element.85), channel_id=1, source_target_pairs={{0,2},{1,3},{2,0},{3,1},{4,6},{5,7},{6,4},{7,5},{8,10},{9,11},{10,... | collective-permute-start | bytes 221192 | tf_op jit(solution)/shard_map/ppermute | solution.py:236
  9.6 8.5 %collective-permute-start.3 = (f32[72,256]{1,0:T(8,128)S(1)}, f32[72,256]{1,0:T(8,128)S(1)}, u32[]{:S(2)}, u32[]{:S(2)}) collective-permute-start(f32[72,256]{1,0:T(8,128)S(1)} %get-tuple-element.86), channel_id=1, source_target_pairs={{0,3},{1,2},{2,1},{3,0},{4,7},{5,6},{6,5},{7,4},{8,11},{9,10},{10,... | collective-permute-start | bytes 221192 | tf_op jit(solution)/shard_map/ppermute | solution.py:236
  9.6 3.7 %collective-permute-start.4 = (f32[8,256]{1,0:T(8,128)S(1)}, f32[8,256]{1,0:T(8,128)S(1)}, u32[]{:S(2)}, u32[]{:S(2)}) collective-permute-start(f32[8,256]{1,0:T(8,128)S(1)} %get-tuple-element.87), channel_id=1, source_target_pairs={{0,8},{8,0},{16,24},{24,16},{1,9},{9,1},{17,25},{25,17},{2,10},{10... | collective-permute-start | bytes 24584 | tf_op jit(solution)/shard_map/ppermute | solution.py:236
  13.2 3.7 %collective-permute-start.5 = (f32[8,256]{1,0:T(8,128)S(1)}, f32[8,256]{1,0:T(8,128)S(1)}, u32[]{:S(2)}, u32[]{:S(2)}) collective-permute-start(f32[8,256]{1,0:T(8,128)S(1)} %add.24), channel_id=1, source_target_pairs={{0,16},{8,24},{16,0},{24,8},{1,17},{9,25},{17,1},{25,9},{2,18},{10... | collective-permute-start | bytes 24584 | tf_op jit(solution)/shard_map/ppermute | solution.py:236
  16.9 1.2 %collective-permute-start.6 = (f32[8,256]{1,0:T(8,128)S(1)}, f32[8,256]{1,0:T(8,128)S(1)}, u32[]{:S(2)}, u32[]{:S(2)}) collective-permute-start(f32[8,256]{1,0:T(8,128)S(1)} %add.25.refs_5_), channel_id=1, source_target_pairs={{0,4},{4,0},{1,5},{5,1},{2,6},{6,2},{3,7},{7,3},{8,12},{12,8},{9,1... | collective-permute-start | bytes 24584 | tf_op jit(solution)/shard_map/ppermute | solution.py:236
  18.1 9.2 %collective-permute-start.9 = (f32[72,256]{1,0:T(8,128)S(1)}, f32[72,256]{1,0:T(8,128)S(1)}, u32[]{:S(2)}, u32[]{:S(2)}) collective-permute-start(f32[72,256]{1,0:T(8,128)S(1)} %get-tuple-element.92.refs_0_), channel_id=1, source_target_pairs={{0,3},{1,2},{2,1},{3,0},{4,7},{5,6},{6,5},{7,4},{8,11},{9,10},{10,... | collective-permute-start | bytes 221192 | tf_op jit(solution)/shard_map/ppermute | solution.py:236
  22.0 5.9 %collective-permute-start.8 = (f32[72,256]{1,0:T(8,128)S(1)}, f32[72,256]{1,0:T(8,128)S(1)}, u32[]{:S(2)}, u32[]{:S(2)}) collective-permute-start(f32[72,256]{1,0:T(8,128)S(1)} %get-tuple-element.92.refs_0_), channel_id=1, source_target_pairs={{0,2},{1,3},{2,0},{3,1},{4,6},{5,7},{6,4},{7,5},{8,10},{9,11},{10,... | collective-permute-start | bytes 221192 | tf_op jit(solution)/shard_map/ppermute | solution.py:236
  22.0 6.0 %collective-permute-start.7 = (f32[72,256]{1,0:T(8,128)S(1)}, f32[72,256]{1,0:T(8,128)S(1)}, u32[]{:S(2)}, u32[]{:S(2)}) collective-permute-start(f32[72,256]{1,0:T(8,128)S(1)} %get-tuple-element.92.refs_0_), channel_id=1, source_target_pairs={{0,1},{1,0},{2,3},{3,2},{4,5},{5,4},{6,7},{7,6},{8,9},{9,8},{10,11... | collective-permute-start | bytes 221192 | tf_op jit(solution)/shard_map/ppermute | solution.py:236
  28.0 1.8 %collective-permute-start.11 = (f32[256,256]{1,0:T(8,128)S(1)}, f32[256,256]{1,0:T(8,128)S(1)}, u32[]{:S(2)}, u32[]{:S(2)}) collective-permute-start(f32[256,256]{1,0:T(8,128)S(1)} %get-tuple-element.96.own_ref), channel_id=1, source_target_pairs={{0,4},{4,0},{1,5},{5,1},{2,6},{6,2},{3,7},{7,3},{8,12},{12,8},{9,1... | collective-permute-start | bytes 786440 | tf_op jit(solution)/shard_map/ppermute | solution.py:236
  35.0 5.0 %collective-permute-start.15 = (f32[128,256]{1,0:T(8,128)S(1)}, f32[128,256]{1,0:T(8,128)S(1)}, u32[]{:S(2)}, u32[]{:S(2)}) collective-permute-start(f32[128,256]{1,0:T(8,128)S(1)} %get-tuple-element.118), channel_id=1, source_target_pairs={{0,8},{4,20},{8,0},{12,28},{16,24},{20,4},{24,16},{28,12},{1,9},{5... | collective-permute-start | bytes 393224 | tf_op jit(solution)/shard_map/ppermute | solution.py:254
  36.6 5.1 %collective-permute-start.12 = (f32[128,256]{1,0:T(8,128)S(1)}, f32[128,256]{1,0:T(8,128)S(1)}, u32[]{:S(2)}, u32[]{:S(2)}) collective-permute-start(f32[128,256]{1,0:T(8,128)S(1)} %get-tuple-element.107), channel_id=1, source_target_pairs={{0,8},{4,20},{8,0},{12,28},{16,24},{20,4},{24,16},{28,12},{1,9},{5... | collective-permute-start | bytes 393224 | tf_op jit(solution)/shard_map/ppermute | solution.py:254
  40.0 5.0 %collective-permute-start.16 = (f32[128,256]{1,0:T(8,128)S(1)}, f32[128,256]{1,0:T(8,128)S(1)}, u32[]{:S(2)}, u32[]{:S(2)}) collective-permute-start(f32[128,256]{1,0:T(8,128)S(1)} %add.28), channel_id=1, source_target_pairs={{0,16},{4,12},{8,24},{12,4},{16,0},{20,28},{24,8},{28,20},{1,17},{... | collective-permute-start | bytes 393224 | tf_op jit(solution)/shard_map/ppermute | solution.py:254
  41.8 5.0 %collective-permute-start.13 = (f32[128,256]{1,0:T(8,128)S(1)}, f32[128,256]{1,0:T(8,128)S(1)}, u32[]{:S(2)}, u32[]{:S(2)}) collective-permute-start(f32[128,256]{1,0:T(8,128)S(1)} %add.27.own_ref), channel_id=1, source_target_pairs={{0,16},{4,12},{8,24},{12,4},{16,0},{20,28},{24,8},{28,20},{1,17},{... | collective-permute-start | bytes 393224 | tf_op jit(solution)/shard_map/ppermute | solution.py:254
  45.1 3.5 %collective-permute-start.17 = (f32[128,256]{1,0:T(8,128)S(1)}, f32[128,256]{1,0:T(8,128)S(1)}, u32[]{:S(2)}, u32[]{:S(2)}) collective-permute-start(f32[128,256]{1,0:T(8,128)S(1)} %add.29), channel_id=1, source_target_pairs={{0,4},{4,0},{1,5},{5,1},{2,6},{6,2},{3,7},{7,3},{8,12},{12,8},{9,1... | collective-permute-start | bytes 393224 | tf_op jit(solution)/shard_map/ppermute | solution.py:236
  47.1 5.0 %collective-permute-start.14 = (f32[128,256]{1,0:T(8,128)S(1)}, f32[128,256]{1,0:T(8,128)S(1)}, u32[]{:S(2)}, u32[]{:S(2)}) collective-permute-start(f32[128,256]{1,0:T(8,128)S(1)} %get-tuple-element.116), channel_id=1, source_target_pairs={{0,1},{1,0},{2,3},{3,2},{4,5},{5,4},{6,7},{7,6},{8,9},{9,8},{10,11... | collective-permute-start | bytes 393224 | tf_op jit(solution)/shard_map/ppermute | solution.py:236
  52.1 8.3 %collective-permute-start.18 = (f32[128,256]{1,0:T(8,128)S(1)}, f32[128,256]{1,0:T(8,128)S(1)}, u32[]{:S(2)}, u32[]{:S(2)}) collective-permute-start(f32[128,256]{1,0:T(8,128)S(1)} %add.30), channel_id=1, source_target_pairs={{0,2},{1,3},{2,0},{3,1},{4,6},{5,7},{6,4},{7,5},{8,10},{9,11},{10,... | collective-permute-start | bytes 393224 | tf_op jit(solution)/shard_map/ppermute | solution.py:236
  53.8 8.9 %collective-permute-start.20 = (f32[128,256]{1,0:T(8,128)S(1)}, f32[128,256]{1,0:T(8,128)S(1)}, u32[]{:S(2)}, u32[]{:S(2)}) collective-permute-start(f32[128,256]{1,0:T(8,128)S(1)} %get-tuple-element.132.refs_2_), channel_id=1, source_target_pairs={{0,4},{4,0},{1,5},{5,1},{2,6},{6,2},{3,7},{7,3},{8,12},{12,8},{9,1... | collective-permute-start | bytes 393224 | tf_op jit(solution)/shard_map/ppermute | solution.py:236
  60.5 2.2 %collective-permute-start.19 = (f32[128,256]{1,0:T(8,128)S(1)}, f32[128,256]{1,0:T(8,128)S(1)}, u32[]{:S(2)}, u32[]{:S(2)}) collective-permute-start(f32[128,256]{1,0:T(8,128)S(1)} %add.31.refs_0_), channel_id=1, source_target_pairs={{0,4},{4,0},{1,5},{5,1},{2,6},{6,2},{3,7},{7,3},{8,12},{12,8},{9,1... | collective-permute-start | bytes 393224 | tf_op jit(solution)/shard_map/ppermute | solution.py:236
  63.9 6.2 %collective-permute-start.22 = (f32[1,256]{1,0:T(1,128)S(1)}, f32[1,256]{1,0:T(1,128)S(1)}, u32[]{:S(2)}, u32[]{:S(2)}) collective-permute-start(f32[1,256]{1,0:T(1,128)S(1)} %get-tuple-element.142.refs_0_), channel_id=1, source_target_pairs={{0,3},{1,2},{2,1},{3,0},{4,7},{5,6},{6,5},{7,4},{8,11},{9,10},{10,... | collective-permute-start | bytes 3080 | tf_op jit(solution)/shard_map/ppermute | solution.py:236
  66.2 3.9 %collective-permute-start.21 = (f32[1,256]{1,0:T(1,128)S(1)}, f32[1,256]{1,0:T(1,128)S(1)}, u32[]{:S(2)}, u32[]{:S(2)}) collective-permute-start(f32[1,256]{1,0:T(1,128)S(1)} %get-tuple-element.142.refs_0_), channel_id=1, source_target_pairs={{0,1},{4,6},{1,0},{5,7},{2,3},{6,4},{3,2},{7,5},{8,9},{12,14},{9,8... | collective-permute-start | bytes 3080 | tf_op jit(solution)/shard_map/ppermute | solution.py:557
  70.1 4.7 %collective-permute-start.23 = (f32[1,256]{1,0:T(1,128)S(1)}, f32[1,256]{1,0:T(1,128)S(1)}, u32[]{:S(2)}, u32[]{:S(2)}) collective-permute-start(f32[1,256]{1,0:T(1,128)S(1)} %collective-permute-done.21), channel_id=1, source_target_pairs={{0,4},{4,0},{1,5},{5,1},{2,6},{6,2},{3,7},{7,3},{8,12},{12,8},{9,1... | collective-permute-start | bytes 3080 | tf_op jit(solution)/shard_map/ppermute | solution.py:236

commit v5 on v4

--- a/solution.py
+++ b/solution.py
@@ -263,11 +263,19 @@
     return x
 
 
-def open_kernel(pick_ref, f_ref, b_ref, w_ref, give_ref, row_ref, f_out_ref, b_out_ref, w_out_ref):
+def core_rows(f_ref, core, week):
+    half = f_ref.shape[0] // 2
+    chunk = half // 4
+    at = [(0, week ^ (1 + core)), (1, week ^ (1 + core)), (core, week ^ 3), (core, week)]
+    return jnp.concatenate(
+        [f_ref[pl.ds(pl.multiple_of(h * half + q * chunk, chunk), chunk), :] for h, q in at], axis=0
+    )
+
+
+def open_kernel(core_ref, week_ref, f_ref, b_ref, w_ref, give_ref, row_ref, f_out_ref, b_out_ref, w_out_ref):
     f = f_ref[...]
     half = f.shape[0] // 2
-    at = pl.multiple_of(pick_ref[0] * half, half)
-    give_ref[:half, :] = dot(f_ref[pl.ds(at, half), :], b_ref[...] * w_ref[...])
+    give_ref[:half, :] = dot(core_rows(f_ref, 1 - core_ref[0], week_ref[0]), b_ref[...] * w_ref[...])
     row = lax.dot_general(
         jnp.ones((8, f.shape[1]), jnp.float32), f, (((1,), (1,)), ((), ())), precision=hp, preferred_element_type=jnp.float32
     )[:1]
@@ -281,11 +289,10 @@
     w_out_ref[...] = w_ref[...]
 
 
-def rest_kernel(pick_ref, f_ref, b_ref, w_ref, keep_ref, small_ref, gram_ref):
+def rest_kernel(core_ref, week_ref, f_ref, b_ref, w_ref, keep_ref, small_ref, gram_ref):
     b = b_ref[...]
-    half, cols = f_ref.shape[0] // 2, f_ref.shape[1]
-    at = pl.multiple_of(pick_ref[0] * half, half)
-    keep_ref[...] = dot(f_ref[pl.ds(at, half), :], b * w_ref[...])
+    cols = f_ref.shape[1]
+    keep_ref[...] = dot(core_rows(f_ref, core_ref[0], week_ref[0]), b * w_ref[...])
     col = jnp.sum(f_ref[...], axis=0, keepdims=True)
     small_ref[...] = jnp.zeros_like(small_ref)
     small_ref[0:1, :] = dot(jnp.broadcast_to(col, (8, cols)), b)[:1]
@@ -309,6 +316,67 @@
             give[chunk + 1 + n : chunk + 2 + n, :] = row[:, n * rank : (n + 1) * rank]
 
 
+def cut_pair_kernel(own_ref, got_ref, row_ref, w_ref, near_ref, far_ref, mine_ref):
+    half, rank = own_ref.shape
+    chunk = half // 4
+    row = row_ref[...] + jnp.concatenate(
+        [got_ref[half + n : half + n + 1, :] for n in range(row_ref.shape[1] // rank)], axis=1
+    )
+    x = own_ref[...] + got_ref[:half, :]
+    for out, part in ((near_ref, x[: 2 * chunk]), (far_ref, x[2 * chunk : 3 * chunk]), (mine_ref, x[3 * chunk :])):
+        m = part.shape[0]
+        out[:m, :] = part
+        out[m:, :] = jnp.zeros_like(out[m:, :])
+        out[m : m + 1, :] = w_ref[...]
+        for n in range(row_ref.shape[1] // rank):
+            out[m + 1 + n : m + 2 + n, :] = row[:, n * rank : (n + 1) * rank]
+
+
+def mix_kernel(near_ref, far_ref, mine_ref, out_ref):
+    chunk = mine_ref.shape[0] - 8
+    out_ref[: 2 * chunk, :] = near_ref[: 2 * chunk, :]
+    out_ref[2 * chunk : 3 * chunk, :] = far_ref[:chunk, :] + mine_ref[:chunk, :]
+    out_ref[3 * chunk :, :] = near_ref[2 * chunk :, :]
+
+
+def fold_pair_kernel(core_ref, mix_ref, side_ref, heads_ref, small_ref, w_ref, pair_ref, own_ref, col_ref):
+    chunk = own_ref.shape[0] - 8
+    core = core_ref[0]
+    for h in range(2):
+        own = mix_ref[2 * chunk : 3 * chunk, :]
+        other = side_ref[2 * chunk : 3 * chunk, :]
+        at = slice(h * chunk, (h + 1) * chunk)
+        pair_ref[at, :] = (mix_ref[at, :] + side_ref[at, :]) + jnp.where(core == h, own, other)
+    own_ref[:chunk, :] = pair_ref[pl.ds(pl.multiple_of(core * chunk, chunk), chunk), :]
+    grand = heads_ref[2:3, :]
+    for out in (pair_ref, own_ref):
+        m = out.shape[0] - 8
+        out[m:, :] = jnp.zeros_like(out[m:, :])
+        out[m : m + 1, :] = w_ref[...] * (heads_ref[0:1, :] / grand)
+    cols = col_ref.shape[1]
+    col_ref[...] = small_ref[1:2, :cols] / grand[:, :cols]
+
+
+def week_at(week, core, d):
+    if core is None:
+        return week ^ d
+    return week ^ (0, 1 + core, 2 - core, 3)[d]
+
+
+def rows_pair_kernel(core_ref, week_ref, pair_ref, near_ref, side_ref, far_ref, far_side_ref, m_ref, shift_ref):
+    chunk, half = far_ref.shape[0] - 8, m_ref.shape[0] // 2
+    shift_ref[...] = jnp.zeros_like(shift_ref)
+    for d, part in enumerate((pair_ref, near_ref, side_ref, far_ref)):
+        m = part.shape[0] - 8
+        shift_ref[pl.ds(week_at(week_ref[0], core_ref[0], d), 1), :] = part[m : m + 1, :]
+    for h in range(2):
+        for d, part in enumerate((pair_ref, near_ref, side_ref)):
+            at = pl.multiple_of(h * half + week_at(week_ref[0], core_ref[0], d) * chunk, chunk)
+            m_ref[pl.ds(at, chunk), :] = part[h * chunk : (h + 1) * chunk, :]
+        at = pl.multiple_of(h * half + week_at(week_ref[0], core_ref[0], 3) * chunk, chunk)
+        m_ref[pl.ds(at, chunk), :] = jnp.where(core_ref[0] == h, far_ref[:chunk, :], far_side_ref[:chunk, :])
+
+
 def fold_kernel(*refs):
     *parts, heads_ref, small_ref, w_ref, give_ref, col_ref = refs
     chunk = give_ref.shape[0] - 8
@@ -323,14 +391,14 @@
     col_ref[...] = small_ref[1:2, :cols] / grand[:, :cols]
 
 
-def first_kernel(me_ref, own_ref, other_ref, *refs):
+def first_kernel(paired, core_ref, week_ref, own_ref, other_ref, *refs):
     *parts, v_ref, gram_ref, row_ref, w_ref = refs
     rank = w_ref.shape[1]
     w_ref[...] = jnp.zeros_like(w_ref)
     row_ref[...] = jnp.zeros_like(row_ref)
     for d, part in enumerate(parts):
         chunk = part.shape[0] - 8
-        at = me_ref[0] ^ d
+        at = week_at(week_ref[0], core_ref[0] if paired else None, d)
         w_ref[pl.ds(at, 1), :] = part[chunk : chunk + 1, :]
         for n in range(row_ref.shape[1] // rank):
             row_ref[pl.ds(at, 1), n * rank : (n + 1) * rank] = part[chunk + 1 + n : chunk + 2 + n, :]
@@ -350,17 +418,14 @@
 
 
 def exporter_kernel(
-    me_ref, top_ref, own_ref, other_ref, row_all_ref, shift_ref, f_ref, col_ref, m_ref, t_ref, s_ref
+    me_ref, sum_ref, row_all_ref, shift_ref, f_ref, col_ref, m_ref, t_ref, s_ref
 ):
-    half = own_ref.shape[0]
-    m_ref[pl.ds(pl.multiple_of(top_ref[0] * half, half), half), :] = own_ref[...]
-    m_ref[pl.ds(pl.multiple_of((1 - top_ref[0]) * half, half), half), :] = other_ref[...]
     rank, cols = shift_ref.shape[1], f_ref.shape[1]
     s_ref[:, :rank] = shift_ref[...]
     week = lax.broadcasted_iota(jnp.int32, (s_ref.shape[0], cols), 0)
     s_ref[:, rank:] = jnp.where(week == me_ref[0], col_ref[...], 0.0)
     terms = outer(row_all_ref[...], s_ref[...])
-    m = m_ref[...] - terms[:, :rank]
+    m = sum_ref[...] - terms[:, :rank]
     m_ref[...] = m
     t_ref[...] = outer(f_ref[...] - terms[:, rank:], m)
 
@@ -424,22 +489,25 @@
     o_ref[...] = raw[:1] / scale
 
 
+def shares_pair(f, b, w, core, week):
+    rows, rank = f.shape[0], w.shape[1]
+    give, row, f, b, w = pl.pallas_call(
+        open_kernel,
+        out_shape=[
+            pltpu.VMEM(s, jnp.float32) for s in ((rows // 2 + 8, rank), (1, rows), f.shape, b.shape, w.shape)
+        ],
+        in_specs=[pl.BlockSpec(memory_space=pltpu.SMEM)] * 2 + [pl.BlockSpec(memory_space=pltpu.VMEM)] * 3,
+        out_specs=[pl.BlockSpec(memory_space=pltpu.VMEM)] * 5,
+        name="open",
+    )(core, week, f, b, w)
+    got = swap(give, "imp", 1)
+    keep, small, gram = call(rest_kernel, [(rows // 2, rank), (8, rank), (rank, rank)], core, week, f, b, w, smem=2)
+    other = swap(gram, "imp", 1)
+    return f, w, keep, got, row, small, gram, other
+
+
 def shares(f, b, w, top, ni):
     rows, rank = f.shape[0], w.shape[1]
-    if ni == 2 and rows % rank == 0 and rows // rank <= 7:
-        give, row, f, b, w = pl.pallas_call(
-            open_kernel,
-            out_shape=[
-                pltpu.VMEM(s, jnp.float32) for s in ((rows // 2 + 8, rank), (1, rows), f.shape, b.shape, w.shape)
-            ],
-            in_specs=[pl.BlockSpec(memory_space=pltpu.SMEM)] + [pl.BlockSpec(memory_space=pltpu.VMEM)] * 3,
-            out_specs=[pl.BlockSpec(memory_space=pltpu.VMEM)] * 5,
-            name="open",
-        )(1 - top, f, b, w)
-        got = swap(give, "imp", 1)
-        keep, small, gram = call(rest_kernel, [(rows // 2, rank), (8, rank), (rank, rank)], top, f, b, w, smem=1)
-        other = swap(gram, "imp", 1)
-        return f, w, keep, got, row, small, gram, other
     low = bits("imp")[:-1]
     sums = jnp.sum(f, 1)[None]
     part = jnp.concatenate([dot(f, b * w).reshape(2, rows // 2, rank), jnp.zeros((2, 8, rank))], axis=1)
@@ -464,37 +532,87 @@
     top = jnp.where((lax.axis_index("imp") & (ni // 2)) != 0, 1, 0).astype(jnp.int32)[None]
     steps = rank // block
 
-    f, w, keep, got, row, small, gram_own, gram_other = shares(f, importer_factor, w, top, ni)
+    chunk = rows // 2 // weeks
+    paired = ni == 2 and weeks == 4 and rows % rank == 0 and rows // rank <= 7 and chunk % 8 == 0
+    tall = -(-weeks // 8) * 8
+    if paired:
+        f, w, keep, got, row, small, gram_own, gram_other = shares_pair(f, importer_factor, w, top, me_k)
+    else:
+        f, w, keep, got, row, small, gram_own, gram_other = shares(f, importer_factor, w, top, ni)
     small = small + swap(small, "exp", 1)
 
-    chunk = keep.shape[0] // weeks
-    gives = call(cut_kernel, [(chunk + 8, rank)] * weeks, me_k, keep, got, row, w, smem=1)
-    got = [swap(g, "wk", d) if d else g for d, g in enumerate(gives)]
+    def near_weeks(x):
+        pairs = [(j * 4 + k, j * 4 + (k ^ (1 + j))) for k in range(4) for j in range(2)]
+        return lax.ppermute(x, ("imp", "wk"), pairs)
+
+    if paired:
+        give_near, give_far, mine = call(
+            cut_pair_kernel, [(2 * chunk + 8, rank), (chunk + 8, rank), (chunk + 8, rank)], keep, got, row, w
+        )
+        got_far = swap(give_far, "wk", 3)
+        got_near = near_weeks(give_near)
+    else:
+        gives = call(cut_kernel, [(chunk + 8, rank)] * weeks, me_k, keep, got, row, w, smem=1)
+        got = [swap(g, "wk", d) if d else g for d, g in enumerate(gives)]
     for bit in bits("exp")[1:]:
         small = small + swap(small, "exp", bit)
     heads = total(small, "imp")
-    give, col_mean = call(fold_kernel, [(chunk + 8, rank), (1, cols)], *got, heads, small, w)
-    gathered = [swap(give, "wk", d) if d else give for d in range(weeks)]
+    if paired:
+        got_near, got_far, heads = lax.optimization_barrier((got_near, got_far, heads))
+        mix = call(mix_kernel, (3 * chunk + 8, rank), got_near, got_far, mine)
+        side_mix = swap(mix, "imp", 1)
+        got = [mine, mix, side_mix, got_far]
+        pair, give, col_mean = call(
+            fold_pair_kernel,
+            [(2 * chunk + 8, rank), (chunk + 8, rank), (1, cols)],
+            top, mix, side_mix, heads, small, w,
+            smem=1,
+        )
+        far = swap(give, "wk", 3)
+        near_rows = near_weeks(pair)
+        gathered = [near_rows, far]
+    else:
+        give, col_mean = call(fold_kernel, [(chunk + 8, rank), (1, cols)], *got, heads, small, w)
+        gathered = [swap(give, "wk", d) if d else give for d in range(weeks)]
+
+    def first(*refs):
+        first_kernel(paired, *refs)
 
     state, gram_c, row_all = call(
-        first_kernel,
-        [(rank, rank), (rank, rank), (-(-weeks // 8) * 8, rows)],
-        me_k, after(gram_own, give), gram_other, *got,
-        smem=1, scratch=[pltpu.VMEM((-(-weeks // 8) * 8, rank), jnp.float32)],
+        first,
+        [(rank, rank), (rank, rank), (tall, rows)],
+        top, me_k, after(gram_own, give), gram_other, *got,
+        smem=2, scratch=[pltpu.VMEM((tall, rank), jnp.float32)],
     )
     state = inverse_piece([state], 0, steps // 2)
-    gathered, state = lax.optimization_barrier((gathered, state))
-    m_rows, shifts = call(rows_kernel, [(chunk * weeks, rank), (-(-weeks // 8) * 8, rank)], me_k, *gathered, smem=1)
-    m_other = swap(m_rows, "imp", ni // 2)
-    state = inverse_piece(after(state, m_rows), steps // 2, steps * 3 // 4)
-    m_other, state = lax.optimization_barrier((m_other, state))
+    if paired:
+        cut = steps
+        state = inverse_piece(state, steps // 2, steps * 7 // 8)
+        near_rows, far, state = lax.optimization_barrier((*gathered, state))
+        near_side, far_side = swap(near_rows, "imp", 1), swap(far, "imp", 1)
+        state = inverse_piece(after(state, near_rows), steps * 7 // 8, steps)
+        near_side, far_side, state = lax.optimization_barrier((near_side, far_side, state))
+        m_rows, shifts = call(
+            rows_pair_kernel, [(rows, rank), (tall, rank)],
+            top, me_k, pair, near_rows, near_side, far, far_side,
+            smem=2,
+        )
+    else:
+        cut = steps * 3 // 4
+        gathered, state = lax.optimization_barrier((gathered, state))
+        m_rows, shifts = call(rows_kernel, [(chunk * weeks, rank), (tall, rank)], me_k, *gathered, smem=1)
+        m_other = swap(m_rows, "imp", ni // 2)
+        state = inverse_piece(after(state, m_rows), steps // 2, cut)
+        m_other, state = lax.optimization_barrier((m_other, state))
+        upper = top[0] != 0
+        m_rows = jnp.concatenate([jnp.where(upper, m_other, m_rows), jnp.where(upper, m_rows, m_other)], axis=0)
     m_a, t = call(
         exporter_kernel,
         [(rows, rank), (cols, rank)],
-        me_k, top, m_rows, m_other, row_all, shifts, f, col_mean,
-        smem=2, scratch=[pltpu.VMEM((-(-weeks // 8) * 8, rank + cols), jnp.float32)],
+        me_k, m_rows, row_all, shifts, f, col_mean,
+        smem=1, scratch=[pltpu.VMEM((tall, rank + cols), jnp.float32)],
     )
-    (inv_a,) = inverse_piece(after(state, t), steps * 3 // 4, steps)
+    (inv_a,) = inverse_piece(after(state, t), cut, steps) if cut < steps else state
     grams = rank // 2 if ni == 2 and rank % 256 == 0 else rank
     raw_a, g_a = call(raw_kernel, [(rows, rank), (grams, rank)], top, m_a, inv_a, smem=1)
 
@@ -510,26 +628,21 @@
     g_a = gather_rows(g_a, "imp") if grams < rank else g_a
 
     def second(*refs):
-        second_kernel(rows * ne, steps // 2, *refs)
-
+        second_kernel(rows * ne, 1, *refs)
+
+    v, gram_a, scale_a, *state = call(second, [(rank, rank), (rank, rank), (1, rank)] + held, after(g_a, m_own), gram_c)
     for bit in bits("wk")[1:]:
-        m_got, g_a = lax.optimization_barrier((m_got, g_a))
+        m_got, v = lax.optimization_barrier((m_got, v))
         m_own = m_own + m_got
         m_got = swap(m_own, "wk", bit)
-    state, gram_a, scale_a = call(
-        second,
-        [(rank, rank), (rank, rank), (1, rank)],
-        after(g_a, m_own), gram_c,
-        scratch=[pltpu.VMEM(x, jnp.float32) for x in held],
-    )
-    paired = weeks == 4 and ni == 2
+    state = [after(v, m_own), *state]
     if ni == 2:
         t_side = swap(t, "imp", 1)
-        state, fac_a = inverse_piece([state], steps // 2, steps - 1, unit=(raw_a, scale_a))
-        m_got, state = lax.optimization_barrier((m_got, state))
+        state, fac_a = inverse_piece(state, 1, steps - 1, unit=(raw_a, scale_a))
+        m_got, *state = lax.optimization_barrier((m_got, *state))
         m_b = m_own + m_got
         m_side = swap(m_b, "imp", 1)
-        (inv_b,) = inverse_piece(after(state, m_b), steps - 1, steps)
+        (inv_b,) = inverse_piece([after(state[0], m_b), *state[1:]], steps - 1, steps)
 
         def both(*refs):
             both_kernel(cols * ni, *refs)
@@ -540,7 +653,7 @@
             m_b, m_side, t, t_side, scale_a, inv_b, gram_a,
         )
     else:
-        (inv_b,), fac_a = inverse_piece([state], steps // 2, steps, unit=(raw_a, scale_a))
+        (inv_b,), fac_a = inverse_piece(state, 1, steps, unit=(raw_a, scale_a))
         raw_b, both = call(importer_kernel, [(cols, rank), (rank + 8, rank)], m_own, m_got, scale_a, inv_b, t)
         for bit in bits("imp")[:-1]:
             both = both + swap(both, "imp", bit)
@@ -552,9 +665,8 @@
 
         state, scale_b = call(third, [(rank, rank), (1, rank)], both, got, gram_a)
     if paired:
-        pairs = [(j * 4 + k, j * 4 + (k ^ (1 + j))) for k in range(4) for j in range(2)]
         far_row = swap(m_mine, "wk", 3)
-        near_row = lax.ppermute(m_mine, ("imp", "wk"), pairs)
+        near_row = near_weeks(m_mine)
     else:
         m_all = [m_mine] + [swap(m_mine, "wk", d) for d in range(1, weeks)]
     state = inverse_piece([state], 0, steps // 2)

time: 75.8 us -> 73.9 us (0.975)
  starting transfers between devices: 26.4 us -> 23.3 us
  waiting for transfers between devices: 16 us -> 17 us
    ppermute x19 -> x17, starting transfers between devices: 21.1 us -> 12.8 us  [swap(): return lax.ppermute(x, axis, [(i, i ^ bit) for i in range(n)])]
    ppermute x1 -> x3, starting transfers between devices: 0.01 us -> 5.38 us  [near_weeks(): return lax.ppermute(x, ('imp', 'wk'), pairs)]
    pallas_call x7, Pallas kernels: 20 us -> 23.1 us  [inverse_piece(): pl.pallas_call(kernel, out_shape=shapes, in_specs=[vmem] * len(args), out...]
    pallas_call x11 -> x12, Pallas kernels: 10.1 us -> 7.15 us  [call(): pl.pallas_call(kernel, out_shape=shapes if many else shapes[0], in_specs=...]
    ppermute x19 -> x17, waiting for transfers between devices: 9.54 us -> 10.5 us  [swap(): return lax.ppermute(x, axis, [(i, i ^ bit) for i in range(n)])]
  transfers between devices with their start and end apart: 24 -> 24, of which waited for: 10 -> 10; matrix products, arithmetic and copies ran while one was open for 0% -> 0% of each run, Pallas kernels for 31% -> 35%
where the time goes in v5:
time: 73.9 us; the launch traced here: 73.7 us
  Pallas kernels  31.8 us (43%)
  starting transfers between devices  23.3 us (32%)
  waiting for transfers between devices  17 us (23%)
  between operations  0.89 us (1%)
    pallas_call x7, Pallas kernels, inverse_piece(): pl.pallas_call(kernel, out_shape=shapes, in_specs=[vmem] * len(args), out...  23.1 us
    ppermute x17, starting transfers between devices, swap(): return lax.ppermute(x, axis, [(i, i ^ bit) for i in range(n)])  12.8 us
    ppermute x17, waiting for transfers between devices, swap(): return lax.ppermute(x, axis, [(i, i ^ bit) for i in range(n)])  10.5 us
    pallas_call x12, Pallas kernels, call(): pl.pallas_call(kernel, out_shape=shapes if many else shapes[0], in_specs=...  7.15 us
    ppermute x4, waiting for transfers between devices, crossed(): return lax.ppermute(x, (axis, side), pairs)  6.41 us
    ppermute x3, starting transfers between devices, near_weeks(): return lax.ppermute(x, ('imp', 'wk'), pairs)  5.38 us
    ppermute x4, starting transfers between devices, crossed(): return lax.ppermute(x, (axis, side), pairs)  5.14 us
    pallas_call x1, Pallas kernels, shares_pair(): pl.pallas_call(open_kernel, out_shape=[pltpu.VMEM(s, jnp.float32) for s i...  1.58 us
  transfers between devices with their start and end apart: 24, of which 10 were waited for; matrix products, arithmetic and copies ran while one was open for 0% of the time, Pallas kernels for 35%

profile of v5, /device:TPU:0, one launch (start us, length us, event | category | flops | bytes accessed | tf_op | source)
XLA Modules:
  0.0 73.7 jit_solution(1154147282154144597)
XLA Ops:
  0.6 1.6 %open.1 = (f32[264,256]{1,0:T(8,128)S(1)}, f32[1,512]{1,0:T(1,128)S(1)}, f32[512,128]{1,0:T(8,128)S(1)}, f32[128,256]{1,0:T(8,128)S(1)}, f32[1,256]{1,0:T(1,128)S(1)}) custom-call(s32[1]{0:T(128)} %bitcast.1.core_ref.refs_0_.top_ref, s32[1]{0:T(128)} %bitcast.week_ref.refs_1_.me_ref, f32[512,128]{1,0:T(8,128)} %bitcast.3, f32[128,256]{1,0:T(8,128)} %b_ref.1, ...), custom_call_target="tpu_custom_call" | custom-call | tf_op jit(solution)/shard_map/open/pallas_call | solution.py:494
  2.2 0.6 collective-permute-start
  2.8 0.7 shard_map.58
  3.5 0.5 collective-permute-done.got_ref
  4.0 3.0 %collective-permute-start.1 = (f32[136,256]{1,0:T(8,128)S(1)}, f32[136,256]{1,0:T(8,128)S(1)}, u32[]{:S(2)}, u32[]{:S(2)}) collective-permute-start(f32[136,256]{1,0:T(8,128)S(1)} %get-tuple-element.85), channel_id=1, source_target_pairs={{0,1},{4,6},{1,0},{5,7},{2,3},{6,4},{3,2},{7,5},{8,9},{12,14},{9,8... | collective-permute-start | bytes 417800 | tf_op jit(solution)/shard_map/ppermute | solution.py:546
  7.0 2.5 %collective-permute-start.2 = (f32[72,256]{1,0:T(8,128)S(1)}, f32[72,256]{1,0:T(8,128)S(1)}, u32[]{:S(2)}, u32[]{:S(2)}) collective-permute-start(f32[72,256]{1,0:T(8,128)S(1)} %get-tuple-element.86), channel_id=1, source_target_pairs={{0,3},{1,2},{2,1},{3,0},{4,7},{5,6},{6,5},{7,4},{8,11},{9,10},{10,... | collective-permute-start | bytes 221192 | tf_op jit(solution)/shard_map/ppermute | solution.py:236
  9.5 1.5 %collective-permute-start.3 = (f32[8,256]{1,0:T(8,128)S(1)}, f32[8,256]{1,0:T(8,128)S(1)}, u32[]{:S(2)}, u32[]{:S(2)}) collective-permute-start(f32[8,256]{1,0:T(8,128)S(1)} %get-tuple-element.87), channel_id=1, source_target_pairs={{0,8},{8,0},{16,24},{24,16},{1,9},{9,1},{17,25},{25,17},{2,10},{10... | collective-permute-start | bytes 24584 | tf_op jit(solution)/shard_map/ppermute | solution.py:236
  11.0 2.2 %collective-permute-done.3 = f32[8,256]{1,0:T(8,128)S(1)} collective-permute-done((f32[8,256]{1,0:T(8,128)S(1)}, f32[8,256]{1,0:T(8,128)S(1)}, u32[]{:S(2)}, u32[]{:S(2)}) %collective-permute-start.3) | collective-permute-done | bytes 8224 | tf_op jit(solution)/shard_map/ppermute | solution.py:236
  13.1 1.5 %collective-permute-start.4 = (f32[8,256]{1,0:T(8,128)S(1)}, f32[8,256]{1,0:T(8,128)S(1)}, u32[]{:S(2)}, u32[]{:S(2)}) collective-permute-start(f32[8,256]{1,0:T(8,128)S(1)} %add.24), channel_id=1, source_target_pairs={{0,16},{8,24},{16,0},{24,8},{1,17},{9,25},{17,1},{25,9},{2,18},{10... | collective-permute-start | bytes 24584 | tf_op jit(solution)/shard_map/ppermute | solution.py:236
  14.7 2.1 %collective-permute-done.4 = f32[8,256]{1,0:T(8,128)S(1)} collective-permute-done((f32[8,256]{1,0:T(8,128)S(1)}, f32[8,256]{1,0:T(8,128)S(1)}, u32[]{:S(2)}, u32[]{:S(2)}) %collective-permute-start.4) | collective-permute-done | bytes 8224 | tf_op jit(solution)/shard_map/ppermute | solution.py:236
  16.8 0.0 collective-permute-start.5
  16.8 1.2 %collective-permute-done.5 = f32[8,256]{1,0:T(8,128)S(1)} collective-permute-done((f32[8,256]{1,0:T(8,128)S(1)}, f32[8,256]{1,0:T(8,128)S(1)}, u32[]{:S(2)}, u32[]{:S(2)}) %collective-permute-start.5) | collective-permute-done | bytes 8224 | tf_op jit(solution)/shard_map/ppermute | solution.py:236
  18.0 0.0 collective-permute-done.2.far_ref.refs_7_
  18.0 0.0 collective-permute-done.1.near_ref
  18.0 0.2 collective-permute-start.6
  18.2 0.3 collective-permute-start.9
  18.6 0.9 %collective-permute-done.6.side_ref.refs_6_ = f32[200,256]{1,0:T(8,128)S(1)} collective-permute-done((f32[200,256]{1,0:T(8,128)S(1)}, f32[200,256]{1,0:T(8,128)S(1)}, u32[]{:S(2)}, u32[]{:S(2)}) %collective-permute-start.6) | collective-permute-done | bytes 204832 | tf_op jit(solution)/shard_map/ppermute | solution.py:236
  19.6 0.7 %collective-permute-start.7 = (f32[136,256]{1,0:T(8,128)S(1)}, f32[136,256]{1,0:T(8,128)S(1)}, u32[]{:S(2)}, u32[]{:S(2)}) collective-permute-start(f32[136,256]{1,0:T(8,128)S(1)} %get-tuple-element.92.pair_ref), channel_id=1, source_target_pairs={{0,1},{4,6},{1,0},{5,7},{2,3},{6,4},{3,2},{7,5},{8,9},{12,14},{9,8... | collective-permute-start | bytes 417800 | tf_op jit(solution)/shard_map/ppermute | solution.py:546
  20.3 0.9 %collective-permute-start.8 = (f32[72,256]{1,0:T(8,128)S(1)}, f32[72,256]{1,0:T(8,128)S(1)}, u32[]{:S(2)}, u32[]{:S(2)}) collective-permute-start(f32[72,256]{1,0:T(8,128)S(1)} %get-tuple-element.93), channel_id=1, source_target_pairs={{0,3},{1,2},{2,1},{3,0},{4,7},{5,6},{6,5},{7,4},{8,11},{9,10},{10,... | collective-permute-start | bytes 221192 | tf_op jit(solution)/shard_map/ppermute | solution.py:236
  21.2 0.0 collective-permute-done.9.refs_3_
  21.2 0.5 shard_map.62
  21.8 4.1 %inverse.7.refs_0_ = f32[256,256]{1,0:T(8,128)S(1)} custom-call(f32[256,256]{1,0:T(8,128)S(1)} %get-tuple-element.96.refs_0_), custom_call_target="tpu_custom_call" | custom-call | tf_op jit(solution)/shard_map/inverse/pallas_call | solution.py:201
  25.9 2.5 %inverse.8 = (f32[256,256]{1,0:T(8,128)S(1)}, f32[64,128]{1,0:T(8,128)S(1)}, f32[32,128]{1,0:T(8,128)S(1)}, f32[32,128]{1,0:T(8,128)S(1)}) custom-call(f32[256,256]{1,0:T(8,128)S(1)} %inverse.7.refs_0_), custom_call_target="tpu_custom_call" | custom-call | tf_op jit(solution)/shard_map/inverse/pallas_call | solution.py:201
  28.3 0.0 collective-permute-done.8.far_ref
  28.3 0.0 collective-permute-done.7.near_ref
  28.3 1.1 %collective-permute-start.10 = (f32[136,256]{1,0:T(8,128)S(1)}, f32[136,256]{1,0:T(8,128)S(1)}, u32[]{:S(2)}, u32[]{:S(2)}) collective-permute-start(f32[136,256]{1,0:T(8,128)S(1)} %collective-permute-done.7.near_ref), channel_id=1, source_target_pairs={{0,4},{4,0},{1,5},{5,1},{2,6},{6,2},{3,7},{7,3},{8,12},{12,8},{9,1... | collective-permute-start | bytes 417800 | tf_op jit(solution)/shard_map/ppermute | solution.py:236
  29.5 0.1 collective-permute-start.11
  29.5 1.6 %inverse.9.inv_ref = f32[256,256]{1,0:T(8,128)S(1)} custom-call(f32[256,256]{1,0:T(8,128)S(1)} %get-tuple-element.107.refs_0_, f32[64,128]{1,0:T(8,128)S(1)} %get-tuple-element.108.refs_1_, f32[32,128]{1,0:T(8,128)S(1)} %get-tuple-element.109.refs_2_, f32[32,128]{1,0:T(8,128)S(1)} %get-tuple-element.110.refs_3_), custom_call_target="tpu_custom_call" | custom-call | tf_op jit(solution)/shard_map/inverse/pallas_call | solution.py:201
  31.1 0.0 collective-permute-done.11.far_side_ref
  31.1 0.0 collective-permute-done.10.side_ref
  31.2 1.5 %shard_map.64 = (f32[512,256]{1,0:T(8,128)S(1)}, f32[128,256]{1,0:T(8,128)S(1)}) custom-call(s32[1]{0:T(128)} %bitcast.week_ref.refs_1_.me_ref, f32[512,256]{1,0:T(8,128)S(1)} %get-tuple-element.113.sum_ref, f32[8,512]{1,0:T(8,128)S(1)} %get-tuple-element.114.row_all_ref, f32[8,256]{1,0:T(8,128)S(1)} %get-tuple-element.115.shift_ref, ...), custom_call_target="tpu_custom_call" | custom-call | tf_op jit(solution)/shard_map/pallas_call | solution.py:160
  32.7 1.4 %shard_map.66 = (f32[512,256]{1,0:T(8,128)S(1)}, f32[128,256]{1,0:T(8,128)S(1)}) custom-call(s32[1]{0:T(128)} %bitcast.1.core_ref.refs_0_.top_ref, f32[512,256]{1,0:T(8,128)S(1)} %get-tuple-element.120.m_ref, f32[256,256]{1,0:T(8,128)S(1)} %inverse.9.inv_ref), custom_call_target="tpu_custom_call" | custom-call | tf_op jit(solution)/shard_map/pallas_call | solution.py:160
  34.1 1.6 %collective-permute-start.15 = (f32[128,256]{1,0:T(8,128)S(1)}, f32[128,256]{1,0:T(8,128)S(1)}, u32[]{:S(2)}, u32[]{:S(2)}) collective-permute-start(f32[128,256]{1,0:T(8,128)S(1)} %get-tuple-element.121), channel_id=1, source_target_pairs={{0,8},{4,20},{8,0},{12,28},{16,24},{20,4},{24,16},{28,12},{1,9},{5... | collective-permute-start | bytes 393224 | tf_op jit(solution)/shard_map/ppermute | solution.py:254
  35.6 0.5 collective-permute-start.12
  36.2 2.9 %collective-permute-done.15 = f32[128,256]{1,0:T(8,128)S(1)} collective-permute-done((f32[128,256]{1,0:T(8,128)S(1)}, f32[128,256]{1,0:T(8,128)S(1)}, u32[]{:S(2)}, u32[]{:S(2)}) %collective-permute-start.15) | collective-permute-done | bytes 131104 | tf_op jit(solution)/shard_map/ppermute | solution.py:254
  39.1 1.6 %collective-permute-start.16 = (f32[128,256]{1,0:T(8,128)S(1)}, f32[128,256]{1,0:T(8,128)S(1)}, u32[]{:S(2)}, u32[]{:S(2)}) collective-permute-start(f32[128,256]{1,0:T(8,128)S(1)} %add.28), channel_id=1, source_target_pairs={{0,16},{4,12},{8,24},{12,4},{16,0},{20,28},{24,8},{28,20},{1,17},{... | collective-permute-start | bytes 393224 | tf_op jit(solution)/shard_map/ppermute | solution.py:254
  40.7 0.0 collective-permute-done.12
  40.7 1.5 %collective-permute-start.13 = (f32[128,256]{1,0:T(8,128)S(1)}, f32[128,256]{1,0:T(8,128)S(1)}, u32[]{:S(2)}, u32[]{:S(2)}) collective-permute-start(f32[128,256]{1,0:T(8,128)S(1)} %add.27.own_ref), channel_id=1, source_target_pairs={{0,16},{4,12},{8,24},{12,4},{16,0},{20,28},{24,8},{28,20},{1,17},{... | collective-permute-start | bytes 393224 | tf_op jit(solution)/shard_map/ppermute | solution.py:254
  42.2 2.0 %collective-permute-done.16 = f32[128,256]{1,0:T(8,128)S(1)} collective-permute-done((f32[128,256]{1,0:T(8,128)S(1)}, f32[128,256]{1,0:T(8,128)S(1)}, u32[]{:S(2)}, u32[]{:S(2)}) %collective-permute-start.16) | collective-permute-done | bytes 131104 | tf_op jit(solution)/shard_map/ppermute | solution.py:254
  44.2 0.1 collective-permute-start.17
  44.3 1.5 %collective-permute-done.13.other_ref = f32[128,256]{1,0:T(8,128)S(1)} collective-permute-done((f32[128,256]{1,0:T(8,128)S(1)}, f32[128,256]{1,0:T(8,128)S(1)}, u32[]{:S(2)}, u32[]{:S(2)}) %collective-permute-start.13) | collective-permute-done | bytes 131104 | tf_op jit(solution)/shard_map/ppermute | solution.py:254
  45.8 0.3 shard_map.65
  46.1 0.5 collective-permute-start.14
  46.6 0.0 collective-permute-done.17
  46.6 1.1 %shard_map.67 = (f32[256,256]{1,0:T(8,128)S(1)}, f32[256,256]{1,0:T(8,128)S(1)}, f32[1,256]{1,0:T(1,128)S(1)}, f32[64,128]{1,0:T(8,128)S(1)}, f32[32,128]{1,0:T(8,128)S(1)}, /*index=5*/f32[32,128]{1,0:T(8,128)S(1)}) custom-call(f32[256,256]{1,0:T(8,128)S(1)} %pad_maximum_fusion.refs_0_, f32[256,256]{1,0:T(8,128)S(1)} %get-tuple-element.123.refs_1_), custom_call_target="tpu_custom_call" | custom-call | tf_op jit(solution)/shard_map/pallas_call | solution.py:160
  47.8 3.3 %collective-permute-done.14 = f32[128,256]{1,0:T(8,128)S(1)} collective-permute-done((f32[128,256]{1,0:T(8,128)S(1)}, f32[128,256]{1,0:T(8,128)S(1)}, u32[]{:S(2)}, u32[]{:S(2)}) %collective-permute-start.14) | collective-permute-done | bytes 131104 | tf_op jit(solution)/shard_map/ppermute | solution.py:236
  51.1 1.3 %collective-permute-start.18 = (f32[128,256]{1,0:T(8,128)S(1)}, f32[128,256]{1,0:T(8,128)S(1)}, u32[]{:S(2)}, u32[]{:S(2)}) collective-permute-start(f32[128,256]{1,0:T(8,128)S(1)} %add.30), channel_id=1, source_target_pairs={{0,2},{1,3},{2,0},{3,1},{4,6},{5,7},{6,4},{7,5},{8,10},{9,11},{10,... | collective-permute-start | bytes 393224 | tf_op jit(solution)/shard_map/ppermute | solution.py:236
  52.5 0.0 collective-permute-start.20
  52.5 5.6 %inverse.10 = (f32[256,256]{1,0:T(8,128)S(1)}, f32[64,128]{1,0:T(8,128)S(1)}, f32[32,128]{1,0:T(8,128)S(1)}, f32[32,128]{1,0:T(8,128)S(1)}, f32[512,256]{1,0:T(8,128)}) custom-call(f32[256,256]{1,0:T(8,128)S(1)} %get-tuple-element.127.refs_0_, f32[64,128]{1,0:T(8,128)S(1)} %get-tuple-element.128.refs_1_, f32[32,128]{1,0:T(8,128)S(1)} %get-tuple-element.129.refs_2_, ...), custom_call_target="tpu_custom_call" | custom-call | tf_op jit(solution)/shard_map/inverse/pallas_call | solution.py:201
  58.0 0.3 collective-permute-done.18
  58.4 0.3 collective-permute-start.19
  58.6 1.6 %inverse.11.refs_5_ = f32[256,256]{1,0:T(8,128)S(1)} custom-call(f32[256,256]{1,0:T(8,128)S(1)} %get-tuple-element.141.refs_0_, f32[64,128]{1,0:T(8,128)S(1)} %get-tuple-element.142.refs_1_, f32[32,128]{1,0:T(8,128)S(1)} %get-tuple-element.143.refs_2_, f32[32,128]{1,0:T(8,128)S(1)} %get-tuple-element.144.refs_3_), custom_call_target="tpu_custom_call" | custom-call | tf_op jit(solution)/shard_map/inverse/pallas_call | solution.py:201
  60.2 0.0 collective-permute-done.20.refs_3_
  60.2 0.0 collective-permute-done.19.refs_1_
  60.2 1.2 %shard_map.68 = (f32[128,256]{1,0:T(8,128)S(1)}, f32[1,256]{1,0:T(1,128)S(1)}, f32[256,256]{1,0:T(8,128)S(1)}, f32[1,256]{1,0:T(1,128)S(1)}) custom-call(f32[128,256]{1,0:T(8,128)S(1)} %add.31.refs_0_, f32[128,256]{1,0:T(8,128)S(1)} %collective-permute-done.19.refs_1_, f32[128,256]{1,0:T(8,128)S(1)} %get-tuple-element.139.refs_2_, ...), custom_call_target="tpu_custom_call" | custom-call | tf_op jit(solution)/shard_map/pallas_call | solution.py:160
  61.5 1.6 %collective-permute-start.21 = (f32[1,256]{1,0:T(1,128)S(1)}, f32[1,256]{1,0:T(1,128)S(1)}, u32[]{:S(2)}, u32[]{:S(2)}) collective-permute-start(f32[1,256]{1,0:T(1,128)S(1)} %get-tuple-element.146.refs_0_), channel_id=1, source_target_pairs={{0,1},{4,6},{1,0},{5,7},{2,3},{6,4},{3,2},{7,5},{8,9},{12,14},{9,8... | collective-permute-start | bytes 3080 | tf_op jit(solution)/shard_map/ppermute | solution.py:546
  63.1 1.5 %collective-permute-start.22 = (f32[1,256]{1,0:T(1,128)S(1)}, f32[1,256]{1,0:T(1,128)S(1)}, u32[]{:S(2)}, u32[]{:S(2)}) collective-permute-start(f32[1,256]{1,0:T(1,128)S(1)} %get-tuple-element.146.refs_0_), channel_id=1, source_target_pairs={{0,3},{1,2},{2,1},{3,0},{4,7},{5,6},{6,5},{7,4},{8,11},{9,10},{10,... | collective-permute-start | bytes 3080 | tf_op jit(solution)/shard_map/ppermute | solution.py:236
  64.6 3.9 %inverse.12.refs_0_ = f32[256,256]{1,0:T(8,128)S(1)} custom-call(f32[256,256]{1,0:T(8,128)S(1)} %get-tuple-element.147.refs_0_), custom_call_target="tpu_custom_call" | custom-call | tf_op jit(solution)/shard_map/inverse/pallas_call | solution.py:201
  68.6 0.0 collective-permute-done.21
  68.6 0.0 collective-permute-done.22.refs_3_
  68.6 0.3 collective-permute-start.23
  68.9 3.9 %inverse.13 = (f32[256,256]{1,0:T(8,128)S(1)}, f32[128,256]{1,0:T(8,128)}) custom-call(f32[256,256]{1,0:T(8,128)S(1)} %inverse.12.refs_0_, f32[128,256]{1,0:T(8,128)S(1)} %get-tuple-element.149.refs_1_, f32[1,256]{1,0:T(1,128)S(1)} %get-tuple-element.150.refs_2_.refs_5_), custom_call_target="tpu_custom_call" | custom-call | tf_op jit(solution)/shard_map/inverse/pallas_call | solution.py:201
  72.9 0.2 shard_map.69
  73.2 0.6 copy.6
  (16 shorter events, 0.3 us)
Async XLA Ops:
  2.2 1.7 %collective-permute-start = (f32[264,256]{1,0:T(8,128)S(1)}, f32[264,256]{1,0:T(8,128)S(1)}, u32[]{:S(2)}, u32[]{:S(2)}) collective-permute-start(f32[264,256]{1,0:T(8,128)S(1)} %get-tuple-element.83), channel_id=1, source_target_pairs={{0,4},{4,0},{1,5},{5,1},{2,6},{6,2},{3,7},{7,3},{8,12},{12,8},{9,1... | collective-permute-start | bytes 811016 | tf_op jit(solution)/shard_map/ppermute | solution.py:236
  4.0 14.0 %collective-permute-start.1 = (f32[136,256]{1,0:T(8,128)S(1)}, f32[136,256]{1,0:T(8,128)S(1)}, u32[]{:S(2)}, u32[]{:S(2)}) collective-permute-start(f32[136,256]{1,0:T(8,128)S(1)} %get-tuple-element.85), channel_id=1, source_target_pairs={{0,1},{4,6},{1,0},{5,7},{2,3},{6,4},{3,2},{7,5},{8,9},{12,14},{9,8... | collective-permute-start | bytes 417800 | tf_op jit(solution)/shard_map/ppermute | solution.py:546
  7.0 11.0 %collective-permute-start.2 = (f32[72,256]{1,0:T(8,128)S(1)}, f32[72,256]{1,0:T(8,128)S(1)}, u32[]{:S(2)}, u32[]{:S(2)}) collective-permute-start(f32[72,256]{1,0:T(8,128)S(1)} %get-tuple-element.86), channel_id=1, source_target_pairs={{0,3},{1,2},{2,1},{3,0},{4,7},{5,6},{6,5},{7,4},{8,11},{9,10},{10,... | collective-permute-start | bytes 221192 | tf_op jit(solution)/shard_map/ppermute | solution.py:236
  9.5 3.7 %collective-permute-start.3 = (f32[8,256]{1,0:T(8,128)S(1)}, f32[8,256]{1,0:T(8,128)S(1)}, u32[]{:S(2)}, u32[]{:S(2)}) collective-permute-start(f32[8,256]{1,0:T(8,128)S(1)} %get-tuple-element.87), channel_id=1, source_target_pairs={{0,8},{8,0},{16,24},{24,16},{1,9},{9,1},{17,25},{25,17},{2,10},{10... | collective-permute-start | bytes 24584 | tf_op jit(solution)/shard_map/ppermute | solution.py:236
  13.1 3.7 %collective-permute-start.4 = (f32[8,256]{1,0:T(8,128)S(1)}, f32[8,256]{1,0:T(8,128)S(1)}, u32[]{:S(2)}, u32[]{:S(2)}) collective-permute-start(f32[8,256]{1,0:T(8,128)S(1)} %add.24), channel_id=1, source_target_pairs={{0,16},{8,24},{16,0},{24,8},{1,17},{9,25},{17,1},{25,9},{2,18},{10... | collective-permute-start | bytes 24584 | tf_op jit(solution)/shard_map/ppermute | solution.py:236
  16.8 1.2 %collective-permute-start.5 = (f32[8,256]{1,0:T(8,128)S(1)}, f32[8,256]{1,0:T(8,128)S(1)}, u32[]{:S(2)}, u32[]{:S(2)}) collective-permute-start(f32[8,256]{1,0:T(8,128)S(1)} %add.25.small_ref), channel_id=1, source_target_pairs={{0,4},{4,0},{1,5},{5,1},{2,6},{6,2},{3,7},{7,3},{8,12},{12,8},{9,1... | collective-permute-start | bytes 24584 | tf_op jit(solution)/shard_map/ppermute | solution.py:236
  18.0 1.5 %collective-permute-start.6 = (f32[200,256]{1,0:T(8,128)S(1)}, f32[200,256]{1,0:T(8,128)S(1)}, u32[]{:S(2)}, u32[]{:S(2)}) collective-permute-start(f32[200,256]{1,0:T(8,128)S(1)} %shard_map.60.mix_ref.refs_5_), channel_id=1, source_target_pairs={{0,4},{4,0},{1,5},{5,1},{2,6},{6,2},{3,7},{7,3},{8,12},{12,8},{9,1... | collective-permute-start | bytes 614408 | tf_op jit(solution)/shard_map/ppermute | solution.py:236
  18.2 3.0 %collective-permute-start.9 = (f32[256,256]{1,0:T(8,128)S(1)}, f32[256,256]{1,0:T(8,128)S(1)}, u32[]{:S(2)}, u32[]{:S(2)}) collective-permute-start(f32[256,256]{1,0:T(8,128)S(1)} %get-tuple-element.95.refs_2_), channel_id=1, source_target_pairs={{0,4},{4,0},{1,5},{5,1},{2,6},{6,2},{3,7},{7,3},{8,12},{12,8},{9,1... | collective-permute-start | bytes 786440 | tf_op jit(solution)/shard_map/ppermute | solution.py:236
  19.6 8.8 %collective-permute-start.7 = (f32[136,256]{1,0:T(8,128)S(1)}, f32[136,256]{1,0:T(8,128)S(1)}, u32[]{:S(2)}, u32[]{:S(2)}) collective-permute-start(f32[136,256]{1,0:T(8,128)S(1)} %get-tuple-element.92.pair_ref), channel_id=1, source_target_pairs={{0,1},{4,6},{1,0},{5,7},{2,3},{6,4},{3,2},{7,5},{8,9},{12,14},{9,8... | collective-permute-start | bytes 417800 | tf_op jit(solution)/shard_map/ppermute | solution.py:546
  20.3 8.0 %collective-permute-start.8 = (f32[72,256]{1,0:T(8,128)S(1)}, f32[72,256]{1,0:T(8,128)S(1)}, u32[]{:S(2)}, u32[]{:S(2)}) collective-permute-start(f32[72,256]{1,0:T(8,128)S(1)} %get-tuple-element.93), channel_id=1, source_target_pairs={{0,3},{1,2},{2,1},{3,0},{4,7},{5,6},{6,5},{7,4},{8,11},{9,10},{10,... | collective-permute-start | bytes 221192 | tf_op jit(solution)/shard_map/ppermute | solution.py:236
  28.3 2.8 %collective-permute-start.10 = (f32[136,256]{1,0:T(8,128)S(1)}, f32[136,256]{1,0:T(8,128)S(1)}, u32[]{:S(2)}, u32[]{:S(2)}) collective-permute-start(f32[136,256]{1,0:T(8,128)S(1)} %collective-permute-done.7.near_ref), channel_id=1, source_target_pairs={{0,4},{4,0},{1,5},{5,1},{2,6},{6,2},{3,7},{7,3},{8,12},{12,8},{9,1... | collective-permute-start | bytes 417800 | tf_op jit(solution)/shard_map/ppermute | solution.py:236
  29.5 1.7 %collective-permute-start.11 = (f32[72,256]{1,0:T(8,128)S(1)}, f32[72,256]{1,0:T(8,128)S(1)}, u32[]{:S(2)}, u32[]{:S(2)}) collective-permute-start(f32[72,256]{1,0:T(8,128)S(1)} %collective-permute-done.8.far_ref), channel_id=1, source_target_pairs={{0,4},{4,0},{1,5},{5,1},{2,6},{6,2},{3,7},{7,3},{8,12},{12,8},{9,1... | collective-permute-start | bytes 221192 | tf_op jit(solution)/shard_map/ppermute | solution.py:236
  34.1 5.0 %collective-permute-start.15 = (f32[128,256]{1,0:T(8,128)S(1)}, f32[128,256]{1,0:T(8,128)S(1)}, u32[]{:S(2)}, u32[]{:S(2)}) collective-permute-start(f32[128,256]{1,0:T(8,128)S(1)} %get-tuple-element.121), channel_id=1, source_target_pairs={{0,8},{4,20},{8,0},{12,28},{16,24},{20,4},{24,16},{28,12},{1,9},{5... | collective-permute-start | bytes 393224 | tf_op jit(solution)/shard_map/ppermute | solution.py:254
  35.6 5.1 %collective-permute-start.12 = (f32[128,256]{1,0:T(8,128)S(1)}, f32[128,256]{1,0:T(8,128)S(1)}, u32[]{:S(2)}, u32[]{:S(2)}) collective-permute-start(f32[128,256]{1,0:T(8,128)S(1)} %get-tuple-element.117), channel_id=1, source_target_pairs={{0,8},{4,20},{8,0},{12,28},{16,24},{20,4},{24,16},{28,12},{1,9},{5... | collective-permute-start | bytes 393224 | tf_op jit(solution)/shard_map/ppermute | solution.py:254
  39.1 5.0 %collective-permute-start.16 = (f32[128,256]{1,0:T(8,128)S(1)}, f32[128,256]{1,0:T(8,128)S(1)}, u32[]{:S(2)}, u32[]{:S(2)}) collective-permute-start(f32[128,256]{1,0:T(8,128)S(1)} %add.28), channel_id=1, source_target_pairs={{0,16},{4,12},{8,24},{12,4},{16,0},{20,28},{24,8},{28,20},{1,17},{... | collective-permute-start | bytes 393224 | tf_op jit(solution)/shard_map/ppermute | solution.py:254
  40.7 5.0 %collective-permute-start.13 = (f32[128,256]{1,0:T(8,128)S(1)}, f32[128,256]{1,0:T(8,128)S(1)}, u32[]{:S(2)}, u32[]{:S(2)}) collective-permute-start(f32[128,256]{1,0:T(8,128)S(1)} %add.27.own_ref), channel_id=1, source_target_pairs={{0,16},{4,12},{8,24},{12,4},{16,0},{20,28},{24,8},{28,20},{1,17},{... | collective-permute-start | bytes 393224 | tf_op jit(solution)/shard_map/ppermute | solution.py:254
  44.2 2.4 %collective-permute-start.17 = (f32[128,256]{1,0:T(8,128)S(1)}, f32[128,256]{1,0:T(8,128)S(1)}, u32[]{:S(2)}, u32[]{:S(2)}) collective-permute-start(f32[128,256]{1,0:T(8,128)S(1)} %add.29), channel_id=1, source_target_pairs={{0,4},{4,0},{1,5},{5,1},{2,6},{6,2},{3,7},{7,3},{8,12},{12,8},{9,1... | collective-permute-start | bytes 393224 | tf_op jit(solution)/shard_map/ppermute | solution.py:236
  46.1 5.0 %collective-permute-start.14 = (f32[128,256]{1,0:T(8,128)S(1)}, f32[128,256]{1,0:T(8,128)S(1)}, u32[]{:S(2)}, u32[]{:S(2)}) collective-permute-start(f32[128,256]{1,0:T(8,128)S(1)} %get-tuple-element.119), channel_id=1, source_target_pairs={{0,1},{1,0},{2,3},{3,2},{4,5},{5,4},{6,7},{7,6},{8,9},{9,8},{10,11... | collective-permute-start | bytes 393224 | tf_op jit(solution)/shard_map/ppermute | solution.py:236
  51.1 7.2 %collective-permute-start.18 = (f32[128,256]{1,0:T(8,128)S(1)}, f32[128,256]{1,0:T(8,128)S(1)}, u32[]{:S(2)}, u32[]{:S(2)}) collective-permute-start(f32[128,256]{1,0:T(8,128)S(1)} %add.30), channel_id=1, source_target_pairs={{0,2},{1,3},{2,0},{3,1},{4,6},{5,7},{6,4},{7,5},{8,10},{9,11},{10,... | collective-permute-start | bytes 393224 | tf_op jit(solution)/shard_map/ppermute | solution.py:236
  52.5 7.8 %collective-permute-start.20 = (f32[128,256]{1,0:T(8,128)S(1)}, f32[128,256]{1,0:T(8,128)S(1)}, u32[]{:S(2)}, u32[]{:S(2)}) collective-permute-start(f32[128,256]{1,0:T(8,128)S(1)} %get-tuple-element.139.refs_2_), channel_id=1, source_target_pairs={{0,4},{4,0},{1,5},{5,1},{2,6},{6,2},{3,7},{7,3},{8,12},{12,8},{9,1... | collective-permute-start | bytes 393224 | tf_op jit(solution)/shard_map/ppermute | solution.py:236
  58.4 1.9 %collective-permute-start.19 = (f32[128,256]{1,0:T(8,128)S(1)}, f32[128,256]{1,0:T(8,128)S(1)}, u32[]{:S(2)}, u32[]{:S(2)}) collective-permute-start(f32[128,256]{1,0:T(8,128)S(1)} %add.31.refs_0_), channel_id=1, source_target_pairs={{0,4},{4,0},{1,5},{5,1},{2,6},{6,2},{3,7},{7,3},{8,12},{12,8},{9,1... | collective-permute-start | bytes 393224 | tf_op jit(solution)/shard_map/ppermute | solution.py:236
  61.5 7.1 %collective-permute-start.21 = (f32[1,256]{1,0:T(1,128)S(1)}, f32[1,256]{1,0:T(1,128)S(1)}, u32[]{:S(2)}, u32[]{:S(2)}) collective-permute-start(f32[1,256]{1,0:T(1,128)S(1)} %get-tuple-element.146.refs_0_), channel_id=1, source_target_pairs={{0,1},{4,6},{1,0},{5,7},{2,3},{6,4},{3,2},{7,5},{8,9},{12,14},{9,8... | collective-permute-start | bytes 3080 | tf_op jit(solution)/shard_map/ppermute | solution.py:546
  63.1 5.5 %collective-permute-start.22 = (f32[1,256]{1,0:T(1,128)S(1)}, f32[1,256]{1,0:T(1,128)S(1)}, u32[]{:S(2)}, u32[]{:S(2)}) collective-permute-start(f32[1,256]{1,0:T(1,128)S(1)} %get-tuple-element.146.refs_0_), channel_id=1, source_target_pairs={{0,3},{1,2},{2,1},{3,0},{4,7},{5,6},{6,5},{7,4},{8,11},{9,10},{10,... | collective-permute-start | bytes 3080 | tf_op jit(solution)/shard_map/ppermute | solution.py:236
  68.6 4.3 %collective-permute-start.23 = (f32[1,256]{1,0:T(1,128)S(1)}, f32[1,256]{1,0:T(1,128)S(1)}, u32[]{:S(2)}, u32[]{:S(2)}) collective-permute-start(f32[1,256]{1,0:T(1,128)S(1)} %collective-permute-done.21), channel_id=1, source_target_pairs={{0,4},{4,0},{1,5},{5,1},{2,6},{6,2},{3,7},{7,3},{8,12},{12,8},{9,1... | collective-permute-start | bytes 3080 | tf_op jit(solution)/shard_map/ppermute | solution.py:236

commit v6 on v5

--- a/solution.py
+++ b/solution.py
@@ -110,7 +110,8 @@
         t_ref[...] = join(part)
         return (back(join(ahead)), *columns(ahead[0][0], block))
 
-    return lax.fori_loop(begin, end, step, (panel, *columns(panel[:8], 0)))[0]
+    twice = 2 if (end - begin) % 2 == 0 else 1
+    return lax.fori_loop(begin, end, step, (panel, *columns(panel[:8], 0)), unroll=twice)[0]
 
 
 side = 128
@@ -217,7 +218,8 @@
     on = eye(n)
     diag = jnp.where(on, h, 0.0)
     trace = jnp.sum(jnp.sum(diag, axis=0, keepdims=True), axis=1, keepdims=True)
-    return h + jnp.where(on, trace * (ridge / n), 0.0)
+    unit = 1.0 / (trace / n)
+    return h * unit + jnp.where(on, ridge, 0.0), unit
 
 
 def normalised(gram, count):
@@ -392,7 +394,7 @@
 
 
 def first_kernel(paired, core_ref, week_ref, own_ref, other_ref, *refs):
-    *parts, v_ref, gram_ref, row_ref, w_ref = refs
+    *parts, v_ref, gram_ref, row_ref, unit_ref, w_ref = refs
     rank = w_ref.shape[1]
     w_ref[...] = jnp.zeros_like(w_ref)
     row_ref[...] = jnp.zeros_like(row_ref)
@@ -404,7 +406,8 @@
             row_ref[pl.ds(at, 1), n * rank : (n + 1) * rank] = part[chunk + 1 + n : chunk + 2 + n, :]
     gram = outer(w_ref[...], w_ref[...])
     gram_ref[...] = gram
-    v_ref[...] = ridged((own_ref[...] + other_ref[...]) * gram)
+    v_ref[...], unit = ridged((own_ref[...] + other_ref[...]) * gram)
+    unit_ref[...] = jnp.broadcast_to(unit, unit_ref.shape)
 
 
 def rows_kernel(me_ref, *refs):
@@ -430,29 +433,30 @@
     t_ref[...] = outer(f_ref[...] - terms[:, rank:], m)
 
 
-def raw_kernel(top_ref, m_ref, inv_ref, raw_ref, g_ref):
-    raw_ref[...] = dot(m_ref[...], inv_ref[...])
+def raw_kernel(top_ref, m_ref, inv_ref, unit_ref, raw_ref, g_ref):
+    raw_ref[...] = dot(m_ref[...], inv_ref[...]) * unit_ref[...]
     grams, rank = g_ref.shape
     at = pl.multiple_of(top_ref[0] * grams, grams) if grams < rank else 0
     g_ref[...] = outer(raw_ref[:, pl.ds(at, grams)], raw_ref[...])
 
 
-def terms_kernel(own_ref, other_ref, inv_ref, w_ref, t_ref, m_ref):
-    t = dot(own_ref[...] + other_ref[...], inv_ref[...])
+def terms_kernel(own_ref, other_ref, inv_ref, unit_ref, w_ref, t_ref, m_ref):
+    t = dot(own_ref[...] + other_ref[...], inv_ref[...]) * unit_ref[...]
     t_ref[...] = t
     m_ref[...] = t * w_ref[...]
 
 
-def second_kernel(count, end, g_ref, gram_c_ref, v_ref, gram_ref, scale_ref, *held_refs):
+def second_kernel(count, end, g_ref, gram_c_ref, v_ref, gram_ref, scale_ref, unit_ref, *held_refs):
     scale, gram = normalised(g_ref[...], count)
     scale_ref[...] = scale
     gram_ref[...] = gram
-    v_ref[...] = ridged(gram * gram_c_ref[...])
+    v_ref[...], unit = ridged(gram * gram_c_ref[...])
+    unit_ref[...] = jnp.broadcast_to(unit, unit_ref.shape)
     eliminate(v_ref, *held_refs, 0, end)
 
 
-def importer_kernel(own_ref, other_ref, scale_ref, inv_ref, t_ref, raw_ref, both_ref):
-    raw = dot((own_ref[...] + other_ref[...]) / scale_ref[...], inv_ref[...])
+def importer_kernel(own_ref, other_ref, scale_ref, inv_ref, unit_ref, t_ref, raw_ref, both_ref):
+    raw = dot((own_ref[...] + other_ref[...]) / scale_ref[...], inv_ref[...]) * unit_ref[...]
     raw_ref[...] = raw
     rank = raw.shape[1]
     both_ref[:rank, :] = outer(raw, raw)
@@ -460,31 +464,35 @@
     both_ref[rank : rank + 1, :] = jnp.sum(raw * t_ref[...], axis=0, keepdims=True)
 
 
-def third_kernel(count, own_ref, other_ref, gram_a_ref, v_ref, scale_ref):
+def third_kernel(count, own_ref, other_ref, gram_a_ref, v_ref, scale_ref, unit_ref):
     rank = own_ref.shape[1]
     scale, gram = normalised(own_ref[:rank, :] + other_ref[:rank, :], count)
     scale_ref[...] = scale
-    v_ref[...] = ridged(gram * gram_a_ref[...])
-
-
-def both_kernel(count, own_ref, side_ref, t_ref, t_side_ref, scale_a_ref, inv_ref, gram_a_ref, raw_ref, week_ref, v_ref, scale_ref):
-    raw = dot(own_ref[...] / scale_a_ref[...], inv_ref[...])
-    raw_side = dot(side_ref[...] / scale_a_ref[...], inv_ref[...])
+    v_ref[...], unit = ridged(gram * gram_a_ref[...])
+    unit_ref[...] = jnp.broadcast_to(unit, unit_ref.shape)
+
+
+def both_kernel(count, *refs):
+    own_ref, side_ref, t_ref, t_side_ref, scale_a_ref, inv_ref, unit_b_ref, gram_a_ref, *outs = refs
+    raw_ref, week_ref, v_ref, scale_ref, unit_ref = outs
+    raw = dot(own_ref[...] / scale_a_ref[...], inv_ref[...]) * unit_b_ref[...]
+    raw_side = dot(side_ref[...] / scale_a_ref[...], inv_ref[...]) * unit_b_ref[...]
     raw_ref[...] = raw
     week_ref[...] = jnp.sum(raw * t_ref[...], axis=0, keepdims=True) + jnp.sum(
         raw_side * t_side_ref[...], axis=0, keepdims=True
     )
     scale, gram = normalised(outer(raw, raw) + outer(raw_side, raw_side), count)
     scale_ref[...] = scale
-    v_ref[...] = ridged(gram * gram_a_ref[...])
+    v_ref[...], unit = ridged(gram * gram_a_ref[...])
+    unit_ref[...] = jnp.broadcast_to(unit, unit_ref.shape)
 
 
 def week_kernel(*refs):
-    *parts, scale_a_ref, scale_b_ref, inv_ref, o_ref, s_ref = refs
+    *parts, scale_a_ref, scale_b_ref, inv_ref, unit_ref, o_ref, s_ref = refs
     s_ref[...] = jnp.zeros_like(s_ref)
     for i, part in enumerate(parts):
         s_ref[i : i + 1, :] = part[...] / scale_a_ref[...] / scale_b_ref[...]
-    raw = dot(s_ref[...], inv_ref[...])
+    raw = dot(s_ref[...], inv_ref[...]) * unit_ref[...]
     scale = jnp.sqrt(jnp.sum(raw * raw, axis=0, keepdims=True) / len(parts) + eps)
     o_ref[...] = raw[:1] / scale
 
@@ -578,9 +586,9 @@
     def first(*refs):
         first_kernel(paired, *refs)
 
-    state, gram_c, row_all = call(
+    state, gram_c, row_all, unit_a = call(
         first,
-        [(rank, rank), (rank, rank), (tall, rows)],
+        [(rank, rank), (rank, rank), (tall, rows), (1, rank)],
         top, me_k, after(gram_own, give), gram_other, *got,
         smem=2, scratch=[pltpu.VMEM((tall, rank), jnp.float32)],
     )
@@ -614,14 +622,14 @@
     )
     (inv_a,) = inverse_piece(after(state, t), cut, steps) if cut < steps else state
     grams = rank // 2 if ni == 2 and rank % 256 == 0 else rank
-    raw_a, g_a = call(raw_kernel, [(rows, rank), (grams, rank)], top, m_a, inv_a, smem=1)
+    raw_a, g_a = call(raw_kernel, [(rows, rank), (grams, rank)], top, m_a, inv_a, unit_a, smem=1)
 
     turns = len(bits("exp"))
     for i in range(turns):
         t_got = crossed(t, "exp", "imp", i)
         if i + 1 < turns:
             t = t + t_got
-    t, m_own = call(terms_kernel, [(cols, rank), (cols, rank)], t, t_got, inv_a, w)
+    t, m_own = call(terms_kernel, [(cols, rank), (cols, rank)], t, t_got, inv_a, unit_a, w)
     m_got = swap(m_own, "wk", 1)
     for i in range(turns):
         g_a = g_a + crossed(g_a, "exp", "imp", i)
@@ -630,7 +638,9 @@
     def second(*refs):
         second_kernel(rows * ne, 1, *refs)
 
-    v, gram_a, scale_a, *state = call(second, [(rank, rank), (rank, rank), (1, rank)] + held, after(g_a, m_own), gram_c)
+    v, gram_a, scale_a, unit_b, *state = call(
+        second, [(rank, rank), (rank, rank), (1, rank), (1, rank)] + held, after(g_a, m_own), gram_c
+    )
     for bit in bits("wk")[1:]:
         m_got, v = lax.optimization_barrier((m_got, v))
         m_own = m_own + m_got
@@ -647,14 +657,14 @@
         def both(*refs):
             both_kernel(cols * ni, *refs)
 
-        raw_b, m_mine, state, scale_b = call(
+        raw_b, m_mine, state, scale_b, unit_c = call(
             both,
-            [(cols, rank), (1, rank), (rank, rank), (1, rank)],
-            m_b, m_side, t, t_side, scale_a, inv_b, gram_a,
+            [(cols, rank), (1, rank), (rank, rank), (1, rank), (1, rank)],
+            m_b, m_side, t, t_side, scale_a, inv_b, unit_b, gram_a,
         )
     else:
         (inv_b,), fac_a = inverse_piece(state, 1, steps, unit=(raw_a, scale_a))
-        raw_b, both = call(importer_kernel, [(cols, rank), (rank + 8, rank)], m_own, m_got, scale_a, inv_b, t)
+        raw_b, both = call(importer_kernel, [(cols, rank), (rank + 8, rank)], m_own, m_got, scale_a, inv_b, unit_b, t)
         for bit in bits("imp")[:-1]:
             both = both + swap(both, "imp", bit)
         got = swap(both, "imp", ni // 2)
@@ -663,7 +673,7 @@
         def third(*refs):
             third_kernel(cols * ni, *refs)
 
-        state, scale_b = call(third, [(rank, rank), (1, rank)], both, got, gram_a)
+        state, scale_b, unit_c = call(third, [(rank, rank), (1, rank), (1, rank)], both, got, gram_a)
     if paired:
         far_row = swap(m_mine, "wk", 3)
         near_row = near_weeks(m_mine)
@@ -677,7 +687,7 @@
         m_all = [m_mine, jnp.where(low, near_row, side_row), jnp.where(low, side_row, near_row), far_row]
     (inv_c,), fac_b = inverse_piece(state, steps // 2, steps, unit=(raw_b, scale_b))
     scratch = [pltpu.VMEM((-(-weeks // 8) * 8, rank), jnp.float32)]
-    fac_c = call(week_kernel, (1, rank), *m_all, scale_a, scale_b, inv_c, scratch=scratch)
+    fac_c = call(week_kernel, (1, rank), *m_all, scale_a, scale_b, inv_c, unit_c, scratch=scratch)
     return (fac_a, fac_b, fac_c)
 
 

time: 73.9 us -> 73.9 us (level)
  no operation moved by 1% of the time
where the time goes in v6:
time: 73.9 us; the launch traced here: 73.7 us
  Pallas kernels  31.8 us (43%)
  starting transfers between devices  23.3 us (32%)
  waiting for transfers between devices  17 us (23%)
  between operations  0.89 us (1%)
    pallas_call x7, Pallas kernels, inverse_piece(): pl.pallas_call(kernel, out_shape=shapes, in_specs=[vmem] * len(args), out...  23.1 us
    ppermute x17, starting transfers between devices, swap(): return lax.ppermute(x, axis, [(i, i ^ bit) for i in range(n)])  12.8 us
    ppermute x17, waiting for transfers between devices, swap(): return lax.ppermute(x, axis, [(i, i ^ bit) for i in range(n)])  10.5 us
    pallas_call x12, Pallas kernels, call(): pl.pallas_call(kernel, out_shape=shapes if many else shapes[0], in_specs=...  7.18 us
    ppermute x4, waiting for transfers between devices, crossed(): return lax.ppermute(x, (axis, side), pairs)  6.41 us
    ppermute x3, starting transfers between devices, near_weeks(): return lax.ppermute(x, ('imp', 'wk'), pairs)  5.38 us
    ppermute x4, starting transfers between devices, crossed(): return lax.ppermute(x, (axis, side), pairs)  5.14 us
    pallas_call x1, Pallas kernels, shares_pair(): pl.pallas_call(open_kernel, out_shape=[pltpu.VMEM(s, jnp.float32) for s i...  1.58 us
  transfers between devices with their start and end apart: 24, of which 10 were waited for; matrix products, arithmetic and copies ran while one was open for 0% of the time, Pallas kernels for 35%

profile of v6, /device:TPU:0, one launch (start us, length us, event | category | flops | bytes accessed | tf_op | source)
XLA Modules:
  0.0 73.7 jit_solution(15056236453948263460)
XLA Ops:
  0.6 1.6 %open.1 = (f32[264,256]{1,0:T(8,128)S(1)}, f32[1,512]{1,0:T(1,128)S(1)}, f32[512,128]{1,0:T(8,128)S(1)}, f32[128,256]{1,0:T(8,128)S(1)}, f32[1,256]{1,0:T(1,128)S(1)}) custom-call(s32[1]{0:T(128)} %bitcast.1.core_ref.refs_0_.top_ref, s32[1]{0:T(128)} %bitcast.week_ref.refs_1_.me_ref, f32[512,128]{1,0:T(8,128)} %bitcast.3, f32[128,256]{1,0:T(8,128)} %b_ref.1, ...), custom_call_target="tpu_custom_call" | custom-call | tf_op jit(solution)/shard_map/open/pallas_call | solution.py:502
  2.2 0.6 collective-permute-start
  2.8 0.7 shard_map.58
  3.5 0.5 collective-permute-done.got_ref
  4.0 3.0 %collective-permute-start.1 = (f32[136,256]{1,0:T(8,128)S(1)}, f32[136,256]{1,0:T(8,128)S(1)}, u32[]{:S(2)}, u32[]{:S(2)}) collective-permute-start(f32[136,256]{1,0:T(8,128)S(1)} %get-tuple-element.88), channel_id=1, source_target_pairs={{0,1},{4,6},{1,0},{5,7},{2,3},{6,4},{3,2},{7,5},{8,9},{12,14},{9,8... | collective-permute-start | bytes 417800 | tf_op jit(solution)/shard_map/ppermute | solution.py:554
  7.0 2.5 %collective-permute-start.2 = (f32[72,256]{1,0:T(8,128)S(1)}, f32[72,256]{1,0:T(8,128)S(1)}, u32[]{:S(2)}, u32[]{:S(2)}) collective-permute-start(f32[72,256]{1,0:T(8,128)S(1)} %get-tuple-element.89), channel_id=1, source_target_pairs={{0,3},{1,2},{2,1},{3,0},{4,7},{5,6},{6,5},{7,4},{8,11},{9,10},{10,... | collective-permute-start | bytes 221192 | tf_op jit(solution)/shard_map/ppermute | solution.py:238
  9.5 1.5 %collective-permute-start.3 = (f32[8,256]{1,0:T(8,128)S(1)}, f32[8,256]{1,0:T(8,128)S(1)}, u32[]{:S(2)}, u32[]{:S(2)}) collective-permute-start(f32[8,256]{1,0:T(8,128)S(1)} %get-tuple-element.90), channel_id=1, source_target_pairs={{0,8},{8,0},{16,24},{24,16},{1,9},{9,1},{17,25},{25,17},{2,10},{10... | collective-permute-start | bytes 24584 | tf_op jit(solution)/shard_map/ppermute | solution.py:238
  11.0 2.2 %collective-permute-done.3 = f32[8,256]{1,0:T(8,128)S(1)} collective-permute-done((f32[8,256]{1,0:T(8,128)S(1)}, f32[8,256]{1,0:T(8,128)S(1)}, u32[]{:S(2)}, u32[]{:S(2)}) %collective-permute-start.3) | collective-permute-done | bytes 8224 | tf_op jit(solution)/shard_map/ppermute | solution.py:238
  13.1 1.5 %collective-permute-start.4 = (f32[8,256]{1,0:T(8,128)S(1)}, f32[8,256]{1,0:T(8,128)S(1)}, u32[]{:S(2)}, u32[]{:S(2)}) collective-permute-start(f32[8,256]{1,0:T(8,128)S(1)} %add.24), channel_id=1, source_target_pairs={{0,16},{8,24},{16,0},{24,8},{1,17},{9,25},{17,1},{25,9},{2,18},{10... | collective-permute-start | bytes 24584 | tf_op jit(solution)/shard_map/ppermute | solution.py:238
  14.7 2.1 %collective-permute-done.4 = f32[8,256]{1,0:T(8,128)S(1)} collective-permute-done((f32[8,256]{1,0:T(8,128)S(1)}, f32[8,256]{1,0:T(8,128)S(1)}, u32[]{:S(2)}, u32[]{:S(2)}) %collective-permute-start.4) | collective-permute-done | bytes 8224 | tf_op jit(solution)/shard_map/ppermute | solution.py:238
  16.8 0.0 collective-permute-start.5
  16.8 1.2 %collective-permute-done.5 = f32[8,256]{1,0:T(8,128)S(1)} collective-permute-done((f32[8,256]{1,0:T(8,128)S(1)}, f32[8,256]{1,0:T(8,128)S(1)}, u32[]{:S(2)}, u32[]{:S(2)}) %collective-permute-start.5) | collective-permute-done | bytes 8224 | tf_op jit(solution)/shard_map/ppermute | solution.py:238
  18.0 0.0 collective-permute-done.2.far_ref.refs_7_
  18.0 0.0 collective-permute-done.1.near_ref
  18.0 0.2 collective-permute-start.6
  18.2 0.3 collective-permute-start.9
  18.6 0.9 %collective-permute-done.6.side_ref.refs_6_ = f32[200,256]{1,0:T(8,128)S(1)} collective-permute-done((f32[200,256]{1,0:T(8,128)S(1)}, f32[200,256]{1,0:T(8,128)S(1)}, u32[]{:S(2)}, u32[]{:S(2)}) %collective-permute-start.6) | collective-permute-done | bytes 204832 | tf_op jit(solution)/shard_map/ppermute | solution.py:238
  19.6 0.7 %collective-permute-start.7 = (f32[136,256]{1,0:T(8,128)S(1)}, f32[136,256]{1,0:T(8,128)S(1)}, u32[]{:S(2)}, u32[]{:S(2)}) collective-permute-start(f32[136,256]{1,0:T(8,128)S(1)} %get-tuple-element.95.pair_ref), channel_id=1, source_target_pairs={{0,1},{4,6},{1,0},{5,7},{2,3},{6,4},{3,2},{7,5},{8,9},{12,14},{9,8... | collective-permute-start | bytes 417800 | tf_op jit(solution)/shard_map/ppermute | solution.py:554
  20.3 0.9 %collective-permute-start.8 = (f32[72,256]{1,0:T(8,128)S(1)}, f32[72,256]{1,0:T(8,128)S(1)}, u32[]{:S(2)}, u32[]{:S(2)}) collective-permute-start(f32[72,256]{1,0:T(8,128)S(1)} %get-tuple-element.96), channel_id=1, source_target_pairs={{0,3},{1,2},{2,1},{3,0},{4,7},{5,6},{6,5},{7,4},{8,11},{9,10},{10,... | collective-permute-start | bytes 221192 | tf_op jit(solution)/shard_map/ppermute | solution.py:238
  21.2 0.0 collective-permute-done.9.refs_3_
  21.2 0.5 shard_map.62
  21.8 4.0 %inverse.7.refs_0_ = f32[256,256]{1,0:T(8,128)S(1)} custom-call(f32[256,256]{1,0:T(8,128)S(1)} %get-tuple-element.99.refs_0_), custom_call_target="tpu_custom_call" | custom-call | tf_op jit(solution)/shard_map/inverse/pallas_call | solution.py:202
  25.8 2.5 %inverse.8 = (f32[256,256]{1,0:T(8,128)S(1)}, f32[64,128]{1,0:T(8,128)S(1)}, f32[32,128]{1,0:T(8,128)S(1)}, f32[32,128]{1,0:T(8,128)S(1)}) custom-call(f32[256,256]{1,0:T(8,128)S(1)} %inverse.7.refs_0_), custom_call_target="tpu_custom_call" | custom-call | tf_op jit(solution)/shard_map/inverse/pallas_call | solution.py:202
  28.3 0.0 collective-permute-done.8.far_ref
  28.3 0.0 collective-permute-done.7.near_ref
  28.3 1.1 %collective-permute-start.10 = (f32[136,256]{1,0:T(8,128)S(1)}, f32[136,256]{1,0:T(8,128)S(1)}, u32[]{:S(2)}, u32[]{:S(2)}) collective-permute-start(f32[136,256]{1,0:T(8,128)S(1)} %collective-permute-done.7.near_ref), channel_id=1, source_target_pairs={{0,4},{4,0},{1,5},{5,1},{2,6},{6,2},{3,7},{7,3},{8,12},{12,8},{9,1... | collective-permute-start | bytes 417800 | tf_op jit(solution)/shard_map/ppermute | solution.py:238
  29.4 0.1 collective-permute-start.11
  29.5 1.6 %inverse.9.inv_ref = f32[256,256]{1,0:T(8,128)S(1)} custom-call(f32[256,256]{1,0:T(8,128)S(1)} %get-tuple-element.110.refs_0_, f32[64,128]{1,0:T(8,128)S(1)} %get-tuple-element.111.refs_1_, f32[32,128]{1,0:T(8,128)S(1)} %get-tuple-element.112.refs_2_, f32[32,128]{1,0:T(8,128)S(1)} %get-tuple-element.113.refs_3_), custom_call_target="tpu_custom_call" | custom-call | tf_op jit(solution)/shard_map/inverse/pallas_call | solution.py:202
  31.0 0.0 collective-permute-done.11.far_side_ref
  31.1 0.0 collective-permute-done.10.side_ref
  31.1 1.5 %shard_map.64 = (f32[512,256]{1,0:T(8,128)S(1)}, f32[128,256]{1,0:T(8,128)S(1)}) custom-call(s32[1]{0:T(128)} %bitcast.week_ref.refs_1_.me_ref, f32[512,256]{1,0:T(8,128)S(1)} %get-tuple-element.116.sum_ref, f32[8,512]{1,0:T(8,128)S(1)} %get-tuple-element.117.row_all_ref, f32[8,256]{1,0:T(8,128)S(1)} %get-tuple-element.118.shift_ref, ...), custom_call_target="tpu_custom_call" | custom-call | tf_op jit(solution)/shard_map/pallas_call | solution.py:161
  32.6 1.4 %shard_map.66 = (f32[512,256]{1,0:T(8,128)S(1)}, f32[128,256]{1,0:T(8,128)S(1)}) custom-call(s32[1]{0:T(128)} %bitcast.1.core_ref.refs_0_.top_ref, f32[512,256]{1,0:T(8,128)S(1)} %get-tuple-element.124.m_ref, f32[256,256]{1,0:T(8,128)S(1)} %inverse.9.inv_ref, f32[1,256]{1,0:T(1,128)S(1)} %get-tuple-element.122.unit_ref), custom_call_target="tpu_custom_call" | custom-call | tf_op jit(solution)/shard_map/pallas_call | solution.py:161
  34.0 1.6 %collective-permute-start.15 = (f32[128,256]{1,0:T(8,128)S(1)}, f32[128,256]{1,0:T(8,128)S(1)}, u32[]{:S(2)}, u32[]{:S(2)}) collective-permute-start(f32[128,256]{1,0:T(8,128)S(1)} %get-tuple-element.125), channel_id=1, source_target_pairs={{0,8},{4,20},{8,0},{12,28},{16,24},{20,4},{24,16},{28,12},{1,9},{5... | collective-permute-start | bytes 393224 | tf_op jit(solution)/shard_map/ppermute | solution.py:256
  35.6 0.5 collective-permute-start.12
  36.1 2.9 %collective-permute-done.15 = f32[128,256]{1,0:T(8,128)S(1)} collective-permute-done((f32[128,256]{1,0:T(8,128)S(1)}, f32[128,256]{1,0:T(8,128)S(1)}, u32[]{:S(2)}, u32[]{:S(2)}) %collective-permute-start.15) | collective-permute-done | bytes 131104 | tf_op jit(solution)/shard_map/ppermute | solution.py:256
  39.1 1.6 %collective-permute-start.16 = (f32[128,256]{1,0:T(8,128)S(1)}, f32[128,256]{1,0:T(8,128)S(1)}, u32[]{:S(2)}, u32[]{:S(2)}) collective-permute-start(f32[128,256]{1,0:T(8,128)S(1)} %add.28), channel_id=1, source_target_pairs={{0,16},{4,12},{8,24},{12,4},{16,0},{20,28},{24,8},{28,20},{1,17},{... | collective-permute-start | bytes 393224 | tf_op jit(solution)/shard_map/ppermute | solution.py:256
  40.6 0.0 collective-permute-done.12
  40.7 1.5 %collective-permute-start.13 = (f32[128,256]{1,0:T(8,128)S(1)}, f32[128,256]{1,0:T(8,128)S(1)}, u32[]{:S(2)}, u32[]{:S(2)}) collective-permute-start(f32[128,256]{1,0:T(8,128)S(1)} %add.27.own_ref), channel_id=1, source_target_pairs={{0,16},{4,12},{8,24},{12,4},{16,0},{20,28},{24,8},{28,20},{1,17},{... | collective-permute-start | bytes 393224 | tf_op jit(solution)/shard_map/ppermute | solution.py:256
  42.1 2.0 %collective-permute-done.16 = f32[128,256]{1,0:T(8,128)S(1)} collective-permute-done((f32[128,256]{1,0:T(8,128)S(1)}, f32[128,256]{1,0:T(8,128)S(1)}, u32[]{:S(2)}, u32[]{:S(2)}) %collective-permute-start.16) | collective-permute-done | bytes 131104 | tf_op jit(solution)/shard_map/ppermute | solution.py:256
  44.1 0.1 collective-permute-start.17
  44.2 1.5 %collective-permute-done.13.other_ref = f32[128,256]{1,0:T(8,128)S(1)} collective-permute-done((f32[128,256]{1,0:T(8,128)S(1)}, f32[128,256]{1,0:T(8,128)S(1)}, u32[]{:S(2)}, u32[]{:S(2)}) %collective-permute-start.13) | collective-permute-done | bytes 131104 | tf_op jit(solution)/shard_map/ppermute | solution.py:256
  45.7 0.3 shard_map.65
  46.0 0.5 collective-permute-start.14
  46.5 0.0 collective-permute-done.17
  46.6 1.1 %shard_map.67 = (f32[256,256]{1,0:T(8,128)S(1)}, f32[256,256]{1,0:T(8,128)S(1)}, f32[1,256]{1,0:T(1,128)S(1)}, f32[1,256]{1,0:T(1,128)S(1)}, f32[64,128]{1,0:T(8...) custom-call(f32[256,256]{1,0:T(8,128)S(1)} %pad_maximum_fusion.refs_0_, f32[256,256]{1,0:T(8,128)S(1)} %get-tuple-element.127.refs_1_), custom_call_target="tpu_custom_call" | custom-call | tf_op jit(solution)/shard_map/pallas_call | solution.py:161
  47.7 3.3 %collective-permute-done.14 = f32[128,256]{1,0:T(8,128)S(1)} collective-permute-done((f32[128,256]{1,0:T(8,128)S(1)}, f32[128,256]{1,0:T(8,128)S(1)}, u32[]{:S(2)}, u32[]{:S(2)}) %collective-permute-start.14) | collective-permute-done | bytes 131104 | tf_op jit(solution)/shard_map/ppermute | solution.py:238
  51.0 1.3 %collective-permute-start.18 = (f32[128,256]{1,0:T(8,128)S(1)}, f32[128,256]{1,0:T(8,128)S(1)}, u32[]{:S(2)}, u32[]{:S(2)}) collective-permute-start(f32[128,256]{1,0:T(8,128)S(1)} %add.30), channel_id=1, source_target_pairs={{0,2},{1,3},{2,0},{3,1},{4,6},{5,7},{6,4},{7,5},{8,10},{9,11},{10,... | collective-permute-start | bytes 393224 | tf_op jit(solution)/shard_map/ppermute | solution.py:238
  52.4 0.0 collective-permute-start.20
  52.4 5.6 %inverse.10 = (f32[256,256]{1,0:T(8,128)S(1)}, f32[64,128]{1,0:T(8,128)S(1)}, f32[32,128]{1,0:T(8,128)S(1)}, f32[32,128]{1,0:T(8,128)S(1)}, f32[512,256]{1,0:T(8,128)}) custom-call(f32[256,256]{1,0:T(8,128)S(1)} %get-tuple-element.131.refs_0_, f32[64,128]{1,0:T(8,128)S(1)} %get-tuple-element.132.refs_1_, f32[32,128]{1,0:T(8,128)S(1)} %get-tuple-element.133.refs_2_, ...), custom_call_target="tpu_custom_call" | custom-call | tf_op jit(solution)/shard_map/inverse/pallas_call | solution.py:202
  58.0 0.3 collective-permute-done.18
  58.3 0.3 collective-permute-start.19
  58.6 1.6 %inverse.11.refs_5_ = f32[256,256]{1,0:T(8,128)S(1)} custom-call(f32[256,256]{1,0:T(8,128)S(1)} %get-tuple-element.145.refs_0_, f32[64,128]{1,0:T(8,128)S(1)} %get-tuple-element.146.refs_1_, f32[32,128]{1,0:T(8,128)S(1)} %get-tuple-element.147.refs_2_, f32[32,128]{1,0:T(8,128)S(1)} %get-tuple-element.148.refs_3_), custom_call_target="tpu_custom_call" | custom-call | tf_op jit(solution)/shard_map/inverse/pallas_call | solution.py:202
  60.1 0.0 collective-permute-done.20.refs_3_
  60.1 0.0 collective-permute-done.19.refs_1_
  60.2 1.2 %shard_map.68 = (f32[128,256]{1,0:T(8,128)S(1)}, f32[1,256]{1,0:T(1,128)S(1)}, f32[256,256]{1,0:T(8,128)S(1)}, f32[1,256]{1,0:T(1,128)S(1)}, f32[1,256]{1,0:T(1,128)S(1)}) custom-call(f32[128,256]{1,0:T(8,128)S(1)} %add.31.refs_0_, f32[128,256]{1,0:T(8,128)S(1)} %collective-permute-done.19.refs_1_, f32[128,256]{1,0:T(8,128)S(1)} %get-tuple-element.143.refs_2_, ...), custom_call_target="tpu_custom_call" | custom-call | tf_op jit(solution)/shard_map/pallas_call | solution.py:161
  61.4 1.6 %collective-permute-start.21 = (f32[1,256]{1,0:T(1,128)S(1)}, f32[1,256]{1,0:T(1,128)S(1)}, u32[]{:S(2)}, u32[]{:S(2)}) collective-permute-start(f32[1,256]{1,0:T(1,128)S(1)} %get-tuple-element.151.refs_0_), channel_id=1, source_target_pairs={{0,1},{4,6},{1,0},{5,7},{2,3},{6,4},{3,2},{7,5},{8,9},{12,14},{9,8... | collective-permute-start | bytes 3080 | tf_op jit(solution)/shard_map/ppermute | solution.py:554
  63.1 1.5 %collective-permute-start.22 = (f32[1,256]{1,0:T(1,128)S(1)}, f32[1,256]{1,0:T(1,128)S(1)}, u32[]{:S(2)}, u32[]{:S(2)}) collective-permute-start(f32[1,256]{1,0:T(1,128)S(1)} %get-tuple-element.151.refs_0_), channel_id=1, source_target_pairs={{0,3},{1,2},{2,1},{3,0},{4,7},{5,6},{6,5},{7,4},{8,11},{9,10},{10,... | collective-permute-start | bytes 3080 | tf_op jit(solution)/shard_map/ppermute | solution.py:238
  64.6 4.0 %inverse.12.refs_0_ = f32[256,256]{1,0:T(8,128)S(1)} custom-call(f32[256,256]{1,0:T(8,128)S(1)} %get-tuple-element.152.refs_0_), custom_call_target="tpu_custom_call" | custom-call | tf_op jit(solution)/shard_map/inverse/pallas_call | solution.py:202
  68.6 0.0 collective-permute-done.21
  68.7 0.3 collective-permute-start.23
  69.0 3.9 %inverse.13 = (f32[256,256]{1,0:T(8,128)S(1)}, f32[128,256]{1,0:T(8,128)}) custom-call(f32[256,256]{1,0:T(8,128)S(1)} %inverse.12.refs_0_, f32[128,256]{1,0:T(8,128)S(1)} %get-tuple-element.154.refs_1_, f32[1,256]{1,0:T(1,128)S(1)} %get-tuple-element.155.refs_2_.refs_5_), custom_call_target="tpu_custom_call" | custom-call | tf_op jit(solution)/shard_map/inverse/pallas_call | solution.py:202
  72.9 0.0 collective-permute-done.23
  72.9 0.2 shard_map.69
  73.1 0.6 copy.6
  (16 shorter events, 0.3 us)
Async XLA Ops:
  2.2 1.7 %collective-permute-start = (f32[264,256]{1,0:T(8,128)S(1)}, f32[264,256]{1,0:T(8,128)S(1)}, u32[]{:S(2)}, u32[]{:S(2)}) collective-permute-start(f32[264,256]{1,0:T(8,128)S(1)} %get-tuple-element.86), channel_id=1, source_target_pairs={{0,4},{4,0},{1,5},{5,1},{2,6},{6,2},{3,7},{7,3},{8,12},{12,8},{9,1... | collective-permute-start | bytes 811016 | tf_op jit(solution)/shard_map/ppermute | solution.py:238
  4.0 14.0 %collective-permute-start.1 = (f32[136,256]{1,0:T(8,128)S(1)}, f32[136,256]{1,0:T(8,128)S(1)}, u32[]{:S(2)}, u32[]{:S(2)}) collective-permute-start(f32[136,256]{1,0:T(8,128)S(1)} %get-tuple-element.88), channel_id=1, source_target_pairs={{0,1},{4,6},{1,0},{5,7},{2,3},{6,4},{3,2},{7,5},{8,9},{12,14},{9,8... | collective-permute-start | bytes 417800 | tf_op jit(solution)/shard_map/ppermute | solution.py:554
  7.0 11.0 %collective-permute-start.2 = (f32[72,256]{1,0:T(8,128)S(1)}, f32[72,256]{1,0:T(8,128)S(1)}, u32[]{:S(2)}, u32[]{:S(2)}) collective-permute-start(f32[72,256]{1,0:T(8,128)S(1)} %get-tuple-element.89), channel_id=1, source_target_pairs={{0,3},{1,2},{2,1},{3,0},{4,7},{5,6},{6,5},{7,4},{8,11},{9,10},{10,... | collective-permute-start | bytes 221192 | tf_op jit(solution)/shard_map/ppermute | solution.py:238
  9.5 3.7 %collective-permute-start.3 = (f32[8,256]{1,0:T(8,128)S(1)}, f32[8,256]{1,0:T(8,128)S(1)}, u32[]{:S(2)}, u32[]{:S(2)}) collective-permute-start(f32[8,256]{1,0:T(8,128)S(1)} %get-tuple-element.90), channel_id=1, source_target_pairs={{0,8},{8,0},{16,24},{24,16},{1,9},{9,1},{17,25},{25,17},{2,10},{10... | collective-permute-start | bytes 24584 | tf_op jit(solution)/shard_map/ppermute | solution.py:238
  13.1 3.7 %collective-permute-start.4 = (f32[8,256]{1,0:T(8,128)S(1)}, f32[8,256]{1,0:T(8,128)S(1)}, u32[]{:S(2)}, u32[]{:S(2)}) collective-permute-start(f32[8,256]{1,0:T(8,128)S(1)} %add.24), channel_id=1, source_target_pairs={{0,16},{8,24},{16,0},{24,8},{1,17},{9,25},{17,1},{25,9},{2,18},{10... | collective-permute-start | bytes 24584 | tf_op jit(solution)/shard_map/ppermute | solution.py:238
  16.8 1.2 %collective-permute-start.5 = (f32[8,256]{1,0:T(8,128)S(1)}, f32[8,256]{1,0:T(8,128)S(1)}, u32[]{:S(2)}, u32[]{:S(2)}) collective-permute-start(f32[8,256]{1,0:T(8,128)S(1)} %add.25.small_ref), channel_id=1, source_target_pairs={{0,4},{4,0},{1,5},{5,1},{2,6},{6,2},{3,7},{7,3},{8,12},{12,8},{9,1... | collective-permute-start | bytes 24584 | tf_op jit(solution)/shard_map/ppermute | solution.py:238
  18.0 1.5 %collective-permute-start.6 = (f32[200,256]{1,0:T(8,128)S(1)}, f32[200,256]{1,0:T(8,128)S(1)}, u32[]{:S(2)}, u32[]{:S(2)}) collective-permute-start(f32[200,256]{1,0:T(8,128)S(1)} %shard_map.60.mix_ref.refs_5_), channel_id=1, source_target_pairs={{0,4},{4,0},{1,5},{5,1},{2,6},{6,2},{3,7},{7,3},{8,12},{12,8},{9,1... | collective-permute-start | bytes 614408 | tf_op jit(solution)/shard_map/ppermute | solution.py:238
  18.2 3.0 %collective-permute-start.9 = (f32[256,256]{1,0:T(8,128)S(1)}, f32[256,256]{1,0:T(8,128)S(1)}, u32[]{:S(2)}, u32[]{:S(2)}) collective-permute-start(f32[256,256]{1,0:T(8,128)S(1)} %get-tuple-element.98.refs_2_), channel_id=1, source_target_pairs={{0,4},{4,0},{1,5},{5,1},{2,6},{6,2},{3,7},{7,3},{8,12},{12,8},{9,1... | collective-permute-start | bytes 786440 | tf_op jit(solution)/shard_map/ppermute | solution.py:238
  19.6 8.7 %collective-permute-start.7 = (f32[136,256]{1,0:T(8,128)S(1)}, f32[136,256]{1,0:T(8,128)S(1)}, u32[]{:S(2)}, u32[]{:S(2)}) collective-permute-start(f32[136,256]{1,0:T(8,128)S(1)} %get-tuple-element.95.pair_ref), channel_id=1, source_target_pairs={{0,1},{4,6},{1,0},{5,7},{2,3},{6,4},{3,2},{7,5},{8,9},{12,14},{9,8... | collective-permute-start | bytes 417800 | tf_op jit(solution)/shard_map/ppermute | solution.py:554
  20.3 8.0 %collective-permute-start.8 = (f32[72,256]{1,0:T(8,128)S(1)}, f32[72,256]{1,0:T(8,128)S(1)}, u32[]{:S(2)}, u32[]{:S(2)}) collective-permute-start(f32[72,256]{1,0:T(8,128)S(1)} %get-tuple-element.96), channel_id=1, source_target_pairs={{0,3},{1,2},{2,1},{3,0},{4,7},{5,6},{6,5},{7,4},{8,11},{9,10},{10,... | collective-permute-start | bytes 221192 | tf_op jit(solution)/shard_map/ppermute | solution.py:238
  28.3 2.8 %collective-permute-start.10 = (f32[136,256]{1,0:T(8,128)S(1)}, f32[136,256]{1,0:T(8,128)S(1)}, u32[]{:S(2)}, u32[]{:S(2)}) collective-permute-start(f32[136,256]{1,0:T(8,128)S(1)} %collective-permute-done.7.near_ref), channel_id=1, source_target_pairs={{0,4},{4,0},{1,5},{5,1},{2,6},{6,2},{3,7},{7,3},{8,12},{12,8},{9,1... | collective-permute-start | bytes 417800 | tf_op jit(solution)/shard_map/ppermute | solution.py:238
  29.4 1.7 %collective-permute-start.11 = (f32[72,256]{1,0:T(8,128)S(1)}, f32[72,256]{1,0:T(8,128)S(1)}, u32[]{:S(2)}, u32[]{:S(2)}) collective-permute-start(f32[72,256]{1,0:T(8,128)S(1)} %collective-permute-done.8.far_ref), channel_id=1, source_target_pairs={{0,4},{4,0},{1,5},{5,1},{2,6},{6,2},{3,7},{7,3},{8,12},{12,8},{9,1... | collective-permute-start | bytes 221192 | tf_op jit(solution)/shard_map/ppermute | solution.py:238
  34.0 5.0 %collective-permute-start.15 = (f32[128,256]{1,0:T(8,128)S(1)}, f32[128,256]{1,0:T(8,128)S(1)}, u32[]{:S(2)}, u32[]{:S(2)}) collective-permute-start(f32[128,256]{1,0:T(8,128)S(1)} %get-tuple-element.125), channel_id=1, source_target_pairs={{0,8},{4,20},{8,0},{12,28},{16,24},{20,4},{24,16},{28,12},{1,9},{5... | collective-permute-start | bytes 393224 | tf_op jit(solution)/shard_map/ppermute | solution.py:256
  35.6 5.1 %collective-permute-start.12 = (f32[128,256]{1,0:T(8,128)S(1)}, f32[128,256]{1,0:T(8,128)S(1)}, u32[]{:S(2)}, u32[]{:S(2)}) collective-permute-start(f32[128,256]{1,0:T(8,128)S(1)} %get-tuple-element.120), channel_id=1, source_target_pairs={{0,8},{4,20},{8,0},{12,28},{16,24},{20,4},{24,16},{28,12},{1,9},{5... | collective-permute-start | bytes 393224 | tf_op jit(solution)/shard_map/ppermute | solution.py:256
  39.1 5.0 %collective-permute-start.16 = (f32[128,256]{1,0:T(8,128)S(1)}, f32[128,256]{1,0:T(8,128)S(1)}, u32[]{:S(2)}, u32[]{:S(2)}) collective-permute-start(f32[128,256]{1,0:T(8,128)S(1)} %add.28), channel_id=1, source_target_pairs={{0,16},{4,12},{8,24},{12,4},{16,0},{20,28},{24,8},{28,20},{1,17},{... | collective-permute-start | bytes 393224 | tf_op jit(solution)/shard_map/ppermute | solution.py:256
  40.7 5.0 %collective-permute-start.13 = (f32[128,256]{1,0:T(8,128)S(1)}, f32[128,256]{1,0:T(8,128)S(1)}, u32[]{:S(2)}, u32[]{:S(2)}) collective-permute-start(f32[128,256]{1,0:T(8,128)S(1)} %add.27.own_ref), channel_id=1, source_target_pairs={{0,16},{4,12},{8,24},{12,4},{16,0},{20,28},{24,8},{28,20},{1,17},{... | collective-permute-start | bytes 393224 | tf_op jit(solution)/shard_map/ppermute | solution.py:256
  44.1 2.4 %collective-permute-start.17 = (f32[128,256]{1,0:T(8,128)S(1)}, f32[128,256]{1,0:T(8,128)S(1)}, u32[]{:S(2)}, u32[]{:S(2)}) collective-permute-start(f32[128,256]{1,0:T(8,128)S(1)} %add.29), channel_id=1, source_target_pairs={{0,4},{4,0},{1,5},{5,1},{2,6},{6,2},{3,7},{7,3},{8,12},{12,8},{9,1... | collective-permute-start | bytes 393224 | tf_op jit(solution)/shard_map/ppermute | solution.py:238
  46.0 5.0 %collective-permute-start.14 = (f32[128,256]{1,0:T(8,128)S(1)}, f32[128,256]{1,0:T(8,128)S(1)}, u32[]{:S(2)}, u32[]{:S(2)}) collective-permute-start(f32[128,256]{1,0:T(8,128)S(1)} %get-tuple-element.123), channel_id=1, source_target_pairs={{0,1},{1,0},{2,3},{3,2},{4,5},{5,4},{6,7},{7,6},{8,9},{9,8},{10,11... | collective-permute-start | bytes 393224 | tf_op jit(solution)/shard_map/ppermute | solution.py:238
  51.0 7.2 %collective-permute-start.18 = (f32[128,256]{1,0:T(8,128)S(1)}, f32[128,256]{1,0:T(8,128)S(1)}, u32[]{:S(2)}, u32[]{:S(2)}) collective-permute-start(f32[128,256]{1,0:T(8,128)S(1)} %add.30), channel_id=1, source_target_pairs={{0,2},{1,3},{2,0},{3,1},{4,6},{5,7},{6,4},{7,5},{8,10},{9,11},{10,... | collective-permute-start | bytes 393224 | tf_op jit(solution)/shard_map/ppermute | solution.py:238
  52.4 7.8 %collective-permute-start.20 = (f32[128,256]{1,0:T(8,128)S(1)}, f32[128,256]{1,0:T(8,128)S(1)}, u32[]{:S(2)}, u32[]{:S(2)}) collective-permute-start(f32[128,256]{1,0:T(8,128)S(1)} %get-tuple-element.143.refs_2_), channel_id=1, source_target_pairs={{0,4},{4,0},{1,5},{5,1},{2,6},{6,2},{3,7},{7,3},{8,12},{12,8},{9,1... | collective-permute-start | bytes 393224 | tf_op jit(solution)/shard_map/ppermute | solution.py:238
  58.3 1.9 %collective-permute-start.19 = (f32[128,256]{1,0:T(8,128)S(1)}, f32[128,256]{1,0:T(8,128)S(1)}, u32[]{:S(2)}, u32[]{:S(2)}) collective-permute-start(f32[128,256]{1,0:T(8,128)S(1)} %add.31.refs_0_), channel_id=1, source_target_pairs={{0,4},{4,0},{1,5},{5,1},{2,6},{6,2},{3,7},{7,3},{8,12},{12,8},{9,1... | collective-permute-start | bytes 393224 | tf_op jit(solution)/shard_map/ppermute | solution.py:238
  61.4 7.2 %collective-permute-start.21 = (f32[1,256]{1,0:T(1,128)S(1)}, f32[1,256]{1,0:T(1,128)S(1)}, u32[]{:S(2)}, u32[]{:S(2)}) collective-permute-start(f32[1,256]{1,0:T(1,128)S(1)} %get-tuple-element.151.refs_0_), channel_id=1, source_target_pairs={{0,1},{4,6},{1,0},{5,7},{2,3},{6,4},{3,2},{7,5},{8,9},{12,14},{9,8... | collective-permute-start | bytes 3080 | tf_op jit(solution)/shard_map/ppermute | solution.py:554
  63.1 5.6 %collective-permute-start.22 = (f32[1,256]{1,0:T(1,128)S(1)}, f32[1,256]{1,0:T(1,128)S(1)}, u32[]{:S(2)}, u32[]{:S(2)}) collective-permute-start(f32[1,256]{1,0:T(1,128)S(1)} %get-tuple-element.151.refs_0_), channel_id=1, source_target_pairs={{0,3},{1,2},{2,1},{3,0},{4,7},{5,6},{6,5},{7,4},{8,11},{9,10},{10,... | collective-permute-start | bytes 3080 | tf_op jit(solution)/shard_map/ppermute | solution.py:238
  68.7 4.2 %collective-permute-start.23 = (f32[1,256]{1,0:T(1,128)S(1)}, f32[1,256]{1,0:T(1,128)S(1)}, u32[]{:S(2)}, u32[]{:S(2)}) collective-permute-start(f32[1,256]{1,0:T(1,128)S(1)} %collective-permute-done.21), channel_id=1, source_target_pairs={{0,4},{4,0},{1,5},{5,1},{2,6},{6,2},{3,7},{7,3},{8,12},{12,8},{9,1... | collective-permute-start | bytes 3080 | tf_op jit(solution)/shard_map/ppermute | solution.py:238
